TPU v7x, 512 devices: a whole 4x4x16 slice. The times are simulated.
512 devices in a mesh: gr: 16 (over z_hi, y, core), gc: 32 (over x, z_lo).
Axes of the slice: x: 4, y: 4, z: 16 (z_hi: 2, z_lo: 8; z = z_hi * 8 + z_lo), core: 2. Of those that a mesh axis runs over, the one named last changes fastest.
Arguments:
- features: bfloat16 [65536, 1024], P(('gr', 'gc')), may hold values from -6 to 6
- weight: bfloat16 [1024, 1024], replicated, may hold values from -0.1875 to 0.1875
- cotangent: bfloat16 [65536, 1024], P(('gr', 'gc')), may hold values from -6 to 6
- block_values: bfloat16 [512, 16, 128, 128], P(('gr', 'gc')), as said below
- block_codes: int32 [512, 16], P(('gr', 'gc')), may hold values from 0 to 511, as said below
- block_count: int32 [512], P(('gr', 'gc')), may hold values from 1 to 16, as said below
Outputs:
- output: float32 [65536, 1024], P(('gr', 'gc'))
- input_grad: float32 [65536, 1024], P(('gr', 'gc'))
- weight_grad: float32 [1024, 1024], P('gc')
Inputs may be any that keep to these rules, and one draw needn't show every extreme that they name: `block_codes`: write code = row * 512 + column. In every slot, row lies in 0 to 0 and column is a block of a slice s + j * 32 with |j| <= 8 (same grid column, at most 8 grid rows away). The codes of the live slots of one slice differ from one another. Every diagonal block (block row equal to block column) is live. The live slots of a slice are its first block_count slots; the entries of later slots are not part of the adjacency. In every draw some slice has all 16 slots live. `block_values`: the adjacency is symmetric: a block is live exactly when its mirror block is, and its entries are the transpose of the mirror's.
All inputs are finite; a program needn't handle non-finite values.
Results may differ from a plain program's by a relative error of at most 0.0045.
Values may be sent and summed in bfloat16 or wider, within the bound.
No kernel may reach another device: no remote copies, remote signals or barrier semaphores. Data moves between devices by JAX's collectives and lax.ppermute only.
A program may use at most 64 MiB of HBM per device.

v0:
```python
import jax
import jax.numpy as jnp
from jax import lax
from jax.sharding import PartitionSpec as P


def dense_tile(row_index, block_index, active, values, piece_blocks, row_blocks):
    block_size = values.shape[-1]
    select_col = (block_index[:, None] == jnp.arange(piece_blocks)[None, :]) & active[:, None]
    select_row = row_index[:, None] == jnp.arange(row_blocks)[None, :]
    tiled = jnp.einsum(
        "ka,km,kij->aimj",
        select_row.astype(jnp.bfloat16),
        select_col.astype(jnp.bfloat16),
        values,
        preferred_element_type=jnp.float32,
    )
    return tiled.astype(jnp.bfloat16).reshape(row_blocks * block_size, piece_blocks * block_size)


def aggregate(source, layout):
    row_index, block_index, active, values = layout
    node_rows = source.shape[0]
    block_size = values.shape[-1]
    row_blocks = node_rows // block_size
    portion = lax.all_gather(source, "gr", axis=0, tiled=True)
    tile = dense_tile(
        row_index, block_index, active, values, portion.shape[0] // block_size, row_blocks
    )
    return jnp.dot(tile, portion, preferred_element_type=jnp.float32)


def local(features, weight, cotangent, block_values, block_codes, block_count):
    node_rows = features.shape[0]
    block_size = block_values.shape[-1]
    row_blocks = node_rows // block_size
    grid_cols = lax.axis_size("gc")
    grid_rows = lax.axis_size("gr")
    all_blocks = row_blocks * grid_rows * grid_cols
    slot_codes = block_codes[0]
    row_index = slot_codes // all_blocks
    column_block = slot_codes % all_blocks
    block_index = column_block // row_blocks // grid_cols * row_blocks + column_block % row_blocks
    active = jnp.arange(slot_codes.shape[0]) < block_count[0]
    layout = (row_index, block_index, active, block_values[0])
    projected = jnp.dot(features, weight, preferred_element_type=jnp.float32).astype(jnp.bfloat16)
    summed = aggregate(projected, layout)
    sigmoid = jax.nn.sigmoid(summed)
    output = summed * sigmoid
    act_slope = (cotangent.astype(jnp.float32) * sigmoid * (1.0 + summed * (1.0 - sigmoid))).astype(
        jnp.bfloat16
    )
    back_grad = aggregate(act_slope, layout).astype(jnp.bfloat16)
    input_grad = lax.dot_general(
        back_grad, weight, (((1,), (1,)), ((), ())), preferred_element_type=jnp.float32
    )
    grad_scale = (node_rows * grid_rows * grid_cols) ** (-0.5)
    partial_grad = (
        lax.dot_general(
            features, back_grad, (((0,), (0,)), ((), ())), preferred_element_type=jnp.float32
        )
        * grad_scale
    )
    row_share = lax.psum_scatter(partial_grad, "gc", scatter_dimension=0, tiled=True)
    weight_grad = lax.psum(row_share, "gr")
    return (output, input_grad, weight_grad)


def solution(mesh):
    in_specs = (
        P(("gr", "gc"), None),
        P(),
        P(("gr", "gc"), None),
        P(("gr", "gc"), None, None, None),
        P(("gr", "gc"), None),
        P(("gr", "gc")),
    )
    out_specs = (P(("gr", "gc"), None), P(("gr", "gc"), None), P("gc", None))
    return jax.shard_map(local, mesh=mesh, in_specs=in_specs, out_specs=out_specs, check_vma=False)
```

profile of v0, /device:TPU:1, one launch (start us, length us, event | category | flops | bytes accessed | tf_op | source)
XLA Modules:
  0.0 770.5 jit_solution(15007061973408233624)
XLA Ops:
  7.2 0.0 copy-start
  7.2 0.0 all-gather.3.cloned.1.call-start
  7.2 1.5 copy-done
  8.8 2.1 convolution_convert_fusion.1
  10.9 0.0 all-gather.3.cloned.1.call-update
  10.9 0.0 all-gather.5.cloned.1.call-start
  11.6 0.7 and_select_fusion.1
  12.3 0.7 compare_convert_fusion
  12.9 1.5 convolution_convert_fusion
  14.4 122.6 %all-gather.3.cloned.1.call-done = bf16[2048,1024]{1,0:T(8,128)(2,1)} async-done(((bf16[128,1024]{1,0:T(8,128)(2,1)}), bf16[2048,1024]{1,0:T(8,128)(2,1)}) %all-gather.3.cloned.1.call-update) | async-done | bytes 4194320 | tf_op jit(solution)/shard_map/all_gather | solution.py:26
  137.0 4.0 multiply_convert_fusion
  141.0 0.0 copy-start.1
  141.0 0.0 all-gather.5.cloned.1.call-update
  141.0 0.0 reduce-scatter.4.cloned.1.call-start
  141.1 112.4 %all-gather.5.cloned.1.call-done = bf16[2048,1024]{1,0:T(8,128)(2,1)} async-done(((bf16[128,1024]{1,0:T(8,128)(2,1)}), bf16[2048,1024]{1,0:T(8,128)(2,1)}) %all-gather.5.cloned.1.call-update) | async-done | bytes 4194320 | tf_op jit(solution)/shard_map/all_gather | solution.py:26
  253.5 2.9 convolution_convert_fusion.2
  256.4 0.0 copy-done.1
  256.4 2.7 multiply_bitcast_fusion
  259.1 5.4 copy.13
  264.5 0.0 reduce-scatter.4.cloned.1.call-update
  264.5 0.0 all-reduce.2.cloned.1.call-start
  264.6 222.1 %reduce-scatter.4.cloned.1.call-done = f32[32,1024]{1,0:T(8,128)} async-done(((f32[1024,1024]{1,0:T(8,128)}), f32[32,1024]{1,0:T(8,128)}) %reduce-scatter.4.cloned.1.call-update) | async-done | bytes 131088
  486.6 1.9 copy.14
  488.5 0.0 all-reduce.2.cloned.1.call-update
  488.6 1.6 fusion.16
  490.2 271.9 %all-reduce.2.cloned.1.call-done = f32[32,1024]{0,1:T(8,128)} async-done(((f32[32,1024]{0,1:T(8,128)}), f32[32,1024]{0,1:T(8,128)}) %all-reduce.2.cloned.1.call-update) | async-done | bytes 131088 | tf_op jit(solution)/shard_map/psum | solution.py:65
  762.1 1.9 copy.12
Async XLA Ops:
  7.2 1.6 copy-start
  7.2 129.8 %all-gather.3.cloned.1.call-start = ((), (), s32[]{:S(2)}) async-start(), calls=%async_computation.1 | async-start | bytes 4456448 | tf_op jit(solution)/shard_map/all_gather | solution.py:26
  10.9 242.6 %all-gather.5.cloned.1.call-start = ((), (), s32[]{:S(2)}) async-start(), calls=%async_computation.2 | async-start | bytes 4456448 | tf_op jit(solution)/shard_map/all_gather | solution.py:26
  141.0 115.4 %copy-start.1 = (bf16[128,1024]{1,0:T(8,128)(2,1)S(1)}, bf16[128,1024]{1,0:T(8,128)(2,1)}, u32[]{:S(2)}) copy-start(bf16[128,1024]{1,0:T(8,128)(2,1)} %param.6) | copy-start | bytes 786436
  141.0 345.6 %reduce-scatter.4.cloned.1.call-start = ((), (), s32[]{:S(2)}) async-start(), calls=%async_computation.4 | async-start | bytes 4325376
  264.5 497.6 %all-reduce.2.cloned.1.call-start = ((), (), s32[]{:S(2)}) async-start(), calls=%async_computation.3 | async-start | bytes 1048576 | tf_op jit(solution)/shard_map/psum | solution.py:65
Sparse Core Ops, SparseCore 0:
  11.9 125.0 all-gather.2
  141.1 112.3 all-gather.4
  264.6 221.9 reduce-scatter.3
  489.4 272.6 all-reduce.1
where the time goes:
time: 771 us; the launch traced here: 770 us
  waiting for transfers between devices  729 us (95%)
  matrix products  14.8 us (2%)
  between operations  14.4 us (2%)
  local copies, waits for them, and re-layouts  10.7 us (1%)
    psum x1, waiting for transfers between devices, local(): weight_grad = lax.psum(row_share, 'gr')  272 us
    all_gather x2, waiting for transfers between devices, aggregate(): portion = lax.all_gather(source, 'gr', axis=0, tiled=True)  235 us
    unnamed x5, waiting for transfers between devices  222 us
  transfers between devices with their start and end apart: 4, of which 4 were waited for; matrix products, arithmetic and copies ran while one was open for 1% of the time, Pallas kernels for 0%

commit v1 on v0

v1 whole, which is shorter than its diff:
```python
import jax
import jax.numpy as jnp
from jax import lax
from jax.experimental import pallas as pl
from jax.experimental.pallas import tpu as pltpu
from jax.sharding import Mesh, PartitionSpec as P

AXES = ("zh", "y", "co", "x", "zl")
SIZES = (2, 4, 2, 4, 8)
BF16, F32 = jnp.bfloat16, jnp.float32
SWAP = [(0, 1), (1, 0)]
VMEM = pl.BlockSpec(memory_space=pltpu.VMEM)


def dot(a, b):
    return jnp.dot(a, b, preferred_element_type=F32)


def call(body, outs, *args):
    return pl.pallas_call(
        body,
        out_shape=outs,
        in_specs=[VMEM] * len(args),
        out_specs=jax.tree.map(lambda _: VMEM, outs),
        compiler_params=pltpu.CompilerParams(vmem_limit_bytes=48 * 2**20),
    )(*args)


def forward_body(tile, near, far_same, far_other, weight, cotangent, out, slope, mixed):
    total = near[...]
    total += dot(tile[:, 1024:1536], far_same[...])
    total += dot(tile[:, 1536:2048], far_other[...])
    mixed_here = total.astype(BF16)
    mixed[...] = mixed_here
    summed = dot(mixed_here, weight[...])
    sigmoid = jax.nn.sigmoid(summed)
    out[...] = summed * sigmoid
    slope[...] = (
        cotangent[...].astype(F32) * sigmoid * (1.0 + summed * (1.0 - sigmoid))
    ).astype(BF16)


def backward_body(tile, near, far_same, far_other, weight, input_grad):
    total = near[...]
    total += dot(tile[:, 1024:1536], far_same[...])
    total += dot(tile[:, 1536:2048], far_other[...])
    input_grad[...] = lax.dot_general(
        total.astype(BF16), weight[...], (((1,), (1,)), ((), ())), preferred_element_type=F32
    )


def near_body(tile, near_same, near_other, near):
    near[...] = dot(tile[:, 0:512], near_same[...]) + dot(tile[:, 512:1024], near_other[...])


def partial_body(core, factors, near_same, near_other, partial):
    mine = core[0]
    total = jnp.zeros(partial.shape, F32)
    for y in range(4):
        rows = slice(128 * y, 128 * y + 128)
        total += dot(factors[2 * y + mine], near_same[rows, :])
        total += dot(factors[2 * y + 1 - mine], near_other[rows, :])
    partial[...] = total


def spread(rows, axes, count):
    return lax.all_to_all(jnp.broadcast_to(rows[None], (count,) + rows.shape), axes, 0, 0)


def over_y(rows):
    same = spread(rows, "y", 4).reshape(512, rows.shape[1])
    return same, lax.ppermute(same, "co", SWAP)


def local(features, weight, cotangent, block_values, block_codes, block_count):
    zh, core = lax.axis_index("zh"), lax.axis_index("co")
    hidden = features.shape[1]
    grid_row = block_codes[0] % 512 // 32
    place = (grid_row // 8 ^ zh) * 8 + (grid_row % 2 ^ core) * 4 + grid_row % 8 // 2
    active = jnp.arange(16) < block_count[0]
    select = (place[:, None] == jnp.arange(16)[None, :]) & active[:, None]
    tile = jnp.einsum("km,kij->imj", select.astype(BF16), block_values[0], preferred_element_type=F32)
    tile = tile.astype(BF16).reshape(128, 2048)
    at = jnp.arange(hidden)
    group, to_x, to_zh, to_zl, last = at // 128, at // 32 % 4, at // 16 % 2, at // 2 % 8, at % 2
    source = 32 * (8 * to_x + to_zl) + 16 * to_zh + 2 * group + last
    regroup = (source[:, None] == at[None, :]).astype(BF16)

    rows_f32 = jax.ShapeDtypeStruct(features.shape, F32)
    rows_bf16 = jax.ShapeDtypeStruct(features.shape, BF16)

    far = lax.ppermute(features, "zh", SWAP)
    near_same, near_other = over_y(features)
    near = call(near_body, rows_f32, tile, near_same, near_other)
    far_same, far_other = over_y(far)
    output, slope, mixed = call(
        forward_body, (rows_f32, rows_bf16, rows_bf16),
        tile, near, far_same, far_other, weight, cotangent,
    )

    far = lax.ppermute(slope, "zh", SWAP)
    near_same, near_other = over_y(slope)
    factors = lax.dot_general(
        regroup, mixed, (((1,), (1,)), ((), ())), preferred_element_type=F32
    ).astype(BF16)
    factors = lax.all_to_all(factors.reshape(8, 128, 128), ("y", "co"), 0, 0)
    partial = pl.pallas_call(
        partial_body,
        out_shape=jax.ShapeDtypeStruct((128, hidden), F32),
        in_specs=[pl.BlockSpec(memory_space=pltpu.SMEM), VMEM, VMEM, VMEM],
        out_specs=VMEM,
        compiler_params=pltpu.CompilerParams(vmem_limit_bytes=48 * 2**20),
    )(core.reshape(1), factors, near_same, near_other)
    near = call(near_body, rows_f32, tile, near_same, near_other)
    far_same, far_other = over_y(far)
    input_grad = call(backward_body, rows_f32, tile, near, far_same, far_other, weight)

    part = lax.all_to_all(partial.reshape(4, 32, hidden), "x", 0, 0).sum(0)
    part = lax.all_to_all(part.reshape(16, 2, hidden), ("zh", "zl"), 0, 0).sum(0)
    part = part * (65536 ** -0.5)
    weight_grad = spread(part, ("zh", "y", "co"), 16).reshape(32, hidden)
    return output, input_grad, weight_grad


def solution(mesh):
    fine = Mesh(mesh.devices.reshape(SIZES), AXES)
    rows = P(AXES)
    return jax.shard_map(
        local,
        mesh=fine,
        in_specs=(rows, P(), rows, rows, rows, rows),
        out_specs=(rows, rows, P(("x", "zl"))),
        check_vma=False,
    )
```

time: 771 us -> 212 us (0.27)
  waiting for transfers between devices: 729 us -> 45.7 us
  starting transfers between devices: 0.16 us -> 117 us
  blocking collectives: 0 us -> 26.3 us
  matrix products: 14.8 us -> 1.23 us
  between operations: 14.4 us -> 1.52 us
  Pallas kernels: 0 us -> 9.25 us
    psum x1 -> x0, waiting for transfers between devices: 272 us -> none  [local(): weight_grad = lax.psum(row_share, 'gr')]
    all_gather x2 -> x0, waiting for transfers between devices: 235 us -> none  [aggregate(): portion = lax.all_gather(source, 'gr', axis=0, tiled=True)]
    unnamed x5 -> x0, waiting for transfers between devices: 222 us -> none
    all_to_all x0 -> x6, starting transfers between devices: none -> 70.6 us  [the longest x1 44.4 us: local(): lax.all_to_all(part.reshape(16, 2, hidden), ('zh', 'zl'), 0, 0).sum(0)]
    ppermute x0 -> x6, starting transfers between devices: none -> 45.9 us  [the longest x4 18.3 us: over_y(): return (same, lax.ppermute(same, 'co', SWAP))]
    all_to_all x0 -> x6, waiting for transfers between devices: none -> 35.8 us  [the longest x4 27.3 us: spread(): lax.all_to_all(jnp.broadcast_to(rows[None], (count,) + rows.shape), axes,...]
    all_to_all x0 -> x2, blocking collectives: none -> 26.3 us  [the longest x1 17.4 us: spread(): lax.all_to_all(jnp.broadcast_to(rows[None], (count,) + rows.shape), axes,...]
    dot_general x6 -> x2, matrix products: 14.8 us -> 1.23 us  [the longest x1 0.83 us: local(): lax.dot_general(regroup, mixed, (((1,), (1,)), ((), ())), preferred_eleme...]
  transfers between devices with their start and end apart: 4 -> 12, of which waited for: 4 -> 6; matrix products, arithmetic and copies ran while one was open for 1% -> 2% of each run, Pallas kernels for 0% -> 3%
where the time goes in v1:
time: 212 us; the launch traced here: 211 us
  starting transfers between devices  117 us (55%)
  waiting for transfers between devices  45.7 us (22%)
  blocking collectives  26.3 us (12%)
  local copies, waits for them, and re-layouts  9.66 us (5%)
  Pallas kernels  9.25 us (4%)
    all_to_all x1, starting transfers between devices, local(): lax.all_to_all(part.reshape(16, 2, hidden), ('zh', 'zl'), 0, 0).sum(0)  44.4 us
    all_to_all x4, waiting for transfers between devices, spread(): lax.all_to_all(jnp.broadcast_to(rows[None], (count,) + rows.shape), axes,...  27.3 us
    all_to_all x4, starting transfers between devices, spread(): lax.all_to_all(jnp.broadcast_to(rows[None], (count,) + rows.shape), axes,...  21.2 us
    ppermute x4, starting transfers between devices, over_y(): return (same, lax.ppermute(same, 'co', SWAP))  18.3 us
    all_to_all x1, blocking collectives, spread(): lax.all_to_all(jnp.broadcast_to(rows[None], (count,) + rows.shape), axes,...  17.4 us
    ppermute x1, starting transfers between devices, local(): far = lax.ppermute(features, 'zh', SWAP)  15.6 us
    ppermute x1, starting transfers between devices, local(): far = lax.ppermute(slope, 'zh', SWAP)  12 us
    all_to_all x1, blocking collectives, local(): factors = lax.all_to_all(factors.reshape(8, 128, 128), ('y', 'co'), 0, 0)  8.92 us
  transfers between devices with their start and end apart: 12, of which 6 were waited for; matrix products, arithmetic and copies ran while one was open for 2% of the time, Pallas kernels for 3%

profile of v1, /device:TPU:1, one launch (start us, length us, event | category | flops | bytes accessed | tf_op | source)
XLA Modules:
  0.0 211.4 jit_solution(10324643512469309360)
XLA Ops:
  0.7 2.1 %broadcast_in_dim.10 = bf16[4,128,1024]{2,1,0:T(8,128)(2,1)} broadcast(bf16[128,1024]{1,0:T(8,128)(2,1)} %param.6), dimensions={1,2} | broadcast | bytes 1310720 | tf_op jit(solution)/shard_map/broadcast_in_dim | solution.py:67
  2.8 5.0 %all-to-all-start = ((bf16[4,128,1024]{2,1,0:T(8,128)(2,1)}), bf16[4,128,1024]{2,1,0:T(8,128)(2,1)S(1)}, u32[]{:S(2)}, u32[]{:S(2)}) async-start(bf16[4,128,1024]{2,1,0:T(8,128)(2,1)} %broadcast_in_dim.10), calls=%async_computation | async-start | bytes 2097152 | tf_op jit(solution)/shard_map/all_to_all | solution.py:67
  7.8 15.6 %collective-permute-start.1 = (bf16[128,1024]{1,0:T(8,128)(2,1)S(1)}, bf16[128,1024]{1,0:T(8,128)(2,1)S(1)}, u32[]{:S(2)}, u32[]{:S(2)}) collective-permute-start(bf16[128,1024]{1,0:T(8,128)(2,1)S(1)} %copy-done.5), channel_id=1, source_target_pairs={{0,256},{256,0},{1,257},{257,1},{2,258},{258,2},{3,259},{259,3},{4... | collective-permute-start | bytes 786440 | tf_op jit(solution)/shard_map/ppermute | solution.py:92
  23.4 4.7 %collective-permute-done.1 = bf16[128,1024]{1,0:T(8,128)(2,1)S(1)} collective-permute-done((bf16[128,1024]{1,0:T(8,128)(2,1)S(1)}, bf16[128,1024]{1,0:T(8,128)(2,1)S(1)}, u32[]{:S(2)}, u32[]{:S(2)}) %collective-permute-start.1) | collective-permute-done | bytes 262176 | tf_op jit(solution)/shard_map/ppermute | solution.py:92
  28.1 1.1 broadcast_in_dim.11
  29.2 3.9 %all-to-all-start.1 = ((bf16[4,128,1024]{2,1,0:T(8,128)(2,1)}), bf16[4,128,1024]{2,1,0:T(8,128)(2,1)S(1)}, u32[]{:S(2)}, u32[]{:S(2)}) async-start(bf16[4,128,1024]{2,1,0:T(8,128)(2,1)} %broadcast_in_dim.11), calls=%async_computation.1 | async-start | bytes 2097152 | tf_op jit(solution)/shard_map/all_to_all | solution.py:67
  33.2 5.3 %collective-permute-start = (bf16[512,1024]{1,0:T(8,128)(2,1)S(1)}, bf16[512,1024]{1,0:T(8,128)(2,1)}, u32[]{:S(2)}, u32[]{:S(2)}) collective-permute-start(bf16[512,1024]{1,0:T(8,128)(2,1)S(1)} %bitcast.33), channel_id=1, source_target_pairs={{0,32},{32,0},{1,33},{33,1},{2,34},{34,2},{3,35},{35,3},{4,36},{36... | collective-permute-start | bytes 3145736 | tf_op jit(solution)/shard_map/ppermute | solution.py:72
  38.5 6.1 %all-to-all-done.1 = bf16[4,128,1024]{2,1,0:T(8,128)(2,1)S(1)} async-done(((bf16[4,128,1024]{2,1,0:T(8,128)(2,1)}), bf16[4,128,1024]{2,1,0:T(8,128)(2,1)S(1)}, u32[]{:S(2)}, u32[]{:S(2)}) %all-to-all-start.1) | async-done | bytes 1048608 | tf_op jit(solution)/shard_map/all_to_all | solution.py:67
  44.6 6.5 %collective-permute-start.2 = (bf16[512,1024]{1,0:T(8,128)(2,1)S(1)}, bf16[512,1024]{1,0:T(8,128)(2,1)}, u32[]{:S(2)}, u32[]{:S(2)}) collective-permute-start(bf16[512,1024]{1,0:T(8,128)(2,1)S(1)} %bitcast.35), channel_id=1, source_target_pairs={{0,32},{32,0},{1,33},{33,1},{2,34},{34,2},{3,35},{35,3},{4,36},{36... | collective-permute-start | bytes 3145736 | tf_op jit(solution)/shard_map/ppermute | solution.py:72
  52.4 1.8 shard_map.85.near
  54.3 2.8 %shard_map.86 = (f32[128,1024]{1,0:T(8,128)}, bf16[128,1024]{1,0:T(8,128)(2,1)S(1)}, bf16[128,1024]{1,0:T(8,128)(2,1)S(1)}) custom-call(bf16[128,2048]{1,0:T(8,128)(2,1)S(1)} %bitcast.27, f32[128,1024]{1,0:T(8,128)S(1)} %shard_map.85.near, bf16[512,1024]{1,0:T(8,128)(2,1)S(1)} %bitcast.36, bf16[512,1024]{1,0:T(8,128)(2,1)} %collective-permute-done.2.far_other, ...), custom_call_target="tpu_custom_call" | custom-call | tf_op jit(solution)/shard_map/pallas_call | solution.py:20
  57.2 17.4 %all_to_all.40 = bf16[4,128,1024]{2,1,0:T(8,128)(2,1)S(1)} all-to-all(bf16[4,128,1024]{2,1,0:T(8,128)(2,1)S(1)} %broadcast_in_dim.12), channel_id=1, replica_groups=mesh['zh'=2,'y'=4,'co'=2,'x'=4,'zl'=8] {'y'}, dimensions={0} | all-to-all | bytes 2097152 | tf_op jit(solution)/shard_map/all_to_all | solution.py:67
  74.6 3.0 %collective-permute-start.3 = (bf16[512,1024]{1,0:T(8,128)(2,1)S(1)}, bf16[512,1024]{1,0:T(8,128)(2,1)S(1)}, u32[]{:S(2)}, u32[]{:S(2)}) collective-permute-start(bf16[512,1024]{1,0:T(8,128)(2,1)S(1)} %bitcast.30), channel_id=1, source_target_pairs={{0,32},{32,0},{1,33},{33,1},{2,34},{34,2},{3,35},{35,3},{4,36},{36... | collective-permute-start | bytes 3145736 | tf_op jit(solution)/shard_map/ppermute | solution.py:72
  77.6 0.8 fusion.2
  78.5 8.9 %all_to_all.41.factors = bf16[8,128,128]{2,1,0:T(8,128)(2,1)S(1)} all-to-all(bf16[8,128,128]{2,1,0:T(8,128)(2,1)S(1)} %bitcast.39), channel_id=1, replica_groups=mesh['zh'=2,'y'=4,'co'=2,'x'=4,'zl'=8] {'y','co'}, dimensions={0} | all-to-all | bytes 524288 | tf_op jit(solution)/shard_map/all_to_all | solution.py:106
  88.1 0.8 copy-done.3
  88.9 5.0 %all-to-all-start.5 = ((f32[4,32,1024]{2,1,0:T(8,128)}), f32[4,32,1024]{2,1,0:T(8,128)}, u32[]{:S(2)}, u32[]{:S(2)}) async-start(f32[4,32,1024]{2,1,0:T(8,128)} %bitcast.37), calls=%async_computation.5 | async-start | bytes 1048576 | tf_op jit(solution)/shard_map/all_to_all | solution.py:118
  93.9 12.0 %collective-permute-start.4 = (bf16[128,1024]{1,0:T(8,128)(2,1)S(1)}, bf16[128,1024]{1,0:T(8,128)(2,1)}, u32[]{:S(2)}, u32[]{:S(2)}) collective-permute-start(bf16[128,1024]{1,0:T(8,128)(2,1)S(1)} %get-tuple-element.7), channel_id=1, source_target_pairs={{0,256},{256,0},{1,257},{257,1},{2,258},{258,2},{3,259},{259,3},{4... | collective-permute-start | bytes 786440 | tf_op jit(solution)/shard_map/ppermute | solution.py:101
  105.9 5.2 %collective-permute-done.4 = bf16[128,1024]{1,0:T(8,128)(2,1)} collective-permute-done((bf16[128,1024]{1,0:T(8,128)(2,1)S(1)}, bf16[128,1024]{1,0:T(8,128)(2,1)}, u32[]{:S(2)}, u32[]{:S(2)}) %collective-permute-start.4) | collective-permute-done | bytes 262176 | tf_op jit(solution)/shard_map/ppermute | solution.py:101
  111.0 2.1 broadcast_in_dim.13
  113.1 4.2 %all-to-all-start.3 = ((bf16[4,128,1024]{2,1,0:T(8,128)(2,1)}), bf16[4,128,1024]{2,1,0:T(8,128)(2,1)}, u32[]{:S(2)}, u32[]{:S(2)}) async-start(bf16[4,128,1024]{2,1,0:T(8,128)(2,1)} %broadcast_in_dim.13), calls=%async_computation.3 | async-start | bytes 2097152 | tf_op jit(solution)/shard_map/all_to_all | solution.py:67
  117.4 1.1 reduce_sum.18
  118.4 0.7 reshape.234
  119.2 11.1 %all-to-all-done.3 = bf16[4,128,1024]{2,1,0:T(8,128)(2,1)} async-done(((bf16[4,128,1024]{2,1,0:T(8,128)(2,1)}), bf16[4,128,1024]{2,1,0:T(8,128)(2,1)}, u32[]{:S(2)}, u32[]{:S(2)}) %all-to-all-start.3) | async-done | bytes 1048608 | tf_op jit(solution)/shard_map/all_to_all | solution.py:67
  130.3 44.4 %all-to-all-start.6 = ((f32[16,2,1024]{2,1,0:T(2,128)}), f32[16,2,1024]{2,1,0:T(2,128)S(1)}, u32[]{:S(2)}, u32[]{:S(2)}) async-start(f32[16,2,1024]{2,1,0:T(2,128)} %reshape.234), calls=%async_computation.6 | async-start | bytes 262144 | tf_op jit(solution)/shard_map/all_to_all | solution.py:119
  174.8 3.5 %collective-permute-start.5 = (bf16[512,1024]{1,0:T(8,128)(2,1)}, bf16[512,1024]{1,0:T(8,128)(2,1)}, u32[]{:S(2)}, u32[]{:S(2)}) collective-permute-start(bf16[512,1024]{1,0:T(8,128)(2,1)} %bitcast.8.far_same), channel_id=1, source_target_pairs={{0,32},{32,0},{1,33},{33,1},{2,34},{34,2},{3,35},{35,3},{4,36},{36... | collective-permute-start | bytes 3145736 | tf_op jit(solution)/shard_map/ppermute | solution.py:72
  178.3 8.5 %all-to-all-done.6 = f32[16,2,1024]{2,1,0:T(2,128)S(1)} async-done(((f32[16,2,1024]{2,1,0:T(2,128)}), f32[16,2,1024]{2,1,0:T(2,128)S(1)}, u32[]{:S(2)}, u32[]{:S(2)}) %all-to-all-start.6) | async-done | bytes 131104 | tf_op jit(solution)/shard_map/all_to_all | solution.py:119
  187.5 8.0 %all-to-all-start.7 = ((f32[16,2,1024]{2,1,0:T(2,128)}), f32[16,2,1024]{2,1,0:T(2,128)S(1)}, u32[]{:S(2)}, u32[]{:S(2)}) async-start(f32[16,2,1024]{2,1,0:T(2,128)} %broadcast_in_dim.14), calls=%async_computation.7 | async-start | bytes 262144 | tf_op jit(solution)/shard_map/all_to_all | solution.py:67
  196.0 1.1 copy-done.2
  197.1 3.5 %shard_map.88 = f32[128,1024]{1,0:T(8,128)} custom-call(bf16[128,2048]{1,0:T(8,128)(2,1)S(1)} %bitcast.29, f32[128,1024]{1,0:T(8,128)S(1)} %shard_map.87.near, bf16[512,1024]{1,0:T(8,128)(2,1)} %bitcast.8.far_same, bf16[512,1024]{1,0:T(8,128)(2,1)} %collective-permute-done.5.far_other, bf16[1024,1024]{1,0:T(8,128)(2,1)S(1)} %copy-done.2), custom_call_target="tpu_custom_call" | custom-call | tf_op jit(solution)/shard_map/pallas_call | solution.py:20
  200.6 10.1 %all-to-all-done.7 = f32[16,2,1024]{2,1,0:T(2,128)S(1)} async-done(((f32[16,2,1024]{2,1,0:T(2,128)}), f32[16,2,1024]{2,1,0:T(2,128)S(1)}, u32[]{:S(2)}, u32[]{:S(2)}) %all-to-all-start.7) | async-done | bytes 131104 | tf_op jit(solution)/shard_map/all_to_all | solution.py:67
  210.6 0.7 reshape.235
  (29 shorter events, 2.7 us)
Async XLA Ops:
  0.6 51.2 %copy-start = (bf16[1,16,128,128]{3,2,1,0:T(8,128)(2,1)S(1)}, bf16[1,16,128,128]{3,2,1,0:T(8,128)(2,1)}, u32[]{:S(2)}) copy-start(bf16[1,16,128,128]{3,2,1,0:T(8,128)(2,1)} %param.9) | copy-start | bytes 1572868
  0.6 7.2 %copy-start.5 = (bf16[128,1024]{1,0:T(8,128)(2,1)S(1)}, bf16[128,1024]{1,0:T(8,128)(2,1)}, u32[]{:S(2)}) copy-start(bf16[128,1024]{1,0:T(8,128)(2,1)} %param.6) | copy-start | bytes 786436
  2.8 25.3 %all-to-all-start = ((bf16[4,128,1024]{2,1,0:T(8,128)(2,1)}), bf16[4,128,1024]{2,1,0:T(8,128)(2,1)S(1)}, u32[]{:S(2)}, u32[]{:S(2)}) async-start(bf16[4,128,1024]{2,1,0:T(8,128)(2,1)} %broadcast_in_dim.10), calls=%async_computation | async-start | bytes 2097152 | tf_op jit(solution)/shard_map/all_to_all | solution.py:67
  7.8 44.0 %copy-start.6 = (s32[1,16]{1,0:T(1,128)S(1)}, s32[1,16]{1,0:T(1,128)}, u32[]{:S(2)}) copy-start(s32[1,16]{1,0:T(1,128)} %param.10) | copy-start | bytes 196
  7.8 20.3 %collective-permute-start.1 = (bf16[128,1024]{1,0:T(8,128)(2,1)S(1)}, bf16[128,1024]{1,0:T(8,128)(2,1)S(1)}, u32[]{:S(2)}, u32[]{:S(2)}) collective-permute-start(bf16[128,1024]{1,0:T(8,128)(2,1)S(1)} %copy-done.5), channel_id=1, source_target_pairs={{0,256},{256,0},{1,257},{257,1},{2,258},{258,2},{3,259},{259,3},{4... | collective-permute-start | bytes 786440 | tf_op jit(solution)/shard_map/ppermute | solution.py:92
  29.2 15.4 %all-to-all-start.1 = ((bf16[4,128,1024]{2,1,0:T(8,128)(2,1)}), bf16[4,128,1024]{2,1,0:T(8,128)(2,1)S(1)}, u32[]{:S(2)}, u32[]{:S(2)}) async-start(bf16[4,128,1024]{2,1,0:T(8,128)(2,1)} %broadcast_in_dim.11), calls=%async_computation.1 | async-start | bytes 2097152 | tf_op jit(solution)/shard_map/all_to_all | solution.py:67
  33.2 19.3 %collective-permute-start = (bf16[512,1024]{1,0:T(8,128)(2,1)S(1)}, bf16[512,1024]{1,0:T(8,128)(2,1)}, u32[]{:S(2)}, u32[]{:S(2)}) collective-permute-start(bf16[512,1024]{1,0:T(8,128)(2,1)S(1)} %bitcast.33), channel_id=1, source_target_pairs={{0,32},{32,0},{1,33},{33,1},{2,34},{34,2},{3,35},{35,3},{4,36},{36... | collective-permute-start | bytes 3145736 | tf_op jit(solution)/shard_map/ppermute | solution.py:72
  44.6 9.7 %collective-permute-start.2 = (bf16[512,1024]{1,0:T(8,128)(2,1)S(1)}, bf16[512,1024]{1,0:T(8,128)(2,1)}, u32[]{:S(2)}, u32[]{:S(2)}) collective-permute-start(bf16[512,1024]{1,0:T(8,128)(2,1)S(1)} %bitcast.35), channel_id=1, source_target_pairs={{0,32},{32,0},{1,33},{33,1},{2,34},{34,2},{3,35},{35,3},{4,36},{36... | collective-permute-start | bytes 3145736 | tf_op jit(solution)/shard_map/ppermute | solution.py:72
  52.2 2.0 copy-start.1
  52.3 2.0 copy-start.4
  74.6 12.8 %collective-permute-start.3 = (bf16[512,1024]{1,0:T(8,128)(2,1)S(1)}, bf16[512,1024]{1,0:T(8,128)(2,1)S(1)}, u32[]{:S(2)}, u32[]{:S(2)}) collective-permute-start(bf16[512,1024]{1,0:T(8,128)(2,1)S(1)} %bitcast.30), channel_id=1, source_target_pairs={{0,32},{32,0},{1,33},{33,1},{2,34},{34,2},{3,35},{35,3},{4,36},{36... | collective-permute-start | bytes 3145736 | tf_op jit(solution)/shard_map/ppermute | solution.py:72
  88.1 0.8 copy-start.3
  88.9 22.2 %all-to-all-start.5 = ((f32[4,32,1024]{2,1,0:T(8,128)}), f32[4,32,1024]{2,1,0:T(8,128)}, u32[]{:S(2)}, u32[]{:S(2)}) async-start(f32[4,32,1024]{2,1,0:T(8,128)} %bitcast.37), calls=%async_computation.5 | async-start | bytes 1048576 | tf_op jit(solution)/shard_map/all_to_all | solution.py:118
  93.9 17.2 %collective-permute-start.4 = (bf16[128,1024]{1,0:T(8,128)(2,1)S(1)}, bf16[128,1024]{1,0:T(8,128)(2,1)}, u32[]{:S(2)}, u32[]{:S(2)}) collective-permute-start(bf16[128,1024]{1,0:T(8,128)(2,1)S(1)} %get-tuple-element.7), channel_id=1, source_target_pairs={{0,256},{256,0},{1,257},{257,1},{2,258},{258,2},{3,259},{259,3},{4... | collective-permute-start | bytes 786440 | tf_op jit(solution)/shard_map/ppermute | solution.py:101
  113.1 17.2 %all-to-all-start.3 = ((bf16[4,128,1024]{2,1,0:T(8,128)(2,1)}), bf16[4,128,1024]{2,1,0:T(8,128)(2,1)}, u32[]{:S(2)}, u32[]{:S(2)}) async-start(bf16[4,128,1024]{2,1,0:T(8,128)(2,1)} %broadcast_in_dim.13), calls=%async_computation.3 | async-start | bytes 2097152 | tf_op jit(solution)/shard_map/all_to_all | solution.py:67
  130.3 56.5 %all-to-all-start.6 = ((f32[16,2,1024]{2,1,0:T(2,128)}), f32[16,2,1024]{2,1,0:T(2,128)S(1)}, u32[]{:S(2)}, u32[]{:S(2)}) async-start(f32[16,2,1024]{2,1,0:T(2,128)} %reshape.234), calls=%async_computation.6 | async-start | bytes 262144 | tf_op jit(solution)/shard_map/all_to_all | solution.py:119
  174.8 21.2 %collective-permute-start.5 = (bf16[512,1024]{1,0:T(8,128)(2,1)}, bf16[512,1024]{1,0:T(8,128)(2,1)}, u32[]{:S(2)}, u32[]{:S(2)}) collective-permute-start(bf16[512,1024]{1,0:T(8,128)(2,1)} %bitcast.8.far_same), channel_id=1, source_target_pairs={{0,32},{32,0},{1,33},{33,1},{2,34},{34,2},{3,35},{35,3},{4,36},{36... | collective-permute-start | bytes 3145736 | tf_op jit(solution)/shard_map/ppermute | solution.py:72
  187.5 23.1 %all-to-all-start.7 = ((f32[16,2,1024]{2,1,0:T(2,128)}), f32[16,2,1024]{2,1,0:T(2,128)S(1)}, u32[]{:S(2)}, u32[]{:S(2)}) async-start(f32[16,2,1024]{2,1,0:T(2,128)} %broadcast_in_dim.14), calls=%async_computation.7 | async-start | bytes 262144 | tf_op jit(solution)/shard_map/all_to_all | solution.py:67
  195.5 1.6 copy-start.2

commit v2 on v1

--- a/solution.py
+++ b/solution.py
@@ -23,6 +23,7 @@
         in_specs=[VMEM] * len(args),
         out_specs=jax.tree.map(lambda _: VMEM, outs),
         compiler_params=pltpu.CompilerParams(vmem_limit_bytes=48 * 2**20),
+        cost_estimate=pl.CostEstimate(flops=1, bytes_accessed=1, transcendentals=0),
     )(*args)
 
 
@@ -40,10 +41,9 @@
     ).astype(BF16)
 
 
-def backward_body(tile, near, far_same, far_other, weight, input_grad):
-    total = near[...]
-    total += dot(tile[:, 1024:1536], far_same[...])
-    total += dot(tile[:, 1536:2048], far_other[...])
+def backward_body(near, far_first, far_last, weight, input_grad):
+    far = jnp.concatenate([far_first[...], far_last[...]], axis=0)
+    total = near[...] + far.astype(F32)
     input_grad[...] = lax.dot_general(
         total.astype(BF16), weight[...], (((1,), (1,)), ((), ())), preferred_element_type=F32
     )
@@ -60,7 +60,31 @@
         rows = slice(128 * y, 128 * y + 128)
         total += dot(factors[2 * y + mine], near_same[rows, :])
         total += dot(factors[2 * y + 1 - mine], near_other[rows, :])
-    partial[...] = total
+    partial[...] = total.astype(partial.dtype)
+
+
+def grouped(core, factors, near_same, near_other, dtype):
+    return pl.pallas_call(
+        partial_body,
+        out_shape=jax.ShapeDtypeStruct((128, near_same.shape[1]), dtype),
+        in_specs=[pl.BlockSpec(memory_space=pltpu.SMEM), VMEM, VMEM, VMEM],
+        out_specs=VMEM,
+        compiler_params=pltpu.CompilerParams(vmem_limit_bytes=48 * 2**20),
+        cost_estimate=pl.CostEstimate(flops=1, bytes_accessed=1, transcendentals=0),
+    )(core, factors, near_same, near_other)
+
+
+def along_z(rows, step):
+    pairs = []
+    for z in range(16):
+        for core in range(2):
+            to = (z + (step if core == 0 else -step)) % 16
+            pairs.append((z // 8 * 16 + core * 8 + z % 8, to // 8 * 16 + core * 8 + to % 8))
+    return lax.ppermute(rows, ("zh", "co", "zl"), pairs)
+
+
+def after(value, *others):
+    return lax.optimization_barrier((value,) + others)[0]
 
 
 def spread(rows, axes, count):
@@ -68,8 +92,11 @@
 
 
 def over_y(rows):
-    same = spread(rows, "y", 4).reshape(512, rows.shape[1])
-    return same, lax.ppermute(same, "co", SWAP)
+    return spread(rows, "y", 4).reshape(512, rows.shape[1])
+
+
+def other_core(rows):
+    return lax.ppermute(rows, "co", SWAP)
 
 
 def local(features, weight, cotangent, block_values, block_codes, block_count):
@@ -78,47 +105,51 @@
     grid_row = block_codes[0] % 512 // 32
     place = (grid_row // 8 ^ zh) * 8 + (grid_row % 2 ^ core) * 4 + grid_row % 8 // 2
     active = jnp.arange(16) < block_count[0]
+    other = (grid_row[:, None] == jnp.arange(8)[None, :] + 8 * (1 - zh)) & active[:, None]
+    mirror = jnp.einsum("km,kij->mji", other.astype(BF16), block_values[0], preferred_element_type=F32)
+    mirror = mirror.astype(BF16)
     select = (place[:, None] == jnp.arange(16)[None, :]) & active[:, None]
     tile = jnp.einsum("km,kij->imj", select.astype(BF16), block_values[0], preferred_element_type=F32)
     tile = tile.astype(BF16).reshape(128, 2048)
     at = jnp.arange(hidden)
-    group, to_x, to_zh, to_zl, last = at // 128, at // 32 % 4, at // 16 % 2, at // 2 % 8, at % 2
-    source = 32 * (8 * to_x + to_zl) + 16 * to_zh + 2 * group + last
+    source = 32 * (at // 4 % 32) + 4 * (at // 128) + at % 4
     regroup = (source[:, None] == at[None, :]).astype(BF16)
 
     rows_f32 = jax.ShapeDtypeStruct(features.shape, F32)
     rows_bf16 = jax.ShapeDtypeStruct(features.shape, BF16)
 
-    far = lax.ppermute(features, "zh", SWAP)
-    near_same, near_other = over_y(features)
+    far = along_z(along_z(features, 1), 7)
+    near_same = over_y(features)
+    near_other = other_core(near_same)
+    mirror = lax.all_to_all(after(mirror, near_same), ("y", "co"), 0, 0)
     near = call(near_body, rows_f32, tile, near_same, near_other)
-    far_same, far_other = over_y(far)
+    far_same = over_y(after(far, mirror))
+    far_other = other_core(far_same)
     output, slope, mixed = call(
         forward_body, (rows_f32, rows_bf16, rows_bf16),
         tile, near, far_same, far_other, weight, cotangent,
     )
 
-    far = lax.ppermute(slope, "zh", SWAP)
-    near_same, near_other = over_y(slope)
     factors = lax.dot_general(
         regroup, mixed, (((1,), (1,)), ((), ())), preferred_element_type=F32
     ).astype(BF16)
     factors = lax.all_to_all(factors.reshape(8, 128, 128), ("y", "co"), 0, 0)
-    partial = pl.pallas_call(
-        partial_body,
-        out_shape=jax.ShapeDtypeStruct((128, hidden), F32),
-        in_specs=[pl.BlockSpec(memory_space=pltpu.SMEM), VMEM, VMEM, VMEM],
-        out_specs=VMEM,
-        compiler_params=pltpu.CompilerParams(vmem_limit_bytes=48 * 2**20),
-    )(core.reshape(1), factors, near_same, near_other)
+    near_same = over_y(slope)
+    near_other = other_core(after(near_same, factors))
+    far = grouped(core.reshape(1), mirror, near_same, near_other, BF16)
+    far = along_z(far, 1)
+    half = far.shape[0] // 2
+    far_first, far_last = along_z(far[:half], 7), along_z(far[half:], 7)
+    partial = grouped(core.reshape(1), factors, near_same, near_other, BF16)
     near = call(near_body, rows_f32, tile, near_same, near_other)
-    far_same, far_other = over_y(far)
-    input_grad = call(backward_body, rows_f32, tile, near, far_same, far_other, weight)
 
-    part = lax.all_to_all(partial.reshape(4, 32, hidden), "x", 0, 0).sum(0)
-    part = lax.all_to_all(part.reshape(16, 2, hidden), ("zh", "zl"), 0, 0).sum(0)
-    part = part * (65536 ** -0.5)
-    weight_grad = spread(part, ("zh", "y", "co"), 16).reshape(32, hidden)
+    part = lax.all_to_all(after(partial, far).reshape(4, 32, hidden), "x", 0, 0)
+    part = part.astype(F32).sum(0).astype(BF16).reshape(8, 4, hidden)
+    part = jnp.concatenate([after(part, far_first)] * 2)
+    part = lax.all_to_all(part, ("zh", "zl"), 0, 0)
+    part = part.astype(F32).sum(0) * (65536 ** -0.5)
+    weight_grad = spread(after(part, far_last), ("y", "co"), 8).reshape(32, hidden)
+    input_grad = call(backward_body, rows_f32, near, far_first, far_last, weight)
     return output, input_grad, weight_grad
 
 

time: 212 us -> 194 us (0.915)
  starting transfers between devices: 117 us -> 88.8 us
  waiting for transfers between devices: 45.7 us -> 56.1 us
    ppermute x6 -> x8, waiting for transfers between devices: 9.91 us -> 40.9 us  [the longest x5 38.4 us: along_z(): return lax.ppermute(rows, ('zh', 'co', 'zl'), pairs)]
    all_to_all x2 -> x3, starting transfers between devices: 49.4 us -> 20.1 us  [the longest x1 10.6 us: local(): part = lax.all_to_all(part, ('zh', 'zl'), 0, 0)]
    all_to_all x4 -> x3, waiting for transfers between devices: 27.3 us -> 14.3 us  [spread(): lax.all_to_all(jnp.broadcast_to(rows[None], (count,) + rows.shape), axes,...]
    all_to_all x2 -> x3, waiting for transfers between devices: 8.46 us -> 0.9 us  [the longest x1 0.9 us: local(): part = lax.all_to_all(part, ('zh', 'zl'), 0, 0)]
    ppermute x6 -> x8, starting transfers between devices: 45.9 us -> 50.5 us  [the longest x5 42.8 us: along_z(): return lax.ppermute(rows, ('zh', 'co', 'zl'), pairs)]
    pallas_call x4, Pallas kernels: 8.56 us -> 5.48 us  [call(): pl.pallas_call(body, out_shape=outs, in_specs=[VMEM] * len(args), out_spe...]
    all_to_all x4 -> x3, starting transfers between devices: 21.2 us -> 18.2 us  [spread(): lax.all_to_all(jnp.broadcast_to(rows[None], (count,) + rows.shape), axes,...]
    broadcast_in_dim x5 -> x4, local copies, waits for them, and re-layouts: 6.12 us -> 4.03 us  [spread(): jnp.broadcast_to(rows[None], (count,) + rows.shape)]
  transfers between devices with their start and end apart: 12 -> 14, of which waited for: 6 -> 10; matrix products, arithmetic and copies ran while one was open for 2% -> 3% of each run, Pallas kernels for 3% -> 3%
where the time goes in v2:
time: 194 us; the launch traced here: 193 us
  starting transfers between devices  88.8 us (46%)
  waiting for transfers between devices  56.1 us (29%)
  blocking collectives  25.7 us (13%)
  local copies, waits for them, and re-layouts  10.2 us (5%)
  Pallas kernels  7.58 us (4%)
    ppermute x5, starting transfers between devices, along_z(): return lax.ppermute(rows, ('zh', 'co', 'zl'), pairs)  42.8 us
    ppermute x5, waiting for transfers between devices, along_z(): return lax.ppermute(rows, ('zh', 'co', 'zl'), pairs)  38.4 us
    all_to_all x3, starting transfers between devices, spread(): lax.all_to_all(jnp.broadcast_to(rows[None], (count,) + rows.shape), axes,...  18.2 us
    all_to_all x1, blocking collectives, spread(): lax.all_to_all(jnp.broadcast_to(rows[None], (count,) + rows.shape), axes,...  16.5 us
    all_to_all x3, waiting for transfers between devices, spread(): lax.all_to_all(jnp.broadcast_to(rows[None], (count,) + rows.shape), axes,...  14.3 us
    all_to_all x1, starting transfers between devices, local(): part = lax.all_to_all(part, ('zh', 'zl'), 0, 0)  10.6 us
    all_to_all x1, blocking collectives, local(): factors = lax.all_to_all(factors.reshape(8, 128, 128), ('y', 'co'), 0, 0)  9.22 us
    ppermute x3, starting transfers between devices, other_core(): return lax.ppermute(rows, 'co', SWAP)  7.68 us
  transfers between devices with their start and end apart: 14, of which 10 were waited for; matrix products, arithmetic and copies ran while one was open for 3% of the time, Pallas kernels for 3%

profile of v2, /device:TPU:1, one launch (start us, length us, event | category | flops | bytes accessed | tf_op | source)
XLA Modules:
  0.0 193.1 jit_solution(2271773868409746300)
XLA Ops:
  0.7 2.1 %broadcast_in_dim.8 = bf16[4,128,1024]{2,1,0:T(8,128)(2,1)} broadcast(bf16[128,1024]{1,0:T(8,128)(2,1)} %param.6), dimensions={1,2} | broadcast | bytes 1310720 | tf_op jit(solution)/shard_map/broadcast_in_dim | solution.py:91
  2.8 5.0 %all-to-all-start = ((bf16[4,128,1024]{2,1,0:T(8,128)(2,1)}), bf16[4,128,1024]{2,1,0:T(8,128)(2,1)S(1)}, u32[]{:S(2)}, u32[]{:S(2)}) async-start(bf16[4,128,1024]{2,1,0:T(8,128)(2,1)} %broadcast_in_dim.8), calls=%async_computation | async-start | bytes 2097152 | tf_op jit(solution)/shard_map/all_to_all | solution.py:91
  7.8 11.1 %collective-permute-start.1 = (bf16[128,1024]{1,0:T(8,128)(2,1)S(1)}, bf16[128,1024]{1,0:T(8,128)(2,1)S(1)}, u32[]{:S(2)}, u32[]{:S(2)}) collective-permute-start(bf16[128,1024]{1,0:T(8,128)(2,1)S(1)} %copy-done.4), channel_id=1, source_target_pairs={{0,1},{32,295},{1,2},{33,32},{2,3},{34,33},{3,4},{35,34},{4,5},{36... | collective-permute-start | bytes 786440 | tf_op jit(solution)/shard_map/ppermute | solution.py:83
  19.7 2.6 %collective-permute-done.1 = bf16[128,1024]{1,0:T(8,128)(2,1)S(1)} collective-permute-done((bf16[128,1024]{1,0:T(8,128)(2,1)S(1)}, bf16[128,1024]{1,0:T(8,128)(2,1)S(1)}, u32[]{:S(2)}, u32[]{:S(2)}) %collective-permute-start.1) | collective-permute-done | bytes 262176 | tf_op jit(solution)/shard_map/ppermute | solution.py:83
  22.2 8.0 %collective-permute-start.2 = (bf16[128,1024]{1,0:T(8,128)(2,1)S(1)}, bf16[128,1024]{1,0:T(8,128)(2,1)S(1)}, u32[]{:S(2)}, u32[]{:S(2)}) collective-permute-start(bf16[128,1024]{1,0:T(8,128)(2,1)S(1)} %collective-permute-done.1), channel_id=1, source_target_pairs={{0,7},{32,289},{1,256},{33,290},{2,257},{34,291},{3,258},{35,292},... | collective-permute-start | bytes 786440 | tf_op jit(solution)/shard_map/ppermute | solution.py:83
  31.5 5.4 %all-to-all-start.1 = ((bf16[8,128,128]{2,1,0:T(8,128)(2,1)}), bf16[8,128,128]{2,1,0:T(8,128)(2,1)S(1)}, u32[]{:S(2)}, u32[]{:S(2)}) async-start(bf16[8,128,128]{2,1,0:T(8,128)(2,1)} %bitcast.24), calls=%async_computation.1 | async-start | bytes 524288 | tf_op jit(solution)/shard_map/all_to_all | solution.py:124
  37.0 12.6 %collective-permute-done.2 = bf16[128,1024]{1,0:T(8,128)(2,1)S(1)} collective-permute-done((bf16[128,1024]{1,0:T(8,128)(2,1)S(1)}, bf16[128,1024]{1,0:T(8,128)(2,1)S(1)}, u32[]{:S(2)}, u32[]{:S(2)}) %collective-permute-start.2) | collective-permute-done | bytes 262176 | tf_op jit(solution)/shard_map/ppermute | solution.py:83
  49.5 1.1 broadcast_in_dim.9
  50.6 4.2 %all-to-all-start.2 = ((bf16[4,128,1024]{2,1,0:T(8,128)(2,1)}), bf16[4,128,1024]{2,1,0:T(8,128)(2,1)S(1)}, u32[]{:S(2)}, u32[]{:S(2)}) async-start(bf16[4,128,1024]{2,1,0:T(8,128)(2,1)} %broadcast_in_dim.9), calls=%async_computation.2 | async-start | bytes 2097152 | tf_op jit(solution)/shard_map/all_to_all | solution.py:91
  54.8 1.9 collective-permute-start
  56.7 12.3 %all-to-all-done.2 = bf16[4,128,1024]{2,1,0:T(8,128)(2,1)S(1)} async-done(((bf16[4,128,1024]{2,1,0:T(8,128)(2,1)}), bf16[4,128,1024]{2,1,0:T(8,128)(2,1)S(1)}, u32[]{:S(2)}, u32[]{:S(2)}) %all-to-all-start.2) | async-done | bytes 1048608 | tf_op jit(solution)/shard_map/all_to_all | solution.py:91
  69.0 1.9 collective-permute-start.3
  71.5 1.8 shard_map.85.near
  73.5 1.6 shard_map.86
  76.0 9.2 %all_to_all.40.factors = bf16[8,128,128]{2,1,0:T(8,128)(2,1)S(1)} all-to-all(bf16[8,128,128]{2,1,0:T(8,128)(2,1)S(1)} %bitcast.43), channel_id=1, replica_groups=mesh['zh'=2,'y'=4,'co'=2,'x'=4,'zl'=8] {'y','co'}, dimensions={0} | all-to-all | bytes 524288 | tf_op jit(solution)/shard_map/all_to_all | solution.py:136
  85.3 16.5 %all_to_all.41 = bf16[4,128,1024]{2,1,0:T(8,128)(2,1)S(1)} all-to-all(bf16[4,128,1024]{2,1,0:T(8,128)(2,1)S(1)} %broadcast_in_dim.10), channel_id=1, replica_groups=mesh['zh'=2,'y'=4,'co'=2,'x'=4,'zl'=8] {'y'}, dimensions={0} | all-to-all | bytes 2097152 | tf_op jit(solution)/shard_map/all_to_all | solution.py:91
  101.8 3.9 %collective-permute-start.4 = (bf16[512,1024]{1,0:T(8,128)(2,1)S(1)}, bf16[512,1024]{1,0:T(8,128)(2,1)S(1)}, u32[]{:S(2)}, u32[]{:S(2)}) collective-permute-start(bf16[512,1024]{1,0:T(8,128)(2,1)S(1)} %bitcast.31), channel_id=1, source_target_pairs={{0,32},{32,0},{1,33},{33,1},{2,34},{34,2},{3,35},{35,3},{4,36},{36... | collective-permute-start | bytes 3145736 | tf_op jit(solution)/shard_map/ppermute | solution.py:99
  105.7 2.3 %collective-permute-done.4.near_other = bf16[512,1024]{1,0:T(8,128)(2,1)S(1)} collective-permute-done((bf16[512,1024]{1,0:T(8,128)(2,1)S(1)}, bf16[512,1024]{1,0:T(8,128)(2,1)S(1)}, u32[]{:S(2)}, u32[]{:S(2)}) %collective-permute-start.4) | collective-permute-done | bytes 1048608 | tf_op jit(solution)/shard_map/ppermute | solution.py:99
  108.7 1.9 collective-permute-start.5
  110.6 1.4 shard_map.90
  112.0 4.1 %collective-permute-done.5 = bf16[128,1024]{1,0:T(8,128)(2,1)S(1)} collective-permute-done((bf16[128,1024]{1,0:T(8,128)(2,1)S(1)}, bf16[128,1024]{1,0:T(8,128)(2,1)S(1)}, u32[]{:S(2)}, u32[]{:S(2)}) %collective-permute-start.5) | collective-permute-done | bytes 262176 | tf_op jit(solution)/shard_map/ppermute | solution.py:83
  116.8 4.0 %all-to-all-start.5 = ((bf16[4,32,1024]{2,1,0:T(8,128)(2,1)}), bf16[4,32,1024]{2,1,0:T(8,128)(2,1)S(1)}, u32[]{:S(2)}, u32[]{:S(2)}) async-start(bf16[4,32,1024]{2,1,0:T(8,128)(2,1)} %bitcast.12), calls=%async_computation.5 | async-start | bytes 524288 | tf_op jit(solution)/shard_map/all_to_all | solution.py:146
  120.8 1.7 fusion.33
  122.5 10.7 %collective-permute-start.6 = (bf16[64,1024]{1,0:T(8,128)(2,1)}, bf16[64,1024]{1,0:T(8,128)(2,1)S(1)}, u32[]{:S(2)}, u32[]{:S(2)}) collective-permute-start(bf16[64,1024]{1,0:T(8,128)(2,1)} %get-tuple-element.24), channel_id=1, source_target_pairs={{0,7},{32,289},{1,256},{33,290},{2,257},{34,291},{3,258},{35,292},... | collective-permute-start | bytes 393224 | tf_op jit(solution)/shard_map/ppermute | solution.py:83
  134.8 10.0 %collective-permute-done.6.far_first = bf16[64,1024]{1,0:T(8,128)(2,1)S(1)} collective-permute-done((bf16[64,1024]{1,0:T(8,128)(2,1)}, bf16[64,1024]{1,0:T(8,128)(2,1)S(1)}, u32[]{:S(2)}, u32[]{:S(2)}) %collective-permute-start.6) | collective-permute-done | bytes 131104 | tf_op jit(solution)/shard_map/ppermute | solution.py:83
  145.5 10.6 %all-to-all-start.6 = ((bf16[16,4,1024]{2,1,0:T(4,128)(2,1)}), bf16[16,4,1024]{2,1,0:T(4,128)(2,1)S(1)}, u32[]{:S(2)}, u32[]{:S(2)}) async-start(bf16[16,4,1024]{2,1,0:T(4,128)(2,1)} %pad_maximum_fusion), calls=%async_computation.6 | async-start | bytes 262144 | tf_op jit(solution)/shard_map/all_to_all | solution.py:149
  156.1 11.1 %collective-permute-start.7 = (bf16[64,1024]{1,0:T(8,128)(2,1)}, bf16[64,1024]{1,0:T(8,128)(2,1)S(1)}, u32[]{:S(2)}, u32[]{:S(2)}) collective-permute-start(bf16[64,1024]{1,0:T(8,128)(2,1)} %get-tuple-element.23), channel_id=1, source_target_pairs={{0,7},{32,289},{1,256},{33,290},{2,257},{34,291},{3,258},{35,292},... | collective-permute-start | bytes 393224 | tf_op jit(solution)/shard_map/ppermute | solution.py:83
  168.2 9.2 %collective-permute-done.7.far_last = bf16[64,1024]{1,0:T(8,128)(2,1)S(1)} collective-permute-done((bf16[64,1024]{1,0:T(8,128)(2,1)}, bf16[64,1024]{1,0:T(8,128)(2,1)S(1)}, u32[]{:S(2)}, u32[]{:S(2)}) %collective-permute-start.7) | collective-permute-done | bytes 131104 | tf_op jit(solution)/shard_map/ppermute | solution.py:83
  178.1 9.0 %all-to-all-start.7 = ((f32[8,4,1024]{2,1,0:T(4,128)}), f32[8,4,1024]{2,1,0:T(4,128)S(1)}, u32[]{:S(2)}, u32[]{:S(2)}) async-start(f32[8,4,1024]{2,1,0:T(4,128)} %broadcast_in_dim.11), calls=%async_computation.7 | async-start | bytes 262144 | tf_op jit(solution)/shard_map/all_to_all | solution.py:91
  187.6 1.1 copy-done.2
  188.7 1.6 shard_map.89
  190.3 2.1 %all-to-all-done.7 = f32[8,4,1024]{2,1,0:T(4,128)S(1)} async-done(((f32[8,4,1024]{2,1,0:T(4,128)}), f32[8,4,1024]{2,1,0:T(4,128)S(1)}, u32[]{:S(2)}, u32[]{:S(2)}) %all-to-all-start.7) | async-done | bytes 131104 | tf_op jit(solution)/shard_map/all_to_all | solution.py:91
  (38 shorter events, 9.5 us)
Async XLA Ops:
  0.6 29.6 %copy-start = (bf16[1,16,128,128]{3,2,1,0:T(8,128)(2,1)S(1)}, bf16[1,16,128,128]{3,2,1,0:T(8,128)(2,1)}, u32[]{:S(2)}) copy-start(bf16[1,16,128,128]{3,2,1,0:T(8,128)(2,1)} %param.9) | copy-start | bytes 1572868
  0.6 7.2 %copy-start.4 = (bf16[128,1024]{1,0:T(8,128)(2,1)S(1)}, bf16[128,1024]{1,0:T(8,128)(2,1)}, u32[]{:S(2)}) copy-start(bf16[128,1024]{1,0:T(8,128)(2,1)} %param.6) | copy-start | bytes 786436
  0.7 19.0 %copy-start.6 = (s32[1,16]{1,0:T(1,128)S(1)}, s32[1,16]{1,0:T(1,128)}, u32[]{:S(2)}) copy-start(s32[1,16]{1,0:T(1,128)} %param.10) | copy-start | bytes 196
  2.8 28.7 %all-to-all-start = ((bf16[4,128,1024]{2,1,0:T(8,128)(2,1)}), bf16[4,128,1024]{2,1,0:T(8,128)(2,1)S(1)}, u32[]{:S(2)}, u32[]{:S(2)}) async-start(bf16[4,128,1024]{2,1,0:T(8,128)(2,1)} %broadcast_in_dim.8), calls=%async_computation | async-start | bytes 2097152 | tf_op jit(solution)/shard_map/all_to_all | solution.py:91
  7.8 14.4 %collective-permute-start.1 = (bf16[128,1024]{1,0:T(8,128)(2,1)S(1)}, bf16[128,1024]{1,0:T(8,128)(2,1)S(1)}, u32[]{:S(2)}, u32[]{:S(2)}) collective-permute-start(bf16[128,1024]{1,0:T(8,128)(2,1)S(1)} %copy-done.4), channel_id=1, source_target_pairs={{0,1},{32,295},{1,2},{33,32},{2,3},{34,33},{3,4},{35,34},{4,5},{36... | collective-permute-start | bytes 786440 | tf_op jit(solution)/shard_map/ppermute | solution.py:83
  22.2 27.3 %collective-permute-start.2 = (bf16[128,1024]{1,0:T(8,128)(2,1)S(1)}, bf16[128,1024]{1,0:T(8,128)(2,1)S(1)}, u32[]{:S(2)}, u32[]{:S(2)}) collective-permute-start(bf16[128,1024]{1,0:T(8,128)(2,1)S(1)} %collective-permute-done.1), channel_id=1, source_target_pairs={{0,7},{32,289},{1,256},{33,290},{2,257},{34,291},{3,258},{35,292},... | collective-permute-start | bytes 786440 | tf_op jit(solution)/shard_map/ppermute | solution.py:83
  31.5 18.0 %all-to-all-start.1 = ((bf16[8,128,128]{2,1,0:T(8,128)(2,1)}), bf16[8,128,128]{2,1,0:T(8,128)(2,1)S(1)}, u32[]{:S(2)}, u32[]{:S(2)}) async-start(bf16[8,128,128]{2,1,0:T(8,128)(2,1)} %bitcast.24), calls=%async_computation.1 | async-start | bytes 524288 | tf_op jit(solution)/shard_map/all_to_all | solution.py:124
  50.6 18.3 %all-to-all-start.2 = ((bf16[4,128,1024]{2,1,0:T(8,128)(2,1)}), bf16[4,128,1024]{2,1,0:T(8,128)(2,1)S(1)}, u32[]{:S(2)}, u32[]{:S(2)}) async-start(bf16[4,128,1024]{2,1,0:T(8,128)(2,1)} %broadcast_in_dim.9), calls=%async_computation.2 | async-start | bytes 2097152 | tf_op jit(solution)/shard_map/all_to_all | solution.py:91
  54.8 16.7 %collective-permute-start = (bf16[512,1024]{1,0:T(8,128)(2,1)S(1)}, bf16[512,1024]{1,0:T(8,128)(2,1)}, u32[]{:S(2)}, u32[]{:S(2)}) collective-permute-start(bf16[512,1024]{1,0:T(8,128)(2,1)S(1)} %bitcast.38), channel_id=1, source_target_pairs={{0,32},{32,0},{1,33},{33,1},{2,34},{34,2},{3,35},{35,3},{4,36},{36... | collective-permute-start | bytes 3145736 | tf_op jit(solution)/shard_map/ppermute | solution.py:99
  69.0 4.5 %collective-permute-start.3 = (bf16[512,1024]{1,0:T(8,128)(2,1)S(1)}, bf16[512,1024]{1,0:T(8,128)(2,1)S(1)}, u32[]{:S(2)}, u32[]{:S(2)}) collective-permute-start(bf16[512,1024]{1,0:T(8,128)(2,1)S(1)} %bitcast.40), channel_id=1, source_target_pairs={{0,32},{32,0},{1,33},{33,1},{2,34},{34,2},{3,35},{35,3},{4,36},{36... | collective-permute-start | bytes 3145736 | tf_op jit(solution)/shard_map/ppermute | solution.py:99
  71.3 2.2 %copy-start.1 = (bf16[1024,1024]{1,0:T(8,128)(2,1)S(1)}, bf16[1024,1024]{1,0:T(8,128)(2,1)}, u32[]{:S(2)}) copy-start(bf16[1024,1024]{1,0:T(8,128)(2,1)} %weight.3) | copy-start | bytes 6291460
  71.3 2.2 %copy-start.3 = (bf16[128,1024]{1,0:T(8,128)(2,1)S(1)}, bf16[128,1024]{1,0:T(8,128)(2,1)}, u32[]{:S(2)}) copy-start(bf16[128,1024]{1,0:T(8,128)(2,1)} %cotangent.1) | copy-start | bytes 786436
  101.8 6.1 %collective-permute-start.4 = (bf16[512,1024]{1,0:T(8,128)(2,1)S(1)}, bf16[512,1024]{1,0:T(8,128)(2,1)S(1)}, u32[]{:S(2)}, u32[]{:S(2)}) collective-permute-start(bf16[512,1024]{1,0:T(8,128)(2,1)S(1)} %bitcast.31), channel_id=1, source_target_pairs={{0,32},{32,0},{1,33},{33,1},{2,34},{34,2},{3,35},{35,3},{4,36},{36... | collective-permute-start | bytes 3145736 | tf_op jit(solution)/shard_map/ppermute | solution.py:99
  108.7 7.4 %collective-permute-start.5 = (bf16[128,1024]{1,0:T(8,128)(2,1)S(1)}, bf16[128,1024]{1,0:T(8,128)(2,1)S(1)}, u32[]{:S(2)}, u32[]{:S(2)}) collective-permute-start(bf16[128,1024]{1,0:T(8,128)(2,1)S(1)} %shard_map.88), channel_id=1, source_target_pairs={{0,1},{32,295},{1,2},{33,32},{2,3},{34,33},{3,4},{35,34},{4,5},{36... | collective-permute-start | bytes 786440 | tf_op jit(solution)/shard_map/ppermute | solution.py:83
  116.1 0.7 copy-start.5
  116.8 16.4 %all-to-all-start.5 = ((bf16[4,32,1024]{2,1,0:T(8,128)(2,1)}), bf16[4,32,1024]{2,1,0:T(8,128)(2,1)S(1)}, u32[]{:S(2)}, u32[]{:S(2)}) async-start(bf16[4,32,1024]{2,1,0:T(8,128)(2,1)} %bitcast.12), calls=%async_computation.5 | async-start | bytes 524288 | tf_op jit(solution)/shard_map/all_to_all | solution.py:146
  122.5 22.3 %collective-permute-start.6 = (bf16[64,1024]{1,0:T(8,128)(2,1)}, bf16[64,1024]{1,0:T(8,128)(2,1)S(1)}, u32[]{:S(2)}, u32[]{:S(2)}) collective-permute-start(bf16[64,1024]{1,0:T(8,128)(2,1)} %get-tuple-element.24), channel_id=1, source_target_pairs={{0,7},{32,289},{1,256},{33,290},{2,257},{34,291},{3,258},{35,292},... | collective-permute-start | bytes 393224 | tf_op jit(solution)/shard_map/ppermute | solution.py:83
  145.5 22.6 %all-to-all-start.6 = ((bf16[16,4,1024]{2,1,0:T(4,128)(2,1)}), bf16[16,4,1024]{2,1,0:T(4,128)(2,1)S(1)}, u32[]{:S(2)}, u32[]{:S(2)}) async-start(bf16[16,4,1024]{2,1,0:T(4,128)(2,1)} %pad_maximum_fusion), calls=%async_computation.6 | async-start | bytes 262144 | tf_op jit(solution)/shard_map/all_to_all | solution.py:149
  156.1 21.3 %collective-permute-start.7 = (bf16[64,1024]{1,0:T(8,128)(2,1)}, bf16[64,1024]{1,0:T(8,128)(2,1)S(1)}, u32[]{:S(2)}, u32[]{:S(2)}) collective-permute-start(bf16[64,1024]{1,0:T(8,128)(2,1)} %get-tuple-element.23), channel_id=1, source_target_pairs={{0,7},{32,289},{1,256},{33,290},{2,257},{34,291},{3,258},{35,292},... | collective-permute-start | bytes 393224 | tf_op jit(solution)/shard_map/ppermute | solution.py:83
  178.1 14.3 %all-to-all-start.7 = ((f32[8,4,1024]{2,1,0:T(4,128)}), f32[8,4,1024]{2,1,0:T(4,128)S(1)}, u32[]{:S(2)}, u32[]{:S(2)}) async-start(f32[8,4,1024]{2,1,0:T(4,128)} %broadcast_in_dim.11), calls=%async_computation.7 | async-start | bytes 262144 | tf_op jit(solution)/shard_map/all_to_all | solution.py:91
  187.1 1.6 copy-start.2

commit v3 on v2

v3 whole, which is shorter than its diff:
```python
import jax
import jax.numpy as jnp
from jax import lax
from jax.experimental import pallas as pl
from jax.experimental.pallas import tpu as pltpu
from jax.sharding import Mesh, PartitionSpec as P

AXES = ("zh", "y", "co", "x", "zl")
SIZES = (2, 4, 2, 4, 8)
BF16, F32 = jnp.bfloat16, jnp.float32
SWAP = [(0, 1), (1, 0)]
VMEM = pl.BlockSpec(memory_space=pltpu.VMEM)
SMEM = pl.BlockSpec(memory_space=pltpu.SMEM)
COLS = slice(0, 1024)


def dot(a, b, over_a=1, over_b=0):
    return lax.dot_general(a, b, (((over_a,), (over_b,)), ((), ())), preferred_element_type=F32)


def call(body, outs, *args, flops=1):
    return pl.pallas_call(
        body,
        out_shape=outs,
        in_specs=[SMEM if a.shape == (1,) else VMEM for a in args],
        out_specs=jax.tree.map(lambda _: VMEM, outs),
        compiler_params=pltpu.CompilerParams(vmem_limit_bytes=48 * 2**20),
        cost_estimate=pl.CostEstimate(flops=flops, bytes_accessed=1, transcendentals=0),
    )(*args)


def block_dot(tile, first, same, other):
    total = 0.0
    for y in range(4):
        at = 128 * (first + y)
        total += dot(tile[:, at : at + 128], same[y, :, COLS])
        total += dot(tile[:, at + 512 : at + 640], other[y, :, COLS])
    return total


def near_body(tile, same, other, near):
    near[...] = block_dot(tile, 0, same, other)


def forward_body(tile, near, same, other, weight, cotangent, regroup, out, message):
    total = near[...] + block_dot(tile, 8, same, other)
    high = total.astype(BF16)
    low = (total - high.astype(F32)).astype(BF16)
    summed = dot(high, weight[...]) + dot(low, weight[...])
    sigmoid = jax.nn.sigmoid(summed)
    out[...] = summed * sigmoid
    slope = cotangent[...].astype(F32) * sigmoid * (1.0 + summed * (1.0 - sigmoid))
    slope = slope.astype(BF16)
    factor = dot(high, regroup[...]).astype(BF16)
    for y in range(4):
        message[y, :, COLS] = slope
        message[y, :, 1024:1280] = factor[:, 256 * y : 256 * y + 256]


def far_body(core, mirror, same, other, far):
    mine = core[0]
    total = 0.0
    for y in range(4):
        total += dot(mirror[2 * y + mine], same[y, :, COLS])
        total += dot(mirror[2 * y + 1 - mine], other[y, :, COLS])
    far[...] = total.astype(BF16)


def partial_body(same, other, partial):
    total = 0.0
    for y in range(4):
        total += dot(same[y, :, 1024:1152], same[y, :, COLS], 0, 0)
        total += dot(other[y, :, 1152:1280], other[y, :, COLS], 0, 0)
    partial[...] = total


def sum_x_body(pieces, out):
    total = pieces[0] + pieces[1] + pieces[2] + pieces[3]
    for z in range(8):
        rows = total[4 * z : 4 * z + 4].astype(BF16)
        out[z] = rows
        out[z + 8] = rows


def sum_z_body(pieces, out):
    total = pieces[0].astype(F32)
    for z in range(1, 16):
        total += pieces[z].astype(F32)
    for group in range(8):
        out[group] = total * (65536 ** -0.5)


def backward_body(tile, same, other, far, back_grad):
    total = block_dot(tile, 0, same, other) + far[...].astype(F32)
    back_grad[...] = total.astype(BF16)


def input_body(back_grad, weight, input_grad):
    input_grad[...] = dot(back_grad[...], weight[...], 1, 1)


def along_z(rows, step):
    pairs = []
    for z in range(16):
        for core in range(2):
            to = (z + (step if core == 0 else -step)) % 16
            pairs.append((z // 8 * 16 + core * 8 + z % 8, to // 8 * 16 + core * 8 + to % 8))
    return lax.ppermute(rows, ("zh", "co", "zl"), pairs)


def after(value, *others):
    return lax.optimization_barrier((value,) + others)[0]


def over_y(rows):
    return lax.all_to_all(jnp.broadcast_to(rows[None], (4,) + rows.shape), "y", 0, 0)


def other_core(rows):
    return lax.ppermute(rows, "co", SWAP)


def local(features, weight, cotangent, block_values, block_codes, block_count):
    zh, core = lax.axis_index("zh"), lax.axis_index("co")
    hidden = features.shape[1]
    grid_row = block_codes[0] % 512 // 32
    place = (grid_row // 8 ^ zh) * 8 + (grid_row % 2 ^ core) * 4 + grid_row % 8 // 2
    active = jnp.arange(16) < block_count[0]
    other = (grid_row[:, None] == jnp.arange(8)[None, :] + 8 * (1 - zh)) & active[:, None]
    mirror = jnp.einsum("km,kij->mji", other.astype(BF16), block_values[0], preferred_element_type=F32)
    mirror = mirror.astype(BF16)
    select = (place[:, None] == jnp.arange(16)[None, :]) & active[:, None]
    tile = jnp.einsum("km,kij->imj", select.astype(BF16), block_values[0], preferred_element_type=F32)
    tile = tile.astype(BF16).reshape(128, 2048)
    at = jnp.arange(hidden)
    group = 2 * (at // 256) + (at // 128 % 2 ^ core)
    source = 32 * (at // 4 % 32) + 4 * group + at % 4
    regroup = (jnp.arange(hidden)[:, None] == source[None, :]).astype(BF16)

    def shape(*dims, dtype=F32):
        return jax.ShapeDtypeStruct(dims, dtype)

    rows_f32, rows_bf16 = shape(128, hidden), shape(128, hidden, dtype=BF16)

    far = along_z(along_z(features, 1), 7)
    near_same = over_y(features)
    near_other = other_core(near_same)
    mirror = lax.all_to_all(after(mirror, near_same), ("y", "co"), 0, 0)
    near = call(near_body, rows_f32, tile, near_same, near_other)
    far_same = over_y(after(far, mirror))
    far_other = other_core(far_same)
    output, message = call(
        forward_body, (rows_f32, shape(4, 128, hidden + 256, dtype=BF16)),
        tile, near, far_same, far_other, weight, cotangent, regroup,
    )

    near_same = lax.all_to_all(message, "y", 0, 0)
    near_other = other_core(near_same)
    far = call(far_body, rows_bf16, core.reshape(1), mirror, near_same, near_other)
    far = along_z(far, 1)
    partial = call(partial_body, rows_f32, near_same, near_other)
    part = lax.all_to_all(partial.reshape(4, 32, hidden), "x", 0, 0)
    part = call(sum_x_body, shape(16, 4, hidden, dtype=BF16), part)
    part, far = lax.optimization_barrier((part, far))
    far = along_z(far, 7)
    part = lax.all_to_all(part, ("zh", "zl"), 0, 0)
    back_grad = call(
        backward_body, rows_bf16, tile, near_same, near_other, far, flops=10**11
    )
    part = call(sum_z_body, shape(8, 4, hidden), after(part, back_grad))
    part = lax.all_to_all(part, ("y", "co"), 0, 0)
    weight_grad = part.reshape(32, hidden)
    input_grad = call(input_body, rows_f32, back_grad, weight)
    return output, input_grad, weight_grad


def solution(mesh):
    fine = Mesh(mesh.devices.reshape(SIZES), AXES)
    rows = P(AXES)
    return jax.shard_map(
        local,
        mesh=fine,
        in_specs=(rows, P(), rows, rows, rows, rows),
        out_specs=(rows, rows, P(("x", "zl"))),
        check_vma=False,
    )
```

time: 194 us -> 174 us (0.90)
  starting transfers between devices: 88.8 us -> 68.1 us
  blocking collectives: 25.7 us -> 19.9 us
  Pallas kernels: 7.58 us -> 13.2 us
    ppermute x5 -> x4, starting transfers between devices: 42.8 us -> 30.3 us  [along_z(): return lax.ppermute(rows, ('zh', 'co', 'zl'), pairs)]
    ppermute x5 -> x4, waiting for transfers between devices: 38.4 us -> 26.5 us  [along_z(): return lax.ppermute(rows, ('zh', 'co', 'zl'), pairs)]
    all_to_all x1, waiting for transfers between devices: 0.9 us -> 6.84 us  [local(): part = lax.all_to_all(part, ('zh', 'zl'), 0, 0)]
    all_to_all x2 -> x1, blocking collectives: 25.7 us -> 19.9 us  [local(): near_same = lax.all_to_all(message, 'y', 0, 0)]
    all_to_all x4, waiting for transfers between devices: 14.3 us -> 20.1 us  [the longest x2 12.3 us: over_y(): lax.all_to_all(jnp.broadcast_to(rows[None], (4,) + rows.shape), 'y', 0, 0)]
    pallas_call x6 -> x8, Pallas kernels: 7.58 us -> 13.2 us  [call(): pl.pallas_call(body, out_shape=outs, in_specs=[SMEM if a.shape == (1,) el...]
    all_to_all x4, starting transfers between devices: 22.2 us -> 18.3 us  [the longest x2 9.18 us: over_y(): lax.all_to_all(jnp.broadcast_to(rows[None], (4,) + rows.shape), 'y', 0, 0)]
    all_to_all x1, starting transfers between devices: 10.6 us -> 7.01 us  [local(): part = lax.all_to_all(part, ('zh', 'zl'), 0, 0)]
  transfers between devices with their start and end apart: 14 -> 13, of which waited for: 10 -> 8; matrix products, arithmetic and copies ran while one was open for 3% -> 2% of each run, Pallas kernels for 3% -> 4%
where the time goes in v3:
time: 174 us; the launch traced here: 172 us
  starting transfers between devices  68.1 us (39%)
  waiting for transfers between devices  56.1 us (32%)
  blocking collectives  19.9 us (11%)
  Pallas kernels  13.2 us (8%)
  local copies, waits for them, and re-layouts  10.1 us (6%)
  other arithmetic  2.29 us (1%)
    ppermute x4, starting transfers between devices, along_z(): return lax.ppermute(rows, ('zh', 'co', 'zl'), pairs)  30.3 us
    ppermute x4, waiting for transfers between devices, along_z(): return lax.ppermute(rows, ('zh', 'co', 'zl'), pairs)  26.5 us
    all_to_all x1, blocking collectives, local(): near_same = lax.all_to_all(message, 'y', 0, 0)  19.9 us
    pallas_call x8, Pallas kernels, call(): pl.pallas_call(body, out_shape=outs, in_specs=[SMEM if a.shape == (1,) el...  13.2 us
    all_to_all x2, waiting for transfers between devices, over_y(): lax.all_to_all(jnp.broadcast_to(rows[None], (4,) + rows.shape), 'y', 0, 0)  12.3 us
    all_to_all x2, starting transfers between devices, over_y(): lax.all_to_all(jnp.broadcast_to(rows[None], (4,) + rows.shape), 'y', 0, 0)  9.18 us
    ppermute x3, starting transfers between devices, other_core(): return lax.ppermute(rows, 'co', SWAP)  7.06 us
    all_to_all x1, starting transfers between devices, local(): part = lax.all_to_all(part, ('zh', 'zl'), 0, 0)  7.01 us
  transfers between devices with their start and end apart: 13, of which 8 were waited for; matrix products, arithmetic and copies ran while one was open for 2% of the time, Pallas kernels for 4%

profile of v3, /device:TPU:1, one launch (start us, length us, event | category | flops | bytes accessed | tf_op | source)
XLA Modules:
  0.0 172.1 jit_solution(10184261883561576719)
XLA Ops:
  0.7 2.1 %broadcast_in_dim.4 = bf16[4,128,1024]{2,1,0:T(8,128)(2,1)} broadcast(bf16[128,1024]{1,0:T(8,128)(2,1)} %param.6), dimensions={1,2} | broadcast | bytes 1310720 | tf_op jit(solution)/shard_map/broadcast_in_dim | solution.py:116
  2.8 5.0 %all-to-all-start = ((bf16[4,128,1024]{2,1,0:T(8,128)(2,1)}), bf16[4,128,1024]{2,1,0:T(8,128)(2,1)S(1)}, u32[]{:S(2)}, u32[]{:S(2)}) async-start(bf16[4,128,1024]{2,1,0:T(8,128)(2,1)} %broadcast_in_dim.4), calls=%async_computation | async-start | bytes 2097152 | tf_op jit(solution)/shard_map/all_to_all | solution.py:116
  7.8 11.1 %collective-permute-start.1 = (bf16[128,1024]{1,0:T(8,128)(2,1)S(1)}, bf16[128,1024]{1,0:T(8,128)(2,1)S(1)}, u32[]{:S(2)}, u32[]{:S(2)}) collective-permute-start(bf16[128,1024]{1,0:T(8,128)(2,1)S(1)} %copy-done.8), channel_id=1, source_target_pairs={{0,1},{32,295},{1,2},{33,32},{2,3},{34,33},{3,4},{35,34},{4,5},{36... | collective-permute-start | bytes 786440 | tf_op jit(solution)/shard_map/ppermute | solution.py:108
  19.7 2.6 %collective-permute-done.1 = bf16[128,1024]{1,0:T(8,128)(2,1)S(1)} collective-permute-done((bf16[128,1024]{1,0:T(8,128)(2,1)S(1)}, bf16[128,1024]{1,0:T(8,128)(2,1)S(1)}, u32[]{:S(2)}, u32[]{:S(2)}) %collective-permute-start.1) | collective-permute-done | bytes 262176 | tf_op jit(solution)/shard_map/ppermute | solution.py:108
  22.2 8.0 %collective-permute-start.2 = (bf16[128,1024]{1,0:T(8,128)(2,1)S(1)}, bf16[128,1024]{1,0:T(8,128)(2,1)S(1)}, u32[]{:S(2)}, u32[]{:S(2)}) collective-permute-start(bf16[128,1024]{1,0:T(8,128)(2,1)S(1)} %collective-permute-done.1), channel_id=1, source_target_pairs={{0,7},{32,289},{1,256},{33,290},{2,257},{34,291},{3,258},{35,292},... | collective-permute-start | bytes 786440 | tf_op jit(solution)/shard_map/ppermute | solution.py:108
  31.5 5.4 %all-to-all-start.1 = ((bf16[8,128,128]{2,1,0:T(8,128)(2,1)}), bf16[8,128,128]{2,1,0:T(8,128)(2,1)S(1)}, u32[]{:S(2)}, u32[]{:S(2)}) async-start(bf16[8,128,128]{2,1,0:T(8,128)(2,1)} %bitcast.20), calls=%async_computation.1 | async-start | bytes 524288 | tf_op jit(solution)/shard_map/all_to_all | solution.py:148
  37.0 12.6 %collective-permute-done.2 = bf16[128,1024]{1,0:T(8,128)(2,1)S(1)} collective-permute-done((bf16[128,1024]{1,0:T(8,128)(2,1)S(1)}, bf16[128,1024]{1,0:T(8,128)(2,1)S(1)}, u32[]{:S(2)}, u32[]{:S(2)}) %collective-permute-start.2) | collective-permute-done | bytes 262176 | tf_op jit(solution)/shard_map/ppermute | solution.py:108
  49.5 1.1 broadcast_in_dim.5
  50.6 4.2 %all-to-all-start.2 = ((bf16[4,128,1024]{2,1,0:T(8,128)(2,1)}), bf16[4,128,1024]{2,1,0:T(8,128)(2,1)S(1)}, u32[]{:S(2)}, u32[]{:S(2)}) async-start(bf16[4,128,1024]{2,1,0:T(8,128)(2,1)} %broadcast_in_dim.5), calls=%async_computation.2 | async-start | bytes 2097152 | tf_op jit(solution)/shard_map/all_to_all | solution.py:116
  54.8 1.9 %collective-permute-start = (bf16[4,128,1024]{2,1,0:T(8,128)(2,1)S(1)}, bf16[4,128,1024]{2,1,0:T(8,128)(2,1)}, u32[]{:S(2)}, u32[]{:S(2)}) collective-permute-start(bf16[4,128,1024]{2,1,0:T(8,128)(2,1)S(1)} %all-to-all-done.same), channel_id=1, source_target_pairs={{0,32},{32,0},{1,33},{33,1},{2,34},{34,2},{3,35},{35,3},{4,36},{36... | collective-permute-start | bytes 3145736 | tf_op jit(solution)/shard_map/ppermute | solution.py:120
  56.7 12.3 %all-to-all-done.2.same = bf16[4,128,1024]{2,1,0:T(8,128)(2,1)S(1)} async-done(((bf16[4,128,1024]{2,1,0:T(8,128)(2,1)}), bf16[4,128,1024]{2,1,0:T(8,128)(2,1)S(1)}, u32[]{:S(2)}, u32[]{:S(2)}) %all-to-all-start.2) | async-done | bytes 1048608 | tf_op jit(solution)/shard_map/all_to_all | solution.py:116
  69.0 1.9 %collective-permute-start.3 = (bf16[4,128,1024]{2,1,0:T(8,128)(2,1)S(1)}, bf16[4,128,1024]{2,1,0:T(8,128)(2,1)S(1)}, u32[]{:S(2)}, u32[]{:S(2)}) collective-permute-start(bf16[4,128,1024]{2,1,0:T(8,128)(2,1)S(1)} %all-to-all-done.2.same), channel_id=1, source_target_pairs={{0,32},{32,0},{1,33},{33,1},{2,34},{34,2},{3,35},{35,3},{4,36},{36... | collective-permute-start | bytes 3145736 | tf_op jit(solution)/shard_map/ppermute | solution.py:120
  71.5 2.2 %fusion.regroup = bf16[1024,1024]{1,0:T(8,128)(2,1)} fusion(s32[1024]{0:T(1024)S(1)} %fusion.16), kind=kLoop, calls=%fused_computation.1 | loop fusion | flops 2097152 | bytes 2101248 | tf_op jit(solution)/shard_map/convert_element_type | solution.py:138
  73.7 1.9 %shard_map.85.near = f32[128,1024]{1,0:T(8,128)S(1)} custom-call(bf16[128,2048]{1,0:T(8,128)(2,1)S(1)} %bitcast.26, bf16[4,128,1024]{2,1,0:T(8,128)(2,1)S(1)} %all-to-all-done.same, bf16[4,128,1024]{2,1,0:T(8,128)(2,1)} %collective-permute-done.other), custom_call_target="tpu_custom_call" | custom-call | flops 1 | bytes 1 | tf_op jit(solution)/shard_map/pallas_call | solution.py:22
  75.7 4.5 %shard_map.86 = (f32[128,1024]{1,0:T(8,128)}, bf16[4,128,1280]{2,1,0:T(8,128)(2,1)S(1)}) custom-call(bf16[128,2048]{1,0:T(8,128)(2,1)S(1)} %bitcast.27, f32[128,1024]{1,0:T(8,128)S(1)} %shard_map.85.near, bf16[4,128,1024]{2,1,0:T(8,128)(2,1)S(1)} %all-to-all-done.2.same, bf16[4,128,1024]{2,1,0:T(8,128)(2,1)S(1)} %collective-permute-done.3.other, ...), custom_call_target="tpu_custom_call" | custom-call | flops 1 | bytes 1 | tf_op jit(solution)/shard_map/pallas_call | solution.py:22
  80.2 19.9 %all_to_all.35.same = bf16[4,128,1280]{2,1,0:T(8,128)(2,1)S(1)} all-to-all(bf16[4,128,1280]{2,1,0:T(8,128)(2,1)S(1)} %get-tuple-element.13), channel_id=1, replica_groups=mesh['zh'=2,'y'=4,'co'=2,'x'=4,'zl'=8] {'y'}, dimensions={0} | all-to-all | bytes 2621440 | tf_op jit(solution)/shard_map/all_to_all | solution.py:157
  100.1 3.2 %collective-permute-start.4 = (bf16[4,128,1280]{2,1,0:T(8,128)(2,1)S(1)}, bf16[4,128,1280]{2,1,0:T(8,128)(2,1)S(1)}, u32[]{:S(2)}, u32[]{:S(2)}) collective-permute-start(bf16[4,128,1280]{2,1,0:T(8,128)(2,1)S(1)} %all_to_all.35.same), channel_id=1, source_target_pairs={{0,32},{32,0},{1,33},{33,1},{2,34},{34,2},{3,35},{35,3},{4,36},{36... | collective-permute-start | bytes 3932168 | tf_op jit(solution)/shard_map/ppermute | solution.py:120
  103.4 2.6 %collective-permute-done.4.other = bf16[4,128,1280]{2,1,0:T(8,128)(2,1)S(1)} collective-permute-done((bf16[4,128,1280]{2,1,0:T(8,128)(2,1)S(1)}, bf16[4,128,1280]{2,1,0:T(8,128)(2,1)S(1)}, u32[]{:S(2)}, u32[]{:S(2)}) %collective-permute-start.4) | collective-permute-done | bytes 1310752 | tf_op jit(solution)/shard_map/ppermute | solution.py:120
  107.6 4.1 %all-to-all-start.4 = ((f32[4,32,1024]{2,1,0:T(8,128)}), f32[4,32,1024]{2,1,0:T(8,128)}, u32[]{:S(2)}, u32[]{:S(2)}) async-start(f32[4,32,1024]{2,1,0:T(8,128)} %bitcast.29), calls=%async_computation.4 | async-start | bytes 1048576 | tf_op jit(solution)/shard_map/all_to_all | solution.py:162
  111.7 1.4 shard_map.89
  113.1 1.9 %collective-permute-start.5 = (bf16[128,1024]{1,0:T(8,128)(2,1)}, bf16[128,1024]{1,0:T(8,128)(2,1)}, u32[]{:S(2)}, u32[]{:S(2)}) collective-permute-start(bf16[128,1024]{1,0:T(8,128)(2,1)} %shard_map.89), channel_id=1, source_target_pairs={{0,1},{32,295},{1,2},{33,32},{2,3},{34,33},{3,4},{35,34},{4,5},{36... | collective-permute-start | bytes 786440 | tf_op jit(solution)/shard_map/ppermute | solution.py:108
  115.0 5.8 %all-to-all-done.4.pieces = f32[4,32,1024]{2,1,0:T(8,128)} async-done(((f32[4,32,1024]{2,1,0:T(8,128)}), f32[4,32,1024]{2,1,0:T(8,128)}, u32[]{:S(2)}, u32[]{:S(2)}) %all-to-all-start.4) | async-done | bytes 524320 | tf_op jit(solution)/shard_map/all_to_all | solution.py:162
  120.8 1.7 %shard_map.88 = bf16[16,4,1024]{2,1,0:T(4,128)(2,1)} custom-call(f32[4,32,1024]{2,1,0:T(8,128)} %all-to-all-done.4.pieces), custom_call_target="tpu_custom_call" | custom-call | flops 1 | bytes 1 | tf_op jit(solution)/shard_map/pallas_call | solution.py:22
  122.5 9.3 %collective-permute-start.6 = (bf16[128,1024]{1,0:T(8,128)(2,1)}, bf16[128,1024]{1,0:T(8,128)(2,1)S(1)}, u32[]{:S(2)}, u32[]{:S(2)}) collective-permute-start(bf16[128,1024]{1,0:T(8,128)(2,1)} %collective-permute-done.5), channel_id=1, source_target_pairs={{0,7},{32,289},{1,256},{33,290},{2,257},{34,291},{3,258},{35,292},... | collective-permute-start | bytes 786440 | tf_op jit(solution)/shard_map/ppermute | solution.py:108
  131.9 7.0 %all-to-all-start.5 = ((bf16[16,4,1024]{2,1,0:T(4,128)(2,1)}), bf16[16,4,1024]{2,1,0:T(4,128)(2,1)S(1)}, u32[]{:S(2)}, u32[]{:S(2)}) async-start(bf16[16,4,1024]{2,1,0:T(4,128)(2,1)} %shard_map.88), calls=%async_computation.5 | async-start | bytes 262144 | tf_op jit(solution)/shard_map/all_to_all | solution.py:166
  138.9 11.3 %collective-permute-done.6.far = bf16[128,1024]{1,0:T(8,128)(2,1)S(1)} collective-permute-done((bf16[128,1024]{1,0:T(8,128)(2,1)}, bf16[128,1024]{1,0:T(8,128)(2,1)S(1)}, u32[]{:S(2)}, u32[]{:S(2)}) %collective-permute-start.6) | collective-permute-done | bytes 262176 | tf_op jit(solution)/shard_map/ppermute | solution.py:108
  150.9 1.0 copy-done.3
  153.6 6.8 %all-to-all-done.5.pieces = bf16[16,4,1024]{2,1,0:T(4,128)(2,1)S(1)} async-done(((bf16[16,4,1024]{2,1,0:T(4,128)(2,1)}), bf16[16,4,1024]{2,1,0:T(4,128)(2,1)S(1)}, u32[]{:S(2)}, u32[]{:S(2)}) %all-to-all-start.5) | async-done | bytes 131104 | tf_op jit(solution)/shard_map/all_to_all | solution.py:166
  161.1 5.0 %all-to-all-start.6 = ((f32[8,4,1024]{2,1,0:T(4,128)}), f32[8,4,1024]{2,1,0:T(4,128)S(1)}, u32[]{:S(2)}, u32[]{:S(2)}) async-start(f32[8,4,1024]{2,1,0:T(4,128)} %shard_map.92), calls=%async_computation.6 | async-start | bytes 262144 | tf_op jit(solution)/shard_map/all_to_all | solution.py:171
  166.1 1.6 copy-done.1
  167.7 1.6 shard_map.91
  169.3 2.1 %all-to-all-done.6 = f32[8,4,1024]{2,1,0:T(4,128)S(1)} async-done(((f32[8,4,1024]{2,1,0:T(4,128)}), f32[8,4,1024]{2,1,0:T(4,128)S(1)}, u32[]{:S(2)}, u32[]{:S(2)}) %all-to-all-start.6) | async-done | bytes 131104 | tf_op jit(solution)/shard_map/all_to_all | solution.py:171
  (35 shorter events, 7.2 us)
Async XLA Ops:
  0.6 29.6 %copy-start = (bf16[1,16,128,128]{3,2,1,0:T(8,128)(2,1)S(1)}, bf16[1,16,128,128]{3,2,1,0:T(8,128)(2,1)}, u32[]{:S(2)}) copy-start(bf16[1,16,128,128]{3,2,1,0:T(8,128)(2,1)} %param.9) | copy-start | bytes 1572868
  0.6 7.2 %copy-start.8 = (bf16[128,1024]{1,0:T(8,128)(2,1)S(1)}, bf16[128,1024]{1,0:T(8,128)(2,1)}, u32[]{:S(2)}) copy-start(bf16[128,1024]{1,0:T(8,128)(2,1)} %param.6) | copy-start | bytes 786436
  0.7 19.0 %copy-start.9 = (s32[1,16]{1,0:T(1,128)S(1)}, s32[1,16]{1,0:T(1,128)}, u32[]{:S(2)}) copy-start(s32[1,16]{1,0:T(1,128)} %param.10) | copy-start | bytes 196
  2.8 28.7 %all-to-all-start = ((bf16[4,128,1024]{2,1,0:T(8,128)(2,1)}), bf16[4,128,1024]{2,1,0:T(8,128)(2,1)S(1)}, u32[]{:S(2)}, u32[]{:S(2)}) async-start(bf16[4,128,1024]{2,1,0:T(8,128)(2,1)} %broadcast_in_dim.4), calls=%async_computation | async-start | bytes 2097152 | tf_op jit(solution)/shard_map/all_to_all | solution.py:116
  7.8 14.4 %collective-permute-start.1 = (bf16[128,1024]{1,0:T(8,128)(2,1)S(1)}, bf16[128,1024]{1,0:T(8,128)(2,1)S(1)}, u32[]{:S(2)}, u32[]{:S(2)}) collective-permute-start(bf16[128,1024]{1,0:T(8,128)(2,1)S(1)} %copy-done.8), channel_id=1, source_target_pairs={{0,1},{32,295},{1,2},{33,32},{2,3},{34,33},{3,4},{35,34},{4,5},{36... | collective-permute-start | bytes 786440 | tf_op jit(solution)/shard_map/ppermute | solution.py:108
  22.2 27.3 %collective-permute-start.2 = (bf16[128,1024]{1,0:T(8,128)(2,1)S(1)}, bf16[128,1024]{1,0:T(8,128)(2,1)S(1)}, u32[]{:S(2)}, u32[]{:S(2)}) collective-permute-start(bf16[128,1024]{1,0:T(8,128)(2,1)S(1)} %collective-permute-done.1), channel_id=1, source_target_pairs={{0,7},{32,289},{1,256},{33,290},{2,257},{34,291},{3,258},{35,292},... | collective-permute-start | bytes 786440 | tf_op jit(solution)/shard_map/ppermute | solution.py:108
  31.5 18.0 %all-to-all-start.1 = ((bf16[8,128,128]{2,1,0:T(8,128)(2,1)}), bf16[8,128,128]{2,1,0:T(8,128)(2,1)S(1)}, u32[]{:S(2)}, u32[]{:S(2)}) async-start(bf16[8,128,128]{2,1,0:T(8,128)(2,1)} %bitcast.20), calls=%async_computation.1 | async-start | bytes 524288 | tf_op jit(solution)/shard_map/all_to_all | solution.py:148
  50.6 18.3 %all-to-all-start.2 = ((bf16[4,128,1024]{2,1,0:T(8,128)(2,1)}), bf16[4,128,1024]{2,1,0:T(8,128)(2,1)S(1)}, u32[]{:S(2)}, u32[]{:S(2)}) async-start(bf16[4,128,1024]{2,1,0:T(8,128)(2,1)} %broadcast_in_dim.5), calls=%async_computation.2 | async-start | bytes 2097152 | tf_op jit(solution)/shard_map/all_to_all | solution.py:116
  54.8 18.9 %collective-permute-start = (bf16[4,128,1024]{2,1,0:T(8,128)(2,1)S(1)}, bf16[4,128,1024]{2,1,0:T(8,128)(2,1)}, u32[]{:S(2)}, u32[]{:S(2)}) collective-permute-start(bf16[4,128,1024]{2,1,0:T(8,128)(2,1)S(1)} %all-to-all-done.same), channel_id=1, source_target_pairs={{0,32},{32,0},{1,33},{33,1},{2,34},{34,2},{3,35},{35,3},{4,36},{36... | collective-permute-start | bytes 3145736 | tf_op jit(solution)/shard_map/ppermute | solution.py:120
  69.0 6.7 %collective-permute-start.3 = (bf16[4,128,1024]{2,1,0:T(8,128)(2,1)S(1)}, bf16[4,128,1024]{2,1,0:T(8,128)(2,1)S(1)}, u32[]{:S(2)}, u32[]{:S(2)}) collective-permute-start(bf16[4,128,1024]{2,1,0:T(8,128)(2,1)S(1)} %all-to-all-done.2.same), channel_id=1, source_target_pairs={{0,32},{32,0},{1,33},{33,1},{2,34},{34,2},{3,35},{35,3},{4,36},{36... | collective-permute-start | bytes 3145736 | tf_op jit(solution)/shard_map/ppermute | solution.py:120
  71.5 4.2 %copy-start.2 = (bf16[16,8,16,128]{3,1,2,0:T(8,128)(2,1)}, bf16[16,8,16,128]{3,1,2,0:T(8,128)(2,1)S(1)}, u32[]{:S(2)}) copy-start(bf16[16,8,16,128]{3,1,2,0:T(8,128)(2,1)S(1)} %copy.18) | copy-start | bytes 1572868
  73.7 2.0 %copy-start.5 = (bf16[128,1024]{1,0:T(8,128)(2,1)S(1)}, bf16[128,1024]{1,0:T(8,128)(2,1)}, u32[]{:S(2)}) copy-start(bf16[128,1024]{1,0:T(8,128)(2,1)} %cotangent.1) | copy-start | bytes 786436
  100.1 5.9 %collective-permute-start.4 = (bf16[4,128,1280]{2,1,0:T(8,128)(2,1)S(1)}, bf16[4,128,1280]{2,1,0:T(8,128)(2,1)S(1)}, u32[]{:S(2)}, u32[]{:S(2)}) collective-permute-start(bf16[4,128,1280]{2,1,0:T(8,128)(2,1)S(1)} %all_to_all.35.same), channel_id=1, source_target_pairs={{0,32},{32,0},{1,33},{33,1},{2,34},{34,2},{3,35},{35,3},{4,36},{36... | collective-permute-start | bytes 3932168 | tf_op jit(solution)/shard_map/ppermute | solution.py:120
  106.8 0.8 copy-start.4
  107.6 13.2 %all-to-all-start.4 = ((f32[4,32,1024]{2,1,0:T(8,128)}), f32[4,32,1024]{2,1,0:T(8,128)}, u32[]{:S(2)}, u32[]{:S(2)}) async-start(f32[4,32,1024]{2,1,0:T(8,128)} %bitcast.29), calls=%async_computation.4 | async-start | bytes 1048576 | tf_op jit(solution)/shard_map/all_to_all | solution.py:162
  113.1 9.4 %collective-permute-start.5 = (bf16[128,1024]{1,0:T(8,128)(2,1)}, bf16[128,1024]{1,0:T(8,128)(2,1)}, u32[]{:S(2)}, u32[]{:S(2)}) collective-permute-start(bf16[128,1024]{1,0:T(8,128)(2,1)} %shard_map.89), channel_id=1, source_target_pairs={{0,1},{32,295},{1,2},{33,32},{2,3},{34,33},{3,4},{35,34},{4,5},{36... | collective-permute-start | bytes 786440 | tf_op jit(solution)/shard_map/ppermute | solution.py:108
  122.5 27.7 %collective-permute-start.6 = (bf16[128,1024]{1,0:T(8,128)(2,1)}, bf16[128,1024]{1,0:T(8,128)(2,1)S(1)}, u32[]{:S(2)}, u32[]{:S(2)}) collective-permute-start(bf16[128,1024]{1,0:T(8,128)(2,1)} %collective-permute-done.5), channel_id=1, source_target_pairs={{0,7},{32,289},{1,256},{33,290},{2,257},{34,291},{3,258},{35,292},... | collective-permute-start | bytes 786440 | tf_op jit(solution)/shard_map/ppermute | solution.py:108
  131.9 28.6 %all-to-all-start.5 = ((bf16[16,4,1024]{2,1,0:T(4,128)(2,1)}), bf16[16,4,1024]{2,1,0:T(4,128)(2,1)S(1)}, u32[]{:S(2)}, u32[]{:S(2)}) async-start(bf16[16,4,1024]{2,1,0:T(4,128)(2,1)} %shard_map.88), calls=%async_computation.5 | async-start | bytes 262144 | tf_op jit(solution)/shard_map/all_to_all | solution.py:166
  150.2 0.7 copy-start.6
  150.9 1.0 copy-start.3
  152.0 0.9 copy-start.7
  161.1 10.2 %all-to-all-start.6 = ((f32[8,4,1024]{2,1,0:T(4,128)}), f32[8,4,1024]{2,1,0:T(4,128)S(1)}, u32[]{:S(2)}, u32[]{:S(2)}) async-start(f32[8,4,1024]{2,1,0:T(4,128)} %shard_map.92), calls=%async_computation.6 | async-start | bytes 262144 | tf_op jit(solution)/shard_map/all_to_all | solution.py:171
  166.1 1.6 copy-start.1

commit v4 on v3

v4 whole, which is shorter than its diff:
```python
import jax
import jax.numpy as jnp
from jax import lax
from jax.experimental import pallas as pl
from jax.experimental.pallas import tpu as pltpu
from jax.sharding import Mesh, PartitionSpec as P

AXES = ("zh", "y", "co", "x", "zl")
SIZES = (2, 4, 2, 4, 8)
BF16, F32 = jnp.bfloat16, jnp.float32
SWAP = [(0, 1), (1, 0)]
VMEM = pl.BlockSpec(memory_space=pltpu.VMEM)
SMEM = pl.BlockSpec(memory_space=pltpu.SMEM)
COLS = slice(0, 1024)


def dot(a, b, over_a=1, over_b=0):
    return lax.dot_general(a, b, (((over_a,), (over_b,)), ((), ())), preferred_element_type=F32)


def call(body, outs, *args, flops=1):
    return pl.pallas_call(
        body,
        out_shape=outs,
        in_specs=[SMEM if a.dtype == jnp.int32 else VMEM for a in args],
        out_specs=jax.tree.map(lambda _: VMEM, outs),
        compiler_params=pltpu.CompilerParams(vmem_limit_bytes=16 * 2**20),
        cost_estimate=pl.CostEstimate(flops=flops, bytes_accessed=1, transcendentals=0),
    )(*args)


def block_dot(tile, same, other):
    total = 0.0
    for y in range(4):
        at = 128 * y
        total += dot(tile[:, at : at + 128], same[y, :, COLS])
        total += dot(tile[:, at + 512 : at + 640], other[y, :, COLS])
    return total


def near_body(tile, same, other, near):
    near[...] = block_dot(tile, same, other)


def forward_body(near, far, weight, cotangent, regroup, out, message):
    total = near[...] + far[...].astype(F32)
    high = total.astype(BF16)
    low = (total - high.astype(F32)).astype(BF16)
    summed = dot(high, weight[...]) + dot(low, weight[...])
    sigmoid = jax.nn.sigmoid(summed)
    out[...] = summed * sigmoid
    slope = cotangent[...].astype(F32) * sigmoid * (1.0 + summed * (1.0 - sigmoid))
    slope = slope.astype(BF16)
    factor = dot(high, regroup[...]).astype(BF16)
    for y in range(4):
        message[y, :, COLS] = slope
        message[y, :, 1024:1280] = factor[:, 256 * y : 256 * y + 256]


def prepare_body(place, codes, count, values, features, message, tile):
    tile[...] = jnp.zeros(tile.shape, BF16)
    for y in range(4):
        message[y, :, COLS] = features[...]
        message[y, :, 1024:1280] = jnp.zeros((128, 256), BF16)

    def slot(k, carry):
        grid_row = lax.div(lax.rem(codes[0, k], 512), 32)
        y, other = lax.div(lax.rem(grid_row, 8), 2), lax.rem(grid_row + place[1], 2)
        own = lax.div(grid_row, 8) == place[0]

        @pl.when(own)
        def _():
            tile[:, pl.ds(pl.multiple_of(512 * other + 128 * y, 128), 128)] = values[0, k]

        @pl.when(jnp.logical_not(own))
        def _():
            message[y, :, pl.ds(pl.multiple_of(1024 + 128 * other, 128), 128)] = values[0, k]

        return carry

    lax.fori_loop(0, count[0], slot, 0)


def grouped(same, other):
    total = 0.0
    for y in range(4):
        total += dot(same[y, :, 1024:1152], same[y, :, COLS], 0, 0)
        total += dot(other[y, :, 1152:1280], other[y, :, COLS], 0, 0)
    return total


def first_far_body(same, other, far, mirror):
    far[...] = grouped(same, other).astype(BF16)
    for y in range(4):
        mirror[y] = same[y, :, 1024:1152]
        mirror[y + 4] = other[y, :, 1152:1280]


def far_body(mirror, same, other, far):
    total = 0.0
    for y in range(4):
        total += dot(mirror[y], same[y, :, COLS], 0, 0)
        total += dot(mirror[y + 4], other[y, :, COLS], 0, 0)
    far[...] = total.astype(BF16)


def partial_body(same, other, partial):
    partial[...] = grouped(same, other)


def sum_x_body(pieces, out):
    total = pieces[0] + pieces[1] + pieces[2] + pieces[3]
    for z in range(8):
        rows = total[4 * z : 4 * z + 4].astype(BF16)
        out[z] = rows
        out[z + 8] = rows


def sum_z_body(pieces, out):
    total = pieces[0].astype(F32)
    for z in range(1, 16):
        total += pieces[z].astype(F32)
    for group in range(8):
        out[group] = total * (65536 ** -0.5)


def backward_body(tile, same, other, far, weight, input_grad):
    total = block_dot(tile, same, other) + far[...].astype(F32)
    input_grad[...] = dot(total.astype(BF16), weight[...], 1, 1)


def partner(rows):
    return lax.ppermute(rows, "zh", SWAP)


def after(value, *others):
    return lax.optimization_barrier((value,) + others)[0]


def over_y(message):
    return lax.all_to_all(message, "y", 0, 0)


def other_core(rows):
    return lax.ppermute(rows, "co", SWAP)


def local(features, weight, cotangent, block_values, block_codes, block_count):
    zh, core = lax.axis_index("zh"), lax.axis_index("co")
    hidden = features.shape[1]
    at = jnp.arange(hidden)
    group = 2 * (at // 256) + (at // 128 % 2 ^ core)
    source = 32 * (at // 4 % 32) + 4 * group + at % 4
    regroup = (jnp.arange(hidden)[:, None] == source[None, :]).astype(BF16)

    def shape(*dims, dtype=F32):
        return jax.ShapeDtypeStruct(dims, dtype)

    rows_f32, rows_bf16 = shape(128, hidden), shape(128, hidden, dtype=BF16)
    message_shape = shape(4, 128, hidden + 256, dtype=BF16)

    message, tile = call(
        prepare_body, (message_shape, shape(128, 1024, dtype=BF16)),
        jnp.stack([zh, core]), block_codes, block_count, block_values, features,
    )
    same = over_y(message)
    other = other_core(same)
    far, mirror = call(first_far_body, (rows_bf16, shape(8, 128, 128, dtype=BF16)), same, other)
    far = partner(far)
    near = call(near_body, rows_f32, tile, same, other)
    output, message = call(
        forward_body, (rows_f32, message_shape), near, far, weight, cotangent, regroup
    )

    same = over_y(message)
    other = other_core(same)
    partial = call(partial_body, rows_f32, same, other)
    part = lax.all_to_all(partial.reshape(4, 32, hidden), "x", 0, 0)
    far = partner(call(far_body, rows_bf16, mirror, same, other))
    part = call(sum_x_body, shape(16, 4, hidden, dtype=BF16), part)
    part = lax.all_to_all(part, ("zh", "zl"), 0, 0)
    input_grad = call(backward_body, rows_f32, tile, same, other, far, weight, flops=10**11)
    part = call(sum_z_body, shape(8, 4, hidden), after(part, input_grad))
    part = lax.all_to_all(part, ("y", "co"), 0, 0)
    weight_grad = part.reshape(32, hidden)
    return output, input_grad, weight_grad


def solution(mesh):
    fine = Mesh(mesh.devices.reshape(SIZES), AXES)
    rows = P(AXES)
    return jax.shard_map(
        local,
        mesh=fine,
        in_specs=(rows, P(), rows, rows, rows, rows),
        out_specs=(rows, rows, P(("x", "zl"))),
        check_vma=False,
    )
```

time: 174 us -> 154 us (0.89)
  waiting for transfers between devices: 56.1 us -> 23.3 us
  blocking collectives: 19.9 us -> 46.6 us
  Pallas kernels: 13.2 us -> 9 us
  local copies, waits for them, and re-layouts: 10.1 us -> 6.69 us
  starting transfers between devices: 68.1 us -> 65.7 us
    all_to_all x1 -> x3, blocking collectives: 19.9 us -> 46.6 us  [the longest x2 37.6 us: over_y(): return lax.all_to_all(message, 'y', 0, 0)]
    ppermute x4 -> x2, waiting for transfers between devices: 26.5 us -> 4.75 us  [partner(): return lax.ppermute(rows, 'zh', SWAP)]
    all_to_all x4 -> x0, starting transfers between devices: 19.6 us -> none  [the longest x2 9.18 us: over_y(): lax.all_to_all(jnp.broadcast_to(rows[None], (4,) + rows.shape), 'y', 0, 0)]
    all_to_all x1, starting transfers between devices: 7.01 us -> 23.3 us  [local(): part = lax.all_to_all(part, ('zh', 'zl'), 0, 0)]
    all_to_all x4 -> x0, waiting for transfers between devices: 14.4 us -> none  [the longest x2 12.3 us: over_y(): lax.all_to_all(jnp.broadcast_to(rows[None], (4,) + rows.shape), 'y', 0, 0)]
    all_to_all x1, waiting for transfers between devices: 6.84 us -> 13.3 us  [local(): part = lax.all_to_all(part, ('zh', 'zl'), 0, 0)]
    all_to_all x1, waiting for transfers between devices: 5.75 us -> 0.01 us  [local(): part = lax.all_to_all(partial.reshape(4, 32, hidden), 'x', 0, 0)]
    pallas_call x8 -> x9, Pallas kernels: 13.2 us -> 9 us  [call(): pl.pallas_call(body, out_shape=outs, in_specs=[SMEM if a.dtype == jnp.int...]
  transfers between devices with their start and end apart: 13 -> 6, of which waited for: 8 -> 4; matrix products, arithmetic and copies ran while one was open for 2% -> 1% of each run, Pallas kernels for 4% -> 3%
where the time goes in v4:
time: 154 us
  starting transfers between devices  65.7 us (43%)
  blocking collectives  46.6 us (30%)
  waiting for transfers between devices  23.3 us (15%)
  Pallas kernels  9 us (6%)
  local copies, waits for them, and re-layouts  6.69 us (4%)
    all_to_all x2, blocking collectives, over_y(): return lax.all_to_all(message, 'y', 0, 0)  37.6 us
    ppermute x2, starting transfers between devices, partner(): return lax.ppermute(rows, 'zh', SWAP)  27.3 us
    all_to_all x1, starting transfers between devices, local(): part = lax.all_to_all(part, ('zh', 'zl'), 0, 0)  23.3 us
    all_to_all x1, waiting for transfers between devices, local(): part = lax.all_to_all(part, ('zh', 'zl'), 0, 0)  13.3 us
    ppermute x2, starting transfers between devices, other_core(): return lax.ppermute(rows, 'co', SWAP)  11.2 us
    pallas_call x9, Pallas kernels, call(): pl.pallas_call(body, out_shape=outs, in_specs=[SMEM if a.dtype == jnp.int...  9 us
    all_to_all x1, blocking collectives, local(): part = lax.all_to_all(part, ('y', 'co'), 0, 0)  8.97 us
    unnamed x18, local copies, waits for them, and re-layouts  5.99 us
  transfers between devices with their start and end apart: 6, of which 4 were waited for; matrix products, arithmetic and copies ran while one was open for 1% of the time, Pallas kernels for 3%

profile of v4, /device:TPU:1, one launch (start us, length us, event | category | flops | bytes accessed | tf_op | source)
XLA Modules:
  0.0 153.7 jit_solution(9483477058872217484)
XLA Ops:
  1.3 0.1 pad_add_fusion.place
  1.4 1.0 copy-done.3
  2.4 0.9 copy-done.5
  3.4 0.7 copy-done.8
  4.0 0.9 shard_map.85
  4.9 18.4 %all_to_all.25.same = bf16[4,128,1280]{2,1,0:T(8,128)(2,1)S(1)} all-to-all(bf16[4,128,1280]{2,1,0:T(8,128)(2,1)S(1)} %get-tuple-element.11), channel_id=1, replica_groups=mesh['zh'=2,'y'=4,'co'=2,'x'=4,'zl'=8] {'y'}, dimensions={0} | all-to-all | bytes 2621440 | tf_op jit(solution)/shard_map/all_to_all | solution.py:141
  23.3 7.2 %collective-permute-start = (bf16[4,128,1280]{2,1,0:T(8,128)(2,1)S(1)}, bf16[4,128,1280]{2,1,0:T(8,128)(2,1)S(1)}, u32[]{:S(2)}, u32[]{:S(2)}) collective-permute-start(bf16[4,128,1280]{2,1,0:T(8,128)(2,1)S(1)} %all_to_all.25.same), channel_id=1, source_target_pairs={{0,32},{32,0},{1,33},{33,1},{2,34},{34,2},{3,35},{35,3},{4,36},{36... | collective-permute-start | bytes 3932168 | tf_op jit(solution)/shard_map/ppermute | solution.py:145
  30.6 2.6 %collective-permute-done.other = bf16[4,128,1280]{2,1,0:T(8,128)(2,1)S(1)} collective-permute-done((bf16[4,128,1280]{2,1,0:T(8,128)(2,1)S(1)}, bf16[4,128,1280]{2,1,0:T(8,128)(2,1)S(1)}, u32[]{:S(2)}, u32[]{:S(2)}) %collective-permute-start) | collective-permute-done | bytes 1310752 | tf_op jit(solution)/shard_map/ppermute | solution.py:145
  33.2 0.7 shard_map.87
  33.9 15.5 %collective-permute-start.1 = (bf16[128,1024]{1,0:T(8,128)(2,1)S(1)}, bf16[128,1024]{1,0:T(8,128)(2,1)S(1)}, u32[]{:S(2)}, u32[]{:S(2)}) collective-permute-start(bf16[128,1024]{1,0:T(8,128)(2,1)S(1)} %get-tuple-element.12), channel_id=1, source_target_pairs={{0,256},{256,0},{1,257},{257,1},{2,258},{258,2},{3,259},{259,3},{4... | collective-permute-start | bytes 786440 | tf_op jit(solution)/shard_map/ppermute | solution.py:133
  49.4 0.9 fusion.regroup
  50.3 0.0 copy-start.4
  50.3 0.7 shard_map.86.near
  51.0 4.7 %collective-permute-done.1.far = bf16[128,1024]{1,0:T(8,128)(2,1)S(1)} collective-permute-done((bf16[128,1024]{1,0:T(8,128)(2,1)S(1)}, bf16[128,1024]{1,0:T(8,128)(2,1)S(1)}, u32[]{:S(2)}, u32[]{:S(2)}) %collective-permute-start.1) | collective-permute-done | bytes 262176 | tf_op jit(solution)/shard_map/ppermute | solution.py:133
  55.8 1.7 %shard_map.88 = (f32[128,1024]{1,0:T(8,128)}, bf16[4,128,1280]{2,1,0:T(8,128)(2,1)S(1)}) custom-call(f32[128,1024]{1,0:T(8,128)S(1)} %shard_map.86.near, bf16[128,1024]{1,0:T(8,128)(2,1)S(1)} %collective-permute-done.1.far, bf16[1024,1024]{1,0:T(8,128)(2,1)S(1)} %copy-done, bf16[128,1024]{1,0:T(8,128)(2,1)S(1)} %copy-done.4, bf16[1024,1024]{1,0:T(8,128)(2,1)S(1)} %fusion.regroup), custom_call_target="tpu_custom_call" | custom-call | flops 1 | bytes 1 | tf_op jit(solution)/shard_map/pallas_call | solution.py:22
  57.5 19.2 %all_to_all.26.same = bf16[4,128,1280]{2,1,0:T(8,128)(2,1)S(1)} all-to-all(bf16[4,128,1280]{2,1,0:T(8,128)(2,1)S(1)} %get-tuple-element.14), channel_id=1, replica_groups=mesh['zh'=2,'y'=4,'co'=2,'x'=4,'zl'=8] {'y'}, dimensions={0} | all-to-all | bytes 2621440 | tf_op jit(solution)/shard_map/all_to_all | solution.py:141
  76.7 4.0 %collective-permute-start.2 = (bf16[4,128,1280]{2,1,0:T(8,128)(2,1)S(1)}, bf16[4,128,1280]{2,1,0:T(8,128)(2,1)S(1)}, u32[]{:S(2)}, u32[]{:S(2)}) collective-permute-start(bf16[4,128,1280]{2,1,0:T(8,128)(2,1)S(1)} %all_to_all.26.same), channel_id=1, source_target_pairs={{0,32},{32,0},{1,33},{33,1},{2,34},{34,2},{3,35},{35,3},{4,36},{36... | collective-permute-start | bytes 3932168 | tf_op jit(solution)/shard_map/ppermute | solution.py:145
  80.7 2.6 %collective-permute-done.2.other = bf16[4,128,1280]{2,1,0:T(8,128)(2,1)S(1)} collective-permute-done((bf16[4,128,1280]{2,1,0:T(8,128)(2,1)S(1)}, bf16[4,128,1280]{2,1,0:T(8,128)(2,1)S(1)}, u32[]{:S(2)}, u32[]{:S(2)}) %collective-permute-start.2) | collective-permute-done | bytes 1310752 | tf_op jit(solution)/shard_map/ppermute | solution.py:145
  83.3 0.7 shard_map.91
  84.0 0.0 copy-start.2
  84.0 0.8 copy-done.2
  84.8 3.9 %all-to-all-start.2 = ((f32[4,32,1024]{2,1,0:T(8,128)}), f32[4,32,1024]{2,1,0:T(8,128)S(1)}, u32[]{:S(2)}, u32[]{:S(2)}) async-start(f32[4,32,1024]{2,1,0:T(8,128)} %bitcast.3), calls=%async_computation.2 | async-start | bytes 1048576 | tf_op jit(solution)/shard_map/all_to_all | solution.py:178
  88.7 1.4 shard_map.89
  90.1 11.8 %collective-permute-start.3 = (bf16[128,1024]{1,0:T(8,128)(2,1)}, bf16[128,1024]{1,0:T(8,128)(2,1)S(1)}, u32[]{:S(2)}, u32[]{:S(2)}) collective-permute-start(bf16[128,1024]{1,0:T(8,128)(2,1)} %shard_map.89), channel_id=1, source_target_pairs={{0,256},{256,0},{1,257},{257,1},{2,258},{258,2},{3,259},{259,3},{4... | collective-permute-start | bytes 786440 | tf_op jit(solution)/shard_map/ppermute | solution.py:133
  101.9 0.7 shard_map.92
  102.6 23.3 %all-to-all-start.3 = ((bf16[16,4,1024]{2,1,0:T(4,128)(2,1)}), bf16[16,4,1024]{2,1,0:T(4,128)(2,1)S(1)}, u32[]{:S(2)}, u32[]{:S(2)}) async-start(bf16[16,4,1024]{2,1,0:T(4,128)(2,1)} %shard_map.92), calls=%async_computation.3 | async-start | bytes 262144 | tf_op jit(solution)/shard_map/all_to_all | solution.py:181
  125.9 1.6 %copy-done.1 = bf16[1024,1024]{1,0:T(8,128)(2,1)S(1)} copy-done((bf16[1024,1024]{1,0:T(8,128)(2,1)S(1)}, bf16[1024,1024]{1,0:T(8,128)(2,1)}, u32[]{:S(2)}) %copy-start.1) | copy-done | bytes 2097176
  127.5 0.9 copy-done.7
  128.5 2.2 %shard_map.90 = f32[128,1024]{1,0:T(8,128)} custom-call(bf16[128,1024]{1,0:T(8,128)(2,1)S(1)} %copy-done.7, bf16[4,128,1280]{2,1,0:T(8,128)(2,1)S(1)} %all_to_all.26.same, bf16[4,128,1280]{2,1,0:T(8,128)(2,1)S(1)} %collective-permute-done.2.other, bf16[128,1024]{1,0:T(8,128)(2,1)S(1)} %collective-permute-done.3.far, bf16[1024,1024]{1,0:T(8,128)(2,1)S(1)} %copy-done.1), custom_call_target="tpu_custom_call" | custom-call | flops 99999997952 | bytes 1 | tf_op jit(solution)/shard_map/pallas_call | solution.py:22
  130.6 13.3 %all-to-all-done.3.pieces = bf16[16,4,1024]{2,1,0:T(4,128)(2,1)S(1)} async-done(((bf16[16,4,1024]{2,1,0:T(4,128)(2,1)}), bf16[16,4,1024]{2,1,0:T(4,128)(2,1)S(1)}, u32[]{:S(2)}, u32[]{:S(2)}) %all-to-all-start.3) | async-done | bytes 131104 | tf_op jit(solution)/shard_map/all_to_all | solution.py:181
  144.0 9.0 %all_to_all.27 = f32[8,4,1024]{2,1,0:T(4,128)S(1)} all-to-all(f32[8,4,1024]{2,1,0:T(4,128)S(1)} %shard_map.93), channel_id=1, replica_groups=mesh['zh'=2,'y'=4,'co'=2,'x'=4,'zl'=8] {'y','co'}, dimensions={0} | all-to-all | bytes 262144 | tf_op jit(solution)/shard_map/all_to_all | solution.py:184
  153.0 0.7 reshape.78
  (14 shorter events, 0.1 us)
Async XLA Ops:
  1.4 1.0 copy-start.3
  2.4 0.9 copy-start.5
  3.3 0.7 copy-start.8
  4.9 45.4 %copy-start.6 = (bf16[128,1024]{1,0:T(8,128)(2,1)}, bf16[128,1024]{1,0:T(8,128)(2,1)S(1)}, u32[]{:S(2)}) copy-start(bf16[128,1024]{1,0:T(8,128)(2,1)S(1)} %get-tuple-element.10.tile) | copy-start | bytes 786436
  23.3 9.9 %collective-permute-start = (bf16[4,128,1280]{2,1,0:T(8,128)(2,1)S(1)}, bf16[4,128,1280]{2,1,0:T(8,128)(2,1)S(1)}, u32[]{:S(2)}, u32[]{:S(2)}) collective-permute-start(bf16[4,128,1280]{2,1,0:T(8,128)(2,1)S(1)} %all_to_all.25.same), channel_id=1, source_target_pairs={{0,32},{32,0},{1,33},{33,1},{2,34},{34,2},{3,35},{35,3},{4,36},{36... | collective-permute-start | bytes 3932168 | tf_op jit(solution)/shard_map/ppermute | solution.py:145
  33.9 21.9 %collective-permute-start.1 = (bf16[128,1024]{1,0:T(8,128)(2,1)S(1)}, bf16[128,1024]{1,0:T(8,128)(2,1)S(1)}, u32[]{:S(2)}, u32[]{:S(2)}) collective-permute-start(bf16[128,1024]{1,0:T(8,128)(2,1)S(1)} %get-tuple-element.12), channel_id=1, source_target_pairs={{0,256},{256,0},{1,257},{257,1},{2,258},{258,2},{3,259},{259,3},{4... | collective-permute-start | bytes 786440 | tf_op jit(solution)/shard_map/ppermute | solution.py:133
  50.3 5.5 %copy-start = (bf16[1024,1024]{1,0:T(8,128)(2,1)S(1)}, bf16[1024,1024]{1,0:T(8,128)(2,1)}, u32[]{:S(2)}) copy-start(bf16[1024,1024]{1,0:T(8,128)(2,1)} %weight.3) | copy-start | bytes 6291460
  50.3 5.5 %copy-start.4 = (bf16[128,1024]{1,0:T(8,128)(2,1)S(1)}, bf16[128,1024]{1,0:T(8,128)(2,1)}, u32[]{:S(2)}) copy-start(bf16[128,1024]{1,0:T(8,128)(2,1)} %cotangent.1) | copy-start | bytes 786436
  76.7 6.6 %collective-permute-start.2 = (bf16[4,128,1280]{2,1,0:T(8,128)(2,1)S(1)}, bf16[4,128,1280]{2,1,0:T(8,128)(2,1)S(1)}, u32[]{:S(2)}, u32[]{:S(2)}) collective-permute-start(bf16[4,128,1280]{2,1,0:T(8,128)(2,1)S(1)} %all_to_all.26.same), channel_id=1, source_target_pairs={{0,32},{32,0},{1,33},{33,1},{2,34},{34,2},{3,35},{35,3},{4,36},{36... | collective-permute-start | bytes 3932168 | tf_op jit(solution)/shard_map/ppermute | solution.py:145
  84.0 0.8 copy-start.2
  84.8 17.1 %all-to-all-start.2 = ((f32[4,32,1024]{2,1,0:T(8,128)}), f32[4,32,1024]{2,1,0:T(8,128)S(1)}, u32[]{:S(2)}, u32[]{:S(2)}) async-start(f32[4,32,1024]{2,1,0:T(8,128)} %bitcast.3), calls=%async_computation.2 | async-start | bytes 1048576 | tf_op jit(solution)/shard_map/all_to_all | solution.py:178
  90.1 35.8 %collective-permute-start.3 = (bf16[128,1024]{1,0:T(8,128)(2,1)}, bf16[128,1024]{1,0:T(8,128)(2,1)S(1)}, u32[]{:S(2)}, u32[]{:S(2)}) collective-permute-start(bf16[128,1024]{1,0:T(8,128)(2,1)} %shard_map.89), channel_id=1, source_target_pairs={{0,256},{256,0},{1,257},{257,1},{2,258},{258,2},{3,259},{259,3},{4... | collective-permute-start | bytes 786440 | tf_op jit(solution)/shard_map/ppermute | solution.py:133
  102.6 41.3 %all-to-all-start.3 = ((bf16[16,4,1024]{2,1,0:T(4,128)(2,1)}), bf16[16,4,1024]{2,1,0:T(4,128)(2,1)S(1)}, u32[]{:S(2)}, u32[]{:S(2)}) async-start(bf16[16,4,1024]{2,1,0:T(4,128)(2,1)} %shard_map.92), calls=%async_computation.3 | async-start | bytes 262144 | tf_op jit(solution)/shard_map/all_to_all | solution.py:181
  125.9 1.6 %copy-start.1 = (bf16[1024,1024]{1,0:T(8,128)(2,1)S(1)}, bf16[1024,1024]{1,0:T(8,128)(2,1)}, u32[]{:S(2)}) copy-start(bf16[1024,1024]{1,0:T(8,128)(2,1)} %weight.3) | copy-start | bytes 6291460
  127.5 0.9 copy-start.7

commit v5 on v4

v5 whole, which is shorter than its diff:
```python
import jax
import jax.numpy as jnp
from jax import lax
from jax.experimental import pallas as pl
from jax.experimental.pallas import tpu as pltpu
from jax.sharding import Mesh, PartitionSpec as P

AXES = ("zh", "y", "co", "x", "zl")
SIZES = (2, 4, 2, 4, 8)
BF16, F32 = jnp.bfloat16, jnp.float32
SWAP = [(0, 1), (1, 0)]
VMEM = pl.BlockSpec(memory_space=pltpu.VMEM)
SMEM = pl.BlockSpec(memory_space=pltpu.SMEM)
COLS, FIRST, LAST = slice(0, 1024), slice(0, 512), slice(512, 1024)


def dot(a, b, over_a=1, over_b=0):
    return lax.dot_general(a, b, (((over_a,), (over_b,)), ((), ())), preferred_element_type=F32)


def call(body, outs, *args, flops=1):
    return pl.pallas_call(
        body,
        out_shape=outs,
        in_specs=[SMEM if a.dtype == jnp.int32 else VMEM for a in args],
        out_specs=jax.tree.map(lambda _: VMEM, outs),
        compiler_params=pltpu.CompilerParams(vmem_limit_bytes=16 * 2**20),
        cost_estimate=pl.CostEstimate(flops=flops, bytes_accessed=1, transcendentals=0),
    )(*args)


def prepare_body(place, codes, count, values, features, message, first, tile):
    tile[...] = jnp.zeros(tile.shape, BF16)
    first[...] = features[:, FIRST]
    for y in range(4):
        message[y, :, COLS] = features[...]
        message[y, :, 1024:1280] = jnp.zeros((128, 256), BF16)

    def slot(k, carry):
        grid_row = lax.div(lax.rem(codes[0, k], 512), 32)
        y, other = lax.div(lax.rem(grid_row, 8), 2), lax.rem(grid_row + place[1], 2)
        own = lax.div(grid_row, 8) == place[0]
        at = 512 * other + 128 * y + jnp.where(own, 0, 1024)
        tile[:, pl.ds(pl.multiple_of(at, 128), 128)] = values[0, k]

        @pl.when(jnp.logical_not(own))
        def _():
            message[y, :, pl.ds(pl.multiple_of(1024 + 128 * other, 128), 128)] = values[0, k]

        return carry

    lax.fori_loop(0, count[0], slot, 0)


def near_body(tile, same, other, near):
    total = 0.0
    for y in range(4):
        at = 128 * y
        total += dot(tile[:, at : at + 128], same[y, :, COLS])
        total += dot(tile[:, at + 512 : at + 640], other[y, :, COLS])
    near[...] = total


def whole(near, tile, last, same, other):
    first = near[:, FIRST]
    for y in range(4):
        at = 1024 + 128 * y
        first += dot(tile[:, at : at + 128], same[y])
        first += dot(tile[:, at + 512 : at + 640], other[y])
    return jnp.concatenate([first, near[:, LAST] + last[...].astype(F32)], axis=1)


def far_body(mirror, same, other, far):
    total = 0.0
    for y in range(4):
        total += dot(mirror[y], same[y, :, LAST], 0, 0)
        total += dot(mirror[y + 4], other[y, :, LAST], 0, 0)
    far[...] = total.astype(BF16)


def first_far_body(same, other, far, mirror):
    for y in range(4):
        mirror[y] = same[y, :, 1024:1152]
        mirror[y + 4] = other[y, :, 1152:1280]
    far_body(mirror, same, other, far)


def forward_body(near, tile, last, same, other, weight, cotangent, regroup, out, message, first):
    total = whole(near, tile, last, same, other)
    high = total.astype(BF16)
    low = (total - high.astype(F32)).astype(BF16)
    summed = dot(high, weight[...]) + dot(low, weight[...])
    sigmoid = jax.nn.sigmoid(summed)
    out[...] = summed * sigmoid
    slope = cotangent[...].astype(F32) * sigmoid * (1.0 + summed * (1.0 - sigmoid))
    slope = slope.astype(BF16)
    first[...] = slope[:, FIRST]
    factor = dot(high, regroup[...]).astype(BF16)
    for y in range(4):
        message[y, :, COLS] = slope
        message[y, :, 1024:1280] = factor[:, 256 * y : 256 * y + 256]


def backward_body(near, tile, last, same, other, weight, input_grad):
    total = whole(near, tile, last, same, other)
    input_grad[...] = dot(total.astype(BF16), weight[...], 1, 1)


def partial_body(same, other, partial):
    total = 0.0
    for y in range(4):
        total += dot(same[y, :, 1024:1152], same[y, :, COLS], 0, 0)
        total += dot(other[y, :, 1152:1280], other[y, :, COLS], 0, 0)
    partial[...] = total


def sum_x_body(pieces, out):
    total = pieces[0] + pieces[1] + pieces[2] + pieces[3]
    for z in range(8):
        rows = total[4 * z : 4 * z + 4].astype(BF16)
        out[z] = rows
        out[z + 8] = rows


def sum_z_body(pieces, out):
    total = pieces[0].astype(F32)
    for z in range(1, 16):
        total += pieces[z].astype(F32)
    for group in range(8):
        out[group] = total * (65536 ** -0.5)


def partner(rows):
    return lax.ppermute(rows, "zh", SWAP)


def over_y(message):
    return lax.all_to_all(message, "y", 0, 0)


def spread(rows):
    return over_y(jnp.broadcast_to(rows[None], (4,) + rows.shape))


def other_core(rows):
    return lax.ppermute(rows, "co", SWAP)


def after(value, *others):
    return lax.optimization_barrier((value,) + others)[0]


def local(features, weight, cotangent, block_values, block_codes, block_count):
    zh, core = lax.axis_index("zh"), lax.axis_index("co")
    hidden = features.shape[1]
    at = jnp.arange(hidden)
    group = 2 * (at // 256) + (at // 128 % 2 ^ core)
    source = 32 * (at // 4 % 32) + 4 * group + at % 4
    regroup = (jnp.arange(hidden)[:, None] == source[None, :]).astype(BF16)

    def shape(*dims, dtype=F32):
        return jax.ShapeDtypeStruct(dims, dtype)

    rows = shape(128, hidden)
    half = shape(128, hidden // 2, dtype=BF16)
    message_shape = shape(4, 128, hidden + 256, dtype=BF16)

    message, first, tile = call(
        prepare_body, (message_shape, half, shape(128, 2048, dtype=BF16)),
        jnp.stack([zh, core]), block_codes, block_count, block_values, features,
    )
    far = partner(first)
    same = over_y(message)
    other = other_core(after(same, far))
    far_same = spread(far)
    last, mirror = call(first_far_body, (half, shape(8, 128, 128, dtype=BF16)), same, other)
    last = partner(last)
    near = call(near_body, rows, tile, same, other)
    far_other = other_core(after(far_same, last))
    output, message, first = call(
        forward_body, (rows, message_shape, half),
        near, tile, last, far_same, far_other, weight, cotangent, regroup,
    )

    far = partner(first)
    same = over_y(message)
    other = other_core(after(same, far))
    far_same = spread(far)
    partial = call(partial_body, rows, same, other)
    far_other = other_core(after(far_same, partial))
    part = lax.all_to_all(partial.reshape(4, 32, hidden), "x", 0, 0)
    last = partner(call(far_body, half, mirror, same, other))
    near = call(near_body, rows, tile, same, other)
    part = call(sum_x_body, shape(16, 4, hidden, dtype=BF16), part)
    part = lax.all_to_all(after(part, far_same), ("zh", "zl"), 0, 0)
    input_grad = call(
        backward_body, rows, near, tile, last, far_same, far_other, weight, flops=10**11
    )
    part = call(sum_z_body, shape(8, 4, hidden), after(part, input_grad))
    part = lax.all_to_all(part, ("y", "co"), 0, 0)
    weight_grad = part.reshape(32, hidden)
    return output, input_grad, weight_grad


def solution(mesh):
    fine = Mesh(mesh.devices.reshape(SIZES), AXES)
    rows = P(AXES)
    return jax.shard_map(
        local,
        mesh=fine,
        in_specs=(rows, P(), rows, rows, rows, rows),
        out_specs=(rows, rows, P(("x", "zl"))),
        check_vma=False,
    )
```

time: 154 us -> 175 us (1.14)
  starting transfers between devices: 65.7 us -> 109 us
  blocking collectives: 46.6 us -> 11.4 us
  Pallas kernels: 9 us -> 14.2 us
  waiting for transfers between devices: 23.3 us -> 26.7 us
  local copies, waits for them, and re-layouts: 6.69 us -> 10 us
    all_to_all x2 -> x0, blocking collectives: 37.6 us -> none  [over_y(): return lax.all_to_all(message, 'y', 0, 0)]
    ppermute x2 -> x4, starting transfers between devices: 27.3 us -> 54.4 us  [partner(): return lax.ppermute(rows, 'zh', SWAP)]
    all_to_all x1, starting transfers between devices: 3.87 us -> 13.2 us  [local(): part = lax.all_to_all(partial.reshape(4, 32, hidden), 'x', 0, 0)]
    ppermute x2 -> x4, waiting for transfers between devices: 4.75 us -> 10.2 us  [partner(): return lax.ppermute(rows, 'zh', SWAP)]
    pallas_call x9 -> x10, Pallas kernels: 9 us -> 14.2 us  [call(): pl.pallas_call(body, out_shape=outs, in_specs=[SMEM if a.dtype == jnp.int...]
    ppermute x2 -> x4, waiting for transfers between devices: 5.26 us -> 0.11 us  [other_core(): return lax.ppermute(rows, 'co', SWAP)]
    all_to_all x1 -> x5, starting transfers between devices: 23.3 us -> 28 us  [the longest x4 17.9 us: over_y(): return lax.all_to_all(message, 'y', 0, 0)]
    all_to_all x1 -> x5, waiting for transfers between devices: 13.3 us -> 16.3 us  [the longest x4 10.1 us: over_y(): return lax.all_to_all(message, 'y', 0, 0)]
  transfers between devices with their start and end apart: 6 -> 14, of which waited for: 4 -> 7; matrix products, arithmetic and copies ran while one was open for 1% -> 1% of each run, Pallas kernels for 3% -> 5%
where the time goes in v5:
time: 175 us; the launch traced here: 174 us
  starting transfers between devices  109 us (62%)
  waiting for transfers between devices  26.7 us (15%)
  Pallas kernels  14.2 us (8%)
  blocking collectives  11.4 us (7%)
  local copies, waits for them, and re-layouts  10 us (6%)
    ppermute x4, starting transfers between devices, partner(): return lax.ppermute(rows, 'zh', SWAP)  54.4 us
    all_to_all x4, starting transfers between devices, over_y(): return lax.all_to_all(message, 'y', 0, 0)  17.9 us
    pallas_call x10, Pallas kernels, call(): pl.pallas_call(body, out_shape=outs, in_specs=[SMEM if a.dtype == jnp.int...  14.2 us
    ppermute x4, starting transfers between devices, other_core(): return lax.ppermute(rows, 'co', SWAP)  13.2 us
    all_to_all x1, starting transfers between devices, local(): part = lax.all_to_all(partial.reshape(4, 32, hidden), 'x', 0, 0)  13.2 us
    all_to_all x1, blocking collectives, local(): part = lax.all_to_all(part, ('y', 'co'), 0, 0)  11.4 us
    ppermute x4, waiting for transfers between devices, partner(): return lax.ppermute(rows, 'zh', SWAP)  10.2 us
    all_to_all x4, waiting for transfers between devices, over_y(): return lax.all_to_all(message, 'y', 0, 0)  10.1 us
  transfers between devices with their start and end apart: 14, of which 7 were waited for; matrix products, arithmetic and copies ran while one was open for 1% of the time, Pallas kernels for 5%

profile of v5, /device:TPU:1, one launch (start us, length us, event | category | flops | bytes accessed | tf_op | source)
XLA Modules:
  0.0 173.5 jit_solution(3307985601483831084)
XLA Ops:
  1.4 1.0 copy-done.5
  2.4 0.9 copy-done.7
  4.0 2.0 %shard_map.85 = (bf16[4,128,1280]{2,1,0:T(8,128)(2,1)}, bf16[128,512]{1,0:T(8,128)(2,1)S(1)}, bf16[128,2048]{1,0:T(8,128)(2,1)S(1)}) custom-call(s32[2]{0:T(128)S(1)} %pad_add_fusion.place, s32[1,16]{1,0:T(1,128)S(1)} %copy-done.8, s32[1]{0:T(128)S(6)} %copy.9.count, bf16[1,16,128,128]{3,2,1,0:T(8,128)(2,1)S(1)} %copy-done.5, bf16[128,1024]{1,0:T(8,128)(2,1)S(1)} %copy-done.7), custom_call_target="tpu_custom_call" | custom-call | flops 1 | bytes 1 | tf_op jit(solution)/shard_map/pallas_call | solution.py:22
  6.0 5.1 %all-to-all-start = ((bf16[4,128,1280]{2,1,0:T(8,128)(2,1)}), bf16[4,128,1280]{2,1,0:T(8,128)(2,1)S(1)}, u32[]{:S(2)}, u32[]{:S(2)}) async-start(bf16[4,128,1280]{2,1,0:T(8,128)(2,1)} %get-tuple-element.18), calls=%async_computation | async-start | bytes 2621440 | tf_op jit(solution)/shard_map/all_to_all | solution.py:138
  11.1 15.3 %collective-permute-start = (bf16[128,512]{1,0:T(8,128)(2,1)S(1)}, bf16[128,512]{1,0:T(8,128)(2,1)S(1)}, u32[]{:S(2)}, u32[]{:S(2)}) collective-permute-start(bf16[128,512]{1,0:T(8,128)(2,1)S(1)} %get-tuple-element.19), channel_id=1, source_target_pairs={{0,256},{256,0},{1,257},{257,1},{2,258},{258,2},{3,259},{259,3},{4... | collective-permute-start | bytes 393224 | tf_op jit(solution)/shard_map/ppermute | solution.py:134
  26.4 2.6 %collective-permute-done = bf16[128,512]{1,0:T(8,128)(2,1)S(1)} collective-permute-done((bf16[128,512]{1,0:T(8,128)(2,1)S(1)}, bf16[128,512]{1,0:T(8,128)(2,1)S(1)}, u32[]{:S(2)}, u32[]{:S(2)}) %collective-permute-start) | collective-permute-done | bytes 131104 | tf_op jit(solution)/shard_map/ppermute | solution.py:134
  29.1 5.1 %collective-permute-start.1 = (bf16[4,128,1280]{2,1,0:T(8,128)(2,1)S(1)}, bf16[4,128,1280]{2,1,0:T(8,128)(2,1)S(1)}, u32[]{:S(2)}, u32[]{:S(2)}) collective-permute-start(bf16[4,128,1280]{2,1,0:T(8,128)(2,1)S(1)} %all-to-all-done.same), channel_id=1, source_target_pairs={{0,32},{32,0},{1,33},{33,1},{2,34},{34,2},{3,35},{35,3},{4,36},{36... | collective-permute-start | bytes 3932168 | tf_op jit(solution)/shard_map/ppermute | solution.py:146
  35.0 4.5 %all-to-all-start.1 = ((bf16[4,128,512]{2,1,0:T(8,128)(2,1)}), bf16[4,128,512]{2,1,0:T(8,128)(2,1)}, u32[]{:S(2)}, u32[]{:S(2)}) async-start(bf16[4,128,512]{2,1,0:T(8,128)(2,1)} %broadcast_in_dim.4), calls=%async_computation.1 | async-start | bytes 1048576 | tf_op jit(solution)/shard_map/all_to_all | solution.py:138
  39.4 1.1 shard_map.87
  40.6 12.7 %collective-permute-start.2 = (bf16[128,512]{1,0:T(8,128)(2,1)}, bf16[128,512]{1,0:T(8,128)(2,1)S(1)}, u32[]{:S(2)}, u32[]{:S(2)}) collective-permute-start(bf16[128,512]{1,0:T(8,128)(2,1)} %get-tuple-element.21), channel_id=1, source_target_pairs={{0,256},{256,0},{1,257},{257,1},{2,258},{258,2},{3,259},{259,3},{4... | collective-permute-start | bytes 393224 | tf_op jit(solution)/shard_map/ppermute | solution.py:134
  53.3 4.0 %collective-permute-done.2.last = bf16[128,512]{1,0:T(8,128)(2,1)S(1)} collective-permute-done((bf16[128,512]{1,0:T(8,128)(2,1)}, bf16[128,512]{1,0:T(8,128)(2,1)S(1)}, u32[]{:S(2)}, u32[]{:S(2)}) %collective-permute-start.2) | collective-permute-done | bytes 131104 | tf_op jit(solution)/shard_map/ppermute | solution.py:134
  57.4 2.5 %collective-permute-start.3 = (bf16[4,128,512]{2,1,0:T(8,128)(2,1)}, bf16[4,128,512]{2,1,0:T(8,128)(2,1)S(1)}, u32[]{:S(2)}, u32[]{:S(2)}) collective-permute-start(bf16[4,128,512]{2,1,0:T(8,128)(2,1)} %all-to-all-done.1.same), channel_id=1, source_target_pairs={{0,32},{32,0},{1,33},{33,1},{2,34},{34,2},{3,35},{35,3},{4,36},{36... | collective-permute-start | bytes 1572872 | tf_op jit(solution)/shard_map/ppermute | solution.py:146
  59.9 0.9 fusion.regroup
  62.4 3.6 %shard_map.88 = (f32[128,1024]{1,0:T(8,128)}, bf16[4,128,1280]{2,1,0:T(8,128)(2,1)}, bf16[128,512]{1,0:T(8,128)(2,1)S(1)}) custom-call(f32[128,1024]{1,0:T(8,128)S(1)} %shard_map.86.near, bf16[128,2048]{1,0:T(8,128)(2,1)S(1)} %get-tuple-element.17.tile, bf16[128,512]{1,0:T(8,128)(2,1)S(1)} %collective-permute-done.2.last, ...), custom_call_target="tpu_custom_call" | custom-call | flops 1 | bytes 1 | tf_op jit(solution)/shard_map/pallas_call | solution.py:22
  66.0 4.2 %all-to-all-start.2 = ((bf16[4,128,1280]{2,1,0:T(8,128)(2,1)}), bf16[4,128,1280]{2,1,0:T(8,128)(2,1)S(1)}, u32[]{:S(2)}, u32[]{:S(2)}) async-start(bf16[4,128,1280]{2,1,0:T(8,128)(2,1)} %get-tuple-element.24), calls=%async_computation.2 | async-start | bytes 2621440 | tf_op jit(solution)/shard_map/all_to_all | solution.py:138
  70.2 12.2 %collective-permute-start.4 = (bf16[128,512]{1,0:T(8,128)(2,1)S(1)}, bf16[128,512]{1,0:T(8,128)(2,1)S(1)}, u32[]{:S(2)}, u32[]{:S(2)}) collective-permute-start(bf16[128,512]{1,0:T(8,128)(2,1)S(1)} %get-tuple-element.25), channel_id=1, source_target_pairs={{0,256},{256,0},{1,257},{257,1},{2,258},{258,2},{3,259},{259,3},{4... | collective-permute-start | bytes 393224 | tf_op jit(solution)/shard_map/ppermute | solution.py:134
  82.4 3.5 %collective-permute-done.4 = bf16[128,512]{1,0:T(8,128)(2,1)S(1)} collective-permute-done((bf16[128,512]{1,0:T(8,128)(2,1)S(1)}, bf16[128,512]{1,0:T(8,128)(2,1)S(1)}, u32[]{:S(2)}, u32[]{:S(2)}) %collective-permute-start.4) | collective-permute-done | bytes 131104 | tf_op jit(solution)/shard_map/ppermute | solution.py:134
  85.9 2.0 %all-to-all-done.2.same = bf16[4,128,1280]{2,1,0:T(8,128)(2,1)S(1)} async-done(((bf16[4,128,1280]{2,1,0:T(8,128)(2,1)}), bf16[4,128,1280]{2,1,0:T(8,128)(2,1)S(1)}, u32[]{:S(2)}, u32[]{:S(2)}) %all-to-all-start.2) | async-done | bytes 1310752 | tf_op jit(solution)/shard_map/all_to_all | solution.py:138
  87.9 3.0 %collective-permute-start.5 = (bf16[4,128,1280]{2,1,0:T(8,128)(2,1)S(1)}, bf16[4,128,1280]{2,1,0:T(8,128)(2,1)S(1)}, u32[]{:S(2)}, u32[]{:S(2)}) collective-permute-start(bf16[4,128,1280]{2,1,0:T(8,128)(2,1)S(1)} %all-to-all-done.2.same), channel_id=1, source_target_pairs={{0,32},{32,0},{1,33},{33,1},{2,34},{34,2},{3,35},{35,3},{4,36},{36... | collective-permute-start | bytes 3932168 | tf_op jit(solution)/shard_map/ppermute | solution.py:146
  90.9 0.8 broadcast_in_dim.5
  91.8 4.1 %all-to-all-start.3 = ((bf16[4,128,512]{2,1,0:T(8,128)(2,1)}), bf16[4,128,512]{2,1,0:T(8,128)(2,1)}, u32[]{:S(2)}, u32[]{:S(2)}) async-start(bf16[4,128,512]{2,1,0:T(8,128)(2,1)} %broadcast_in_dim.5), calls=%async_computation.3 | async-start | bytes 1048576 | tf_op jit(solution)/shard_map/all_to_all | solution.py:138
  97.5 8.1 %all-to-all-done.3.same = bf16[4,128,512]{2,1,0:T(8,128)(2,1)} async-done(((bf16[4,128,512]{2,1,0:T(8,128)(2,1)}), bf16[4,128,512]{2,1,0:T(8,128)(2,1)}, u32[]{:S(2)}, u32[]{:S(2)}) %all-to-all-start.3) | async-done | bytes 524320 | tf_op jit(solution)/shard_map/all_to_all | solution.py:138
  105.6 2.7 %collective-permute-start.7 = (bf16[4,128,512]{2,1,0:T(8,128)(2,1)}, bf16[4,128,512]{2,1,0:T(8,128)(2,1)}, u32[]{:S(2)}, u32[]{:S(2)}) collective-permute-start(bf16[4,128,512]{2,1,0:T(8,128)(2,1)} %all-to-all-done.3.same), channel_id=1, source_target_pairs={{0,32},{32,0},{1,33},{33,1},{2,34},{34,2},{3,35},{35,3},{4,36},{36... | collective-permute-start | bytes 1572872 | tf_op jit(solution)/shard_map/ppermute | solution.py:146
  108.3 13.2 %all-to-all-start.4 = ((f32[4,32,1024]{2,1,0:T(8,128)}), f32[4,32,1024]{2,1,0:T(8,128)}, u32[]{:S(2)}, u32[]{:S(2)}) async-start(f32[4,32,1024]{2,1,0:T(8,128)} %bitcast.3), calls=%async_computation.4 | async-start | bytes 1048576 | tf_op jit(solution)/shard_map/all_to_all | solution.py:191
  122.0 14.1 %collective-permute-start.6 = (bf16[128,512]{1,0:T(8,128)(2,1)S(1)}, bf16[128,512]{1,0:T(8,128)(2,1)S(1)}, u32[]{:S(2)}, u32[]{:S(2)}) collective-permute-start(bf16[128,512]{1,0:T(8,128)(2,1)S(1)} %shard_map.90), channel_id=1, source_target_pairs={{0,256},{256,0},{1,257},{257,1},{2,258},{258,2},{3,259},{259,3},{4... | collective-permute-start | bytes 393224 | tf_op jit(solution)/shard_map/ppermute | solution.py:134
  137.6 1.7 shard_map.93
  139.3 10.1 %all-to-all-start.5 = ((bf16[16,4,1024]{2,1,0:T(4,128)(2,1)}), bf16[16,4,1024]{2,1,0:T(4,128)(2,1)S(1)}, u32[]{:S(2)}, u32[]{:S(2)}) async-start(bf16[16,4,1024]{2,1,0:T(4,128)(2,1)} %shard_map.93), calls=%async_computation.5 | async-start | bytes 262144 | tf_op jit(solution)/shard_map/all_to_all | solution.py:195
  149.5 1.6 copy-done.1
  151.1 1.0 copy-done.4
  152.1 3.1 %shard_map.92 = f32[128,1024]{1,0:T(8,128)} custom-call(f32[128,1024]{1,0:T(8,128)S(1)} %copy-done.4, bf16[128,2048]{1,0:T(8,128)(2,1)S(1)} %get-tuple-element.17.tile, bf16[128,512]{1,0:T(8,128)(2,1)S(1)} %collective-permute-done.6.last, bf16[4,128,512]{2,1,0:T(8,128)(2,1)} %all-to-all-done.3.same, bf16[4,128,512]{2,1,0:T(8,128)(2,1)} %collective-permute-done.7.other, ...), custom_call_target="tpu_custom_call" | custom-call | flops 99999997952 | bytes 1 | tf_op jit(solution)/shard_map/pallas_call | solution.py:22
  155.2 6.2 %all-to-all-done.5.pieces = bf16[16,4,1024]{2,1,0:T(4,128)(2,1)S(1)} async-done(((bf16[16,4,1024]{2,1,0:T(4,128)(2,1)}), bf16[16,4,1024]{2,1,0:T(4,128)(2,1)S(1)}, u32[]{:S(2)}, u32[]{:S(2)}) %all-to-all-start.5) | async-done | bytes 131104 | tf_op jit(solution)/shard_map/all_to_all | solution.py:195
  161.5 11.4 %all_to_all.35 = f32[8,4,1024]{2,1,0:T(4,128)S(1)} all-to-all(f32[8,4,1024]{2,1,0:T(4,128)S(1)} %shard_map.94), channel_id=1, replica_groups=mesh['zh'=2,'y'=4,'co'=2,'x'=4,'zl'=8] {'y','co'}, dimensions={0} | all-to-all | bytes 262144 | tf_op jit(solution)/shard_map/all_to_all | solution.py:200
  (31 shorter events, 7.4 us)
Async XLA Ops:
  1.4 1.0 copy-start.5
  2.4 0.9 copy-start.7
  3.3 0.7 copy-start.8
  6.0 23.1 %all-to-all-start = ((bf16[4,128,1280]{2,1,0:T(8,128)(2,1)}), bf16[4,128,1280]{2,1,0:T(8,128)(2,1)S(1)}, u32[]{:S(2)}, u32[]{:S(2)}) async-start(bf16[4,128,1280]{2,1,0:T(8,128)(2,1)} %get-tuple-element.18), calls=%async_computation | async-start | bytes 2621440 | tf_op jit(solution)/shard_map/all_to_all | solution.py:138
  11.1 18.0 %collective-permute-start = (bf16[128,512]{1,0:T(8,128)(2,1)S(1)}, bf16[128,512]{1,0:T(8,128)(2,1)S(1)}, u32[]{:S(2)}, u32[]{:S(2)}) collective-permute-start(bf16[128,512]{1,0:T(8,128)(2,1)S(1)} %get-tuple-element.19), channel_id=1, source_target_pairs={{0,256},{256,0},{1,257},{257,1},{2,258},{258,2},{3,259},{259,3},{4... | collective-permute-start | bytes 393224 | tf_op jit(solution)/shard_map/ppermute | solution.py:134
  29.1 10.4 %collective-permute-start.1 = (bf16[4,128,1280]{2,1,0:T(8,128)(2,1)S(1)}, bf16[4,128,1280]{2,1,0:T(8,128)(2,1)S(1)}, u32[]{:S(2)}, u32[]{:S(2)}) collective-permute-start(bf16[4,128,1280]{2,1,0:T(8,128)(2,1)S(1)} %all-to-all-done.same), channel_id=1, source_target_pairs={{0,32},{32,0},{1,33},{33,1},{2,34},{34,2},{3,35},{35,3},{4,36},{36... | collective-permute-start | bytes 3932168 | tf_op jit(solution)/shard_map/ppermute | solution.py:146
  35.0 18.3 %all-to-all-start.1 = ((bf16[4,128,512]{2,1,0:T(8,128)(2,1)}), bf16[4,128,512]{2,1,0:T(8,128)(2,1)}, u32[]{:S(2)}, u32[]{:S(2)}) async-start(bf16[4,128,512]{2,1,0:T(8,128)(2,1)} %broadcast_in_dim.4), calls=%async_computation.1 | async-start | bytes 1048576 | tf_op jit(solution)/shard_map/all_to_all | solution.py:138
  40.6 16.8 %collective-permute-start.2 = (bf16[128,512]{1,0:T(8,128)(2,1)}, bf16[128,512]{1,0:T(8,128)(2,1)S(1)}, u32[]{:S(2)}, u32[]{:S(2)}) collective-permute-start(bf16[128,512]{1,0:T(8,128)(2,1)} %get-tuple-element.21), channel_id=1, source_target_pairs={{0,256},{256,0},{1,257},{257,1},{2,258},{258,2},{3,259},{259,3},{4... | collective-permute-start | bytes 393224 | tf_op jit(solution)/shard_map/ppermute | solution.py:134
  57.4 4.2 %collective-permute-start.3 = (bf16[4,128,512]{2,1,0:T(8,128)(2,1)}, bf16[4,128,512]{2,1,0:T(8,128)(2,1)S(1)}, u32[]{:S(2)}, u32[]{:S(2)}) collective-permute-start(bf16[4,128,512]{2,1,0:T(8,128)(2,1)} %all-to-all-done.1.same), channel_id=1, source_target_pairs={{0,32},{32,0},{1,33},{33,1},{2,34},{34,2},{3,35},{35,3},{4,36},{36... | collective-permute-start | bytes 1572872 | tf_op jit(solution)/shard_map/ppermute | solution.py:146
  60.8 1.6 copy-start
  60.8 1.6 copy-start.6
  66.0 21.9 %all-to-all-start.2 = ((bf16[4,128,1280]{2,1,0:T(8,128)(2,1)}), bf16[4,128,1280]{2,1,0:T(8,128)(2,1)S(1)}, u32[]{:S(2)}, u32[]{:S(2)}) async-start(bf16[4,128,1280]{2,1,0:T(8,128)(2,1)} %get-tuple-element.24), calls=%async_computation.2 | async-start | bytes 2621440 | tf_op jit(solution)/shard_map/all_to_all | solution.py:138
  70.2 15.7 %collective-permute-start.4 = (bf16[128,512]{1,0:T(8,128)(2,1)S(1)}, bf16[128,512]{1,0:T(8,128)(2,1)S(1)}, u32[]{:S(2)}, u32[]{:S(2)}) collective-permute-start(bf16[128,512]{1,0:T(8,128)(2,1)S(1)} %get-tuple-element.25), channel_id=1, source_target_pairs={{0,256},{256,0},{1,257},{257,1},{2,258},{258,2},{3,259},{259,3},{4... | collective-permute-start | bytes 393224 | tf_op jit(solution)/shard_map/ppermute | solution.py:134
  87.9 8.0 %collective-permute-start.5 = (bf16[4,128,1280]{2,1,0:T(8,128)(2,1)S(1)}, bf16[4,128,1280]{2,1,0:T(8,128)(2,1)S(1)}, u32[]{:S(2)}, u32[]{:S(2)}) collective-permute-start(bf16[4,128,1280]{2,1,0:T(8,128)(2,1)S(1)} %all-to-all-done.2.same), channel_id=1, source_target_pairs={{0,32},{32,0},{1,33},{33,1},{2,34},{34,2},{3,35},{35,3},{4,36},{36... | collective-permute-start | bytes 3932168 | tf_op jit(solution)/shard_map/ppermute | solution.py:146
  91.8 13.8 %all-to-all-start.3 = ((bf16[4,128,512]{2,1,0:T(8,128)(2,1)}), bf16[4,128,512]{2,1,0:T(8,128)(2,1)}, u32[]{:S(2)}, u32[]{:S(2)}) async-start(bf16[4,128,512]{2,1,0:T(8,128)(2,1)} %broadcast_in_dim.5), calls=%async_computation.3 | async-start | bytes 1048576 | tf_op jit(solution)/shard_map/all_to_all | solution.py:138
  96.7 0.8 copy-start.2
  105.6 43.8 %collective-permute-start.7 = (bf16[4,128,512]{2,1,0:T(8,128)(2,1)}, bf16[4,128,512]{2,1,0:T(8,128)(2,1)}, u32[]{:S(2)}, u32[]{:S(2)}) collective-permute-start(bf16[4,128,512]{2,1,0:T(8,128)(2,1)} %all-to-all-done.3.same), channel_id=1, source_target_pairs={{0,32},{32,0},{1,33},{33,1},{2,34},{34,2},{3,35},{35,3},{4,36},{36... | collective-permute-start | bytes 1572872 | tf_op jit(solution)/shard_map/ppermute | solution.py:146
  108.3 29.3 %all-to-all-start.4 = ((f32[4,32,1024]{2,1,0:T(8,128)}), f32[4,32,1024]{2,1,0:T(8,128)}, u32[]{:S(2)}, u32[]{:S(2)}) async-start(f32[4,32,1024]{2,1,0:T(8,128)} %bitcast.3), calls=%async_computation.4 | async-start | bytes 1048576 | tf_op jit(solution)/shard_map/all_to_all | solution.py:191
  122.0 27.5 %collective-permute-start.6 = (bf16[128,512]{1,0:T(8,128)(2,1)S(1)}, bf16[128,512]{1,0:T(8,128)(2,1)S(1)}, u32[]{:S(2)}, u32[]{:S(2)}) collective-permute-start(bf16[128,512]{1,0:T(8,128)(2,1)S(1)} %shard_map.90), channel_id=1, source_target_pairs={{0,256},{256,0},{1,257},{257,1},{2,258},{258,2},{3,259},{259,3},{4... | collective-permute-start | bytes 393224 | tf_op jit(solution)/shard_map/ppermute | solution.py:134
  136.8 0.8 copy-start.3
  139.3 22.1 %all-to-all-start.5 = ((bf16[16,4,1024]{2,1,0:T(4,128)(2,1)}), bf16[16,4,1024]{2,1,0:T(4,128)(2,1)S(1)}, u32[]{:S(2)}, u32[]{:S(2)}) async-start(bf16[16,4,1024]{2,1,0:T(4,128)(2,1)} %shard_map.93), calls=%async_computation.5 | async-start | bytes 262144 | tf_op jit(solution)/shard_map/all_to_all | solution.py:195
  149.5 1.6 copy-start.1
  151.1 1.0 copy-start.4

commit v6 on v4

--- a/solution.py
+++ b/solution.py
@@ -29,32 +29,42 @@
     )(*args)
 
 
-def block_dot(tile, same, other):
+def second_body(tile, begun, same, other, near):
+    near_body(tile, same, other, near)
+    near[...] += begun[...]
+
+
+def near_body(tile, same, other, near):
     total = 0.0
     for y in range(4):
         at = 128 * y
         total += dot(tile[:, at : at + 128], same[y, :, COLS])
         total += dot(tile[:, at + 512 : at + 640], other[y, :, COLS])
-    return total
-
-
-def near_body(tile, same, other, near):
-    near[...] = block_dot(tile, same, other)
-
-
-def forward_body(near, far, weight, cotangent, regroup, out, message):
+    near[...] = total
+
+
+def forward_body(near, far, weight, cotangent, regroup, summed_out, message, own):
     total = near[...] + far[...].astype(F32)
     high = total.astype(BF16)
     low = (total - high.astype(F32)).astype(BF16)
     summed = dot(high, weight[...]) + dot(low, weight[...])
     sigmoid = jax.nn.sigmoid(summed)
-    out[...] = summed * sigmoid
+    summed_out[...] = summed
     slope = cotangent[...].astype(F32) * sigmoid * (1.0 + summed * (1.0 - sigmoid))
     slope = slope.astype(BF16)
+    own[...] = slope
     factor = dot(high, regroup[...]).astype(BF16)
     for y in range(4):
         message[y, :, COLS] = slope
         message[y, :, 1024:1280] = factor[:, 256 * y : 256 * y + 256]
+
+
+def output_body(summed, out):
+    out[...] = summed[...] * jax.nn.sigmoid(summed[...])
+
+
+def start_body(tile, far, begun):
+    begun[...] = dot(tile[:, 1024:1152], far[...])
 
 
 def prepare_body(place, codes, count, values, features, message, tile):
@@ -68,9 +78,8 @@
         y, other = lax.div(lax.rem(grid_row, 8), 2), lax.rem(grid_row + place[1], 2)
         own = lax.div(grid_row, 8) == place[0]
 
-        @pl.when(own)
-        def _():
-            tile[:, pl.ds(pl.multiple_of(512 * other + 128 * y, 128), 128)] = values[0, k]
+        at = 512 * other + jnp.where(own, 128 * y, 1024 + 128 * lax.rem(place[2] - y + 4, 4))
+        tile[:, pl.ds(pl.multiple_of(at, 128), 128)] = values[0, k]
 
         @pl.when(jnp.logical_not(own))
         def _():
@@ -81,35 +90,29 @@
     lax.fori_loop(0, count[0], slot, 0)
 
 
-def grouped(same, other):
+def far_body(same, other, far):
     total = 0.0
     for y in range(4):
         total += dot(same[y, :, 1024:1152], same[y, :, COLS], 0, 0)
         total += dot(other[y, :, 1152:1280], other[y, :, COLS], 0, 0)
-    return total
-
-
-def first_far_body(same, other, far, mirror):
-    far[...] = grouped(same, other).astype(BF16)
-    for y in range(4):
-        mirror[y] = same[y, :, 1024:1152]
-        mirror[y + 4] = other[y, :, 1152:1280]
-
-
-def far_body(mirror, same, other, far):
+    far[...] = total.astype(BF16)
+
+
+def partial_body(same, partial):
     total = 0.0
     for y in range(4):
-        total += dot(mirror[y], same[y, :, COLS], 0, 0)
-        total += dot(mirror[y + 4], other[y, :, COLS], 0, 0)
-    far[...] = total.astype(BF16)
-
-
-def partial_body(same, other, partial):
-    partial[...] = grouped(same, other)
-
-
-def sum_x_body(pieces, out):
+        total += dot(same[y, :, 1024:1280], same[y, :, COLS], 0, 0)
+    partial[...] = total
+
+
+def sum_x_body(pieces, keep, send):
     total = pieces[0] + pieces[1] + pieces[2] + pieces[3]
+    keep[...] = total[0:32]
+    send[...] = total[32:64]
+
+
+def sum_core_body(keep, received, out):
+    total = keep[...] + received[...]
     for z in range(8):
         rows = total[4 * z : 4 * z + 4].astype(BF16)
         out[z] = rows
@@ -124,8 +127,11 @@
         out[group] = total * (65536 ** -0.5)
 
 
-def backward_body(tile, same, other, far, weight, input_grad):
-    total = block_dot(tile, same, other) + far[...].astype(F32)
+def backward_body(tile, near, weight, *refs):
+    *rows, input_grad = refs
+    total = near[...]
+    for i, piece in enumerate(rows):
+        total += dot(tile[:, 1152 + 128 * i : 1280 + 128 * i], piece[...])
     input_grad[...] = dot(total.astype(BF16), weight[...], 1, 1)
 
 
@@ -149,8 +155,8 @@
     zh, core = lax.axis_index("zh"), lax.axis_index("co")
     hidden = features.shape[1]
     at = jnp.arange(hidden)
-    group = 2 * (at // 256) + (at // 128 % 2 ^ core)
-    source = 32 * (at // 4 % 32) + 4 * group + at % 4
+    row = 8 * (at // 256) + 4 * (at // 32 % 2 ^ core) + at % 4
+    source = 32 * (8 * (at // 64 % 4) + at // 4 % 8) + row
     regroup = (jnp.arange(hidden)[:, None] == source[None, :]).astype(BF16)
 
     def shape(*dims, dtype=F32):
@@ -160,26 +166,34 @@
     message_shape = shape(4, 128, hidden + 256, dtype=BF16)
 
     message, tile = call(
-        prepare_body, (message_shape, shape(128, 1024, dtype=BF16)),
-        jnp.stack([zh, core]), block_codes, block_count, block_values, features,
+        prepare_body, (message_shape, shape(128, 2048, dtype=BF16)),
+        jnp.stack([zh, core, lax.axis_index("y")]), block_codes, block_count, block_values, features,
     )
     same = over_y(message)
     other = other_core(same)
-    far, mirror = call(first_far_body, (rows_bf16, shape(8, 128, 128, dtype=BF16)), same, other)
-    far = partner(far)
+    far = partner(call(far_body, rows_bf16, same, other))
     near = call(near_body, rows_f32, tile, same, other)
-    output, message = call(
-        forward_body, (rows_f32, message_shape), near, far, weight, cotangent, regroup
-    )
-
+    summed, message, slope = call(
+        forward_body, (rows_f32, message_shape, rows_bf16),
+        near, far, weight, cotangent, regroup,
+    )
+
+    far = partner(slope)
     same = over_y(message)
-    other = other_core(same)
-    partial = call(partial_body, rows_f32, same, other)
-    part = lax.all_to_all(partial.reshape(4, 32, hidden), "x", 0, 0)
-    far = partner(call(far_body, rows_bf16, mirror, same, other))
-    part = call(sum_x_body, shape(16, 4, hidden, dtype=BF16), part)
+    output = call(output_body, rows_f32, summed, flops=10**11)
+    partial = call(partial_body, shape(256, hidden), after(same, output))
+    part = lax.all_to_all(partial.reshape(4, 64, hidden), "x", 0, 0)
+    begun = call(start_body, rows_f32, tile, far, flops=10**11)
+    keep, send = call(
+        sum_x_body, (shape(32, hidden), shape(32, hidden)), after(part, begun)
+    )
+    others = [lax.ppermute(far, "y", [(i, (i + k) % 4) for i in range(4)]) for k in (1, 2, 3)]
+    other = other_core(after(same, keep))
+    near = call(second_body, rows_f32, tile, begun, same, other)
+    part = call(sum_core_body, shape(16, 4, hidden, dtype=BF16), keep, other_core(send))
     part = lax.all_to_all(part, ("zh", "zl"), 0, 0)
-    input_grad = call(backward_body, rows_f32, tile, same, other, far, weight, flops=10**11)
+    swapped = [other_core(v) for v in (far, *others)]
+    input_grad = call(backward_body, rows_f32, tile, near, weight, *others, *swapped)
     part = call(sum_z_body, shape(8, 4, hidden), after(part, input_grad))
     part = lax.all_to_all(part, ("y", "co"), 0, 0)
     weight_grad = part.reshape(32, hidden)

time: 154 us -> 166 us (1.078)
  starting transfers between devices: 65.7 us -> 94.2 us
  blocking collectives: 46.6 us -> 28.4 us
  Pallas kernels: 9 us -> 10.8 us
    all_to_all x2 -> x1, blocking collectives: 37.6 us -> 18.5 us  [over_y(): return lax.all_to_all(message, 'y', 0, 0)]
    all_to_all x1 -> x2, waiting for transfers between devices: 0.01 us -> 14.3 us  [the longest x1 10.3 us: local(): part = lax.all_to_all(partial.reshape(4, 64, hidden), 'x', 0, 0)]
    all_to_all x1, waiting for transfers between devices: 13.3 us -> 0.01 us  [local(): part = lax.all_to_all(part, ('zh', 'zl'), 0, 0)]
    ppermute x2 -> x7, starting transfers between devices: 11.2 us -> 24.3 us  [other_core(): return lax.ppermute(rows, 'co', SWAP)]
    ppermute x0 -> x3, starting transfers between devices: none -> 7.81 us  [local(): lax.ppermute(far, 'y', [(i, (i + k) % 4) for i in range(4)])]
    all_to_all x1, starting transfers between devices: 23.3 us -> 27.4 us  [local(): part = lax.all_to_all(part, ('zh', 'zl'), 0, 0)]
    all_to_all x1 -> x2, starting transfers between devices: 3.87 us -> 7.51 us  [the longest x1 3.98 us: local(): part = lax.all_to_all(partial.reshape(4, 64, hidden), 'x', 0, 0)]
    ppermute x2 -> x7, waiting for transfers between devices: 5.26 us -> 2.64 us  [other_core(): return lax.ppermute(rows, 'co', SWAP)]
  transfers between devices with their start and end apart: 6 -> 15, of which waited for: 4 -> 5; matrix products, arithmetic and copies ran while one was open for 1% -> 1% of each run, Pallas kernels for 3% -> 4%
where the time goes in v6:
time: 166 us; the launch traced here: 165 us
  starting transfers between devices  94.2 us (57%)
  blocking collectives  28.4 us (17%)
  waiting for transfers between devices  22.3 us (13%)
  Pallas kernels  10.8 us (7%)
  local copies, waits for them, and re-layouts  6.68 us (4%)
    all_to_all x1, starting transfers between devices, local(): part = lax.all_to_all(part, ('zh', 'zl'), 0, 0)  27.4 us
    ppermute x2, starting transfers between devices, partner(): return lax.ppermute(rows, 'zh', SWAP)  27.2 us
    ppermute x7, starting transfers between devices, other_core(): return lax.ppermute(rows, 'co', SWAP)  24.3 us
    all_to_all x1, blocking collectives, over_y(): return lax.all_to_all(message, 'y', 0, 0)  18.5 us
    pallas_call x12, Pallas kernels, call(): pl.pallas_call(body, out_shape=outs, in_specs=[SMEM if a.dtype == jnp.int...  10.8 us
    all_to_all x1, waiting for transfers between devices, local(): part = lax.all_to_all(partial.reshape(4, 64, hidden), 'x', 0, 0)  10.3 us
    all_to_all x1, blocking collectives, local(): part = lax.all_to_all(part, ('y', 'co'), 0, 0)  9.91 us
    ppermute x3, starting transfers between devices, local(): lax.ppermute(far, 'y', [(i, (i + k) % 4) for i in range(4)])  7.81 us
  transfers between devices with their start and end apart: 15, of which 5 were waited for; matrix products, arithmetic and copies ran while one was open for 1% of the time, Pallas kernels for 4%

profile of v6, /device:TPU:1, one launch (start us, length us, event | category | flops | bytes accessed | tf_op | source)
XLA Modules:
  0.0 165.0 jit_solution(3635891623143767591)
XLA Ops:
  1.4 1.0 copy-done.3
  2.4 0.9 copy-done.7
  4.0 0.8 shard_map.85
  4.8 18.5 %all_to_all.25.same = bf16[4,128,1280]{2,1,0:T(8,128)(2,1)S(1)} all-to-all(bf16[4,128,1280]{2,1,0:T(8,128)(2,1)S(1)} %get-tuple-element.15), channel_id=1, replica_groups=mesh['zh'=2,'y'=4,'co'=2,'x'=4,'zl'=8] {'y'}, dimensions={0} | all-to-all | bytes 2621440 | tf_op jit(solution)/shard_map/all_to_all | solution.py:147
  23.4 7.2 %collective-permute-start = (bf16[4,128,1280]{2,1,0:T(8,128)(2,1)S(1)}, bf16[4,128,1280]{2,1,0:T(8,128)(2,1)S(1)}, u32[]{:S(2)}, u32[]{:S(2)}) collective-permute-start(bf16[4,128,1280]{2,1,0:T(8,128)(2,1)S(1)} %all_to_all.25.same), channel_id=1, source_target_pairs={{0,32},{32,0},{1,33},{33,1},{2,34},{34,2},{3,35},{35,3},{4,36},{36... | collective-permute-start | bytes 3932168 | tf_op jit(solution)/shard_map/ppermute | solution.py:151
  30.6 2.6 %collective-permute-done.other = bf16[4,128,1280]{2,1,0:T(8,128)(2,1)S(1)} collective-permute-done((bf16[4,128,1280]{2,1,0:T(8,128)(2,1)S(1)}, bf16[4,128,1280]{2,1,0:T(8,128)(2,1)S(1)}, u32[]{:S(2)}, u32[]{:S(2)}) %collective-permute-start) | collective-permute-done | bytes 1310752 | tf_op jit(solution)/shard_map/ppermute | solution.py:151
  33.2 0.7 shard_map.87
  34.0 15.4 %collective-permute-start.1 = (bf16[128,1024]{1,0:T(8,128)(2,1)S(1)}, bf16[128,1024]{1,0:T(8,128)(2,1)S(1)}, u32[]{:S(2)}, u32[]{:S(2)}) collective-permute-start(bf16[128,1024]{1,0:T(8,128)(2,1)S(1)} %shard_map.87), channel_id=1, source_target_pairs={{0,256},{256,0},{1,257},{257,1},{2,258},{258,2},{3,259},{259,3},{4... | collective-permute-start | bytes 786440 | tf_op jit(solution)/shard_map/ppermute | solution.py:139
  49.3 0.9 fusion.regroup
  51.0 4.8 %collective-permute-done.1.far = bf16[128,1024]{1,0:T(8,128)(2,1)S(1)} collective-permute-done((bf16[128,1024]{1,0:T(8,128)(2,1)S(1)}, bf16[128,1024]{1,0:T(8,128)(2,1)S(1)}, u32[]{:S(2)}, u32[]{:S(2)}) %collective-permute-start.1) | collective-permute-done | bytes 262176 | tf_op jit(solution)/shard_map/ppermute | solution.py:139
  55.7 2.2 %shard_map.88 = (f32[128,1024]{1,0:T(8,128)S(1)}, bf16[4,128,1280]{2,1,0:T(8,128)(2,1)}, bf16[128,1024]{1,0:T(8,128)(2,1)S(1)}) custom-call(f32[128,1024]{1,0:T(8,128)S(1)} %shard_map.86.near, bf16[128,1024]{1,0:T(8,128)(2,1)S(1)} %collective-permute-done.1.far, bf16[1024,1024]{1,0:T(8,128)(2,1)S(1)} %copy-done, bf16[128,1024]{1,0:T(8,128)(2,1)S(1)} %copy-done.6, ...), custom_call_target="tpu_custom_call" | custom-call | flops 1 | bytes 1 | tf_op jit(solution)/shard_map/pallas_call | solution.py:22
  57.9 3.5 %all-to-all-start.1 = ((bf16[4,128,1280]{2,1,0:T(8,128)(2,1)}), bf16[4,128,1280]{2,1,0:T(8,128)(2,1)S(1)}, u32[]{:S(2)}, u32[]{:S(2)}) async-start(bf16[4,128,1280]{2,1,0:T(8,128)(2,1)} %get-tuple-element.18), calls=%async_computation.1 | async-start | bytes 2621440 | tf_op jit(solution)/shard_map/all_to_all | solution.py:147
  61.5 11.8 %collective-permute-start.2 = (bf16[128,1024]{1,0:T(8,128)(2,1)S(1)}, bf16[128,1024]{1,0:T(8,128)(2,1)S(1)}, u32[]{:S(2)}, u32[]{:S(2)}) collective-permute-start(bf16[128,1024]{1,0:T(8,128)(2,1)S(1)} %get-tuple-element.17), channel_id=1, source_target_pairs={{0,256},{256,0},{1,257},{257,1},{2,258},{258,2},{3,259},{259,3},{4... | collective-permute-start | bytes 786440 | tf_op jit(solution)/shard_map/ppermute | solution.py:139
  73.3 0.9 shard_map.89
  74.2 4.0 %all-to-all-done.1.same = bf16[4,128,1280]{2,1,0:T(8,128)(2,1)S(1)} async-done(((bf16[4,128,1280]{2,1,0:T(8,128)(2,1)}), bf16[4,128,1280]{2,1,0:T(8,128)(2,1)S(1)}, u32[]{:S(2)}, u32[]{:S(2)}) %all-to-all-start.1) | async-done | bytes 1310752 | tf_op jit(solution)/shard_map/all_to_all | solution.py:147
  78.9 1.0 copy-done.2
  79.9 4.0 %all-to-all-start.2 = ((f32[4,64,1024]{2,1,0:T(8,128)}), f32[4,64,1024]{2,1,0:T(8,128)S(1)}, u32[]{:S(2)}, u32[]{:S(2)}) async-start(f32[4,64,1024]{2,1,0:T(8,128)} %bitcast.4), calls=%async_computation.2 | async-start | bytes 2097152 | tf_op jit(solution)/shard_map/all_to_all | solution.py:185
  85.2 0.8 copy-done.4
  86.0 10.3 %all-to-all-done.2.pieces = f32[4,64,1024]{2,1,0:T(8,128)S(1)} async-done(((f32[4,64,1024]{2,1,0:T(8,128)}), f32[4,64,1024]{2,1,0:T(8,128)S(1)}, u32[]{:S(2)}, u32[]{:S(2)}) %all-to-all-start.2) | async-done | bytes 1048608 | tf_op jit(solution)/shard_map/all_to_all | solution.py:185
  96.4 5.5 %collective-permute-start.3 = (bf16[4,128,1280]{2,1,0:T(8,128)(2,1)S(1)}, bf16[4,128,1280]{2,1,0:T(8,128)(2,1)S(1)}, u32[]{:S(2)}, u32[]{:S(2)}) collective-permute-start(bf16[4,128,1280]{2,1,0:T(8,128)(2,1)S(1)} %all-to-all-done.1.same), channel_id=1, source_target_pairs={{0,32},{32,0},{1,33},{33,1},{2,34},{34,2},{3,35},{35,3},{4,36},{36... | collective-permute-start | bytes 3932168 | tf_op jit(solution)/shard_map/ppermute | solution.py:151
  101.9 1.9 %collective-permute-start.11 = (f32[32,1024]{1,0:T(8,128)S(1)}, f32[32,1024]{1,0:T(8,128)S(1)}, u32[]{:S(2)}, u32[]{:S(2)}) collective-permute-start(f32[32,1024]{1,0:T(8,128)S(1)} %get-tuple-element.23), channel_id=1, source_target_pairs={{0,32},{32,0},{1,33},{33,1},{2,34},{34,2},{3,35},{35,3},{4,36},{36... | collective-permute-start | bytes 393224 | tf_op jit(solution)/shard_map/ppermute | solution.py:151
  103.8 2.8 %collective-permute-start.6 = (bf16[128,1024]{1,0:T(8,128)(2,1)}, bf16[128,1024]{1,0:T(8,128)(2,1)S(1)}, u32[]{:S(2)}, u32[]{:S(2)}) collective-permute-start(bf16[128,1024]{1,0:T(8,128)(2,1)} %copy-done.9), channel_id=1, source_target_pairs={{0,192},{64,0},{128,64},{192,128},{1,193},{65,1},{129,65},{193,129... | collective-permute-start | bytes 786440 | tf_op jit(solution)/shard_map/ppermute | solution.py:190
  106.6 2.5 %collective-permute-start.4 = (bf16[128,1024]{1,0:T(8,128)(2,1)}, bf16[128,1024]{1,0:T(8,128)(2,1)}, u32[]{:S(2)}, u32[]{:S(2)}) collective-permute-start(bf16[128,1024]{1,0:T(8,128)(2,1)} %copy-done.9), channel_id=1, source_target_pairs={{0,64},{64,128},{128,192},{192,0},{1,65},{65,129},{129,193},{193,1... | collective-permute-start | bytes 786440 | tf_op jit(solution)/shard_map/ppermute | solution.py:190
  109.1 2.5 %collective-permute-start.5 = (bf16[128,1024]{1,0:T(8,128)(2,1)}, bf16[128,1024]{1,0:T(8,128)(2,1)}, u32[]{:S(2)}, u32[]{:S(2)}) collective-permute-start(bf16[128,1024]{1,0:T(8,128)(2,1)} %copy-done.9), channel_id=1, source_target_pairs={{0,128},{64,192},{128,0},{192,64},{1,129},{65,193},{129,1},{193,65... | collective-permute-start | bytes 786440 | tf_op jit(solution)/shard_map/ppermute | solution.py:190
  112.4 27.4 %all-to-all-start.3 = ((bf16[16,4,1024]{2,1,0:T(4,128)(2,1)}), bf16[16,4,1024]{2,1,0:T(4,128)(2,1)S(1)}, u32[]{:S(2)}, u32[]{:S(2)}) async-start(bf16[16,4,1024]{2,1,0:T(4,128)(2,1)} %shard_map.95), calls=%async_computation.3 | async-start | bytes 262144 | tf_op jit(solution)/shard_map/all_to_all | solution.py:194
  139.8 3.4 %collective-permute-start.7 = (bf16[128,1024]{1,0:T(8,128)(2,1)}, bf16[128,1024]{1,0:T(8,128)(2,1)S(1)}, u32[]{:S(2)}, u32[]{:S(2)}) collective-permute-start(bf16[128,1024]{1,0:T(8,128)(2,1)} %copy-done.9), channel_id=1, source_target_pairs={{0,32},{32,0},{1,33},{33,1},{2,34},{34,2},{3,35},{35,3},{4,36},{36... | collective-permute-start | bytes 786440 | tf_op jit(solution)/shard_map/ppermute | solution.py:151
  143.2 1.9 %collective-permute-start.10 = (bf16[128,1024]{1,0:T(8,128)(2,1)S(1)}, bf16[128,1024]{1,0:T(8,128)(2,1)S(1)}, u32[]{:S(2)}, u32[]{:S(2)}) collective-permute-start(bf16[128,1024]{1,0:T(8,128)(2,1)S(1)} %collective-permute-done.6.refs_2_), channel_id=1, source_target_pairs={{0,32},{32,0},{1,33},{33,1},{2,34},{34,2},{3,35},{35,3},{4,36},{36... | collective-permute-start | bytes 786440 | tf_op jit(solution)/shard_map/ppermute | solution.py:151
  145.1 2.4 %collective-permute-start.8 = (bf16[128,1024]{1,0:T(8,128)(2,1)}, bf16[128,1024]{1,0:T(8,128)(2,1)S(1)}, u32[]{:S(2)}, u32[]{:S(2)}) collective-permute-start(bf16[128,1024]{1,0:T(8,128)(2,1)} %collective-permute-done.4.refs_0_), channel_id=1, source_target_pairs={{0,32},{32,0},{1,33},{33,1},{2,34},{34,2},{3,35},{35,3},{4,36},{36... | collective-permute-start | bytes 786440 | tf_op jit(solution)/shard_map/ppermute | solution.py:151
  147.5 1.9 %collective-permute-start.9 = (bf16[128,1024]{1,0:T(8,128)(2,1)}, bf16[128,1024]{1,0:T(8,128)(2,1)S(1)}, u32[]{:S(2)}, u32[]{:S(2)}) collective-permute-start(bf16[128,1024]{1,0:T(8,128)(2,1)} %collective-permute-done.5.refs_1_), channel_id=1, source_target_pairs={{0,32},{32,0},{1,33},{33,1},{2,34},{34,2},{3,35},{35,3},{4,36},{36... | collective-permute-start | bytes 786440 | tf_op jit(solution)/shard_map/ppermute | solution.py:151
  149.5 1.0 copy-done.5
  151.3 3.1 %shard_map.94 = f32[128,1024]{1,0:T(8,128)} custom-call(bf16[128,2048]{1,0:T(8,128)(2,1)S(1)} %get-tuple-element.14.tile, f32[128,1024]{1,0:T(8,128)S(1)} %shard_map.93.near, bf16[1024,1024]{1,0:T(8,128)(2,1)S(1)} %copy-done.1, bf16[128,1024]{1,0:T(8,128)(2,1)} %collective-permute-done.4.refs_0_, bf16[128,1024]{1,0:T(8,128)(2,1)} %collective-permute-done.5.refs_1_, ...), custom_call_target="tpu_custom_call" | custom-call | flops 1 | bytes 1 | tf_op jit(solution)/shard_map/pallas_call | solution.py:22
  154.4 9.9 %all_to_all.26 = f32[8,4,1024]{2,1,0:T(4,128)S(1)} all-to-all(f32[8,4,1024]{2,1,0:T(4,128)S(1)} %shard_map.96), channel_id=1, replica_groups=mesh['zh'=2,'y'=4,'co'=2,'x'=4,'zl'=8] {'y','co'}, dimensions={0} | all-to-all | bytes 262144 | tf_op jit(solution)/shard_map/all_to_all | solution.py:198
  (36 shorter events, 5.6 us)
Async XLA Ops:
  1.4 1.0 copy-start.3
  2.4 0.9 copy-start.7
  3.4 0.7 copy-start.8
  23.4 9.9 %collective-permute-start = (bf16[4,128,1280]{2,1,0:T(8,128)(2,1)S(1)}, bf16[4,128,1280]{2,1,0:T(8,128)(2,1)S(1)}, u32[]{:S(2)}, u32[]{:S(2)}) collective-permute-start(bf16[4,128,1280]{2,1,0:T(8,128)(2,1)S(1)} %all_to_all.25.same), channel_id=1, source_target_pairs={{0,32},{32,0},{1,33},{33,1},{2,34},{34,2},{3,35},{35,3},{4,36},{36... | collective-permute-start | bytes 3932168 | tf_op jit(solution)/shard_map/ppermute | solution.py:151
  34.0 21.8 %collective-permute-start.1 = (bf16[128,1024]{1,0:T(8,128)(2,1)S(1)}, bf16[128,1024]{1,0:T(8,128)(2,1)S(1)}, u32[]{:S(2)}, u32[]{:S(2)}) collective-permute-start(bf16[128,1024]{1,0:T(8,128)(2,1)S(1)} %shard_map.87), channel_id=1, source_target_pairs={{0,256},{256,0},{1,257},{257,1},{2,258},{258,2},{3,259},{259,3},{4... | collective-permute-start | bytes 786440 | tf_op jit(solution)/shard_map/ppermute | solution.py:139
  50.2 5.5 %copy-start = (bf16[1024,1024]{1,0:T(8,128)(2,1)S(1)}, bf16[1024,1024]{1,0:T(8,128)(2,1)}, u32[]{:S(2)}) copy-start(bf16[1024,1024]{1,0:T(8,128)(2,1)} %weight.3) | copy-start | bytes 6291460
  50.2 5.5 %copy-start.6 = (bf16[128,1024]{1,0:T(8,128)(2,1)S(1)}, bf16[128,1024]{1,0:T(8,128)(2,1)}, u32[]{:S(2)}) copy-start(bf16[128,1024]{1,0:T(8,128)(2,1)} %cotangent.1) | copy-start | bytes 786436
  57.9 20.3 %all-to-all-start.1 = ((bf16[4,128,1280]{2,1,0:T(8,128)(2,1)}), bf16[4,128,1280]{2,1,0:T(8,128)(2,1)S(1)}, u32[]{:S(2)}, u32[]{:S(2)}) async-start(bf16[4,128,1280]{2,1,0:T(8,128)(2,1)} %get-tuple-element.18), calls=%async_computation.1 | async-start | bytes 2621440 | tf_op jit(solution)/shard_map/all_to_all | solution.py:147
  61.5 23.0 %collective-permute-start.2 = (bf16[128,1024]{1,0:T(8,128)(2,1)S(1)}, bf16[128,1024]{1,0:T(8,128)(2,1)S(1)}, u32[]{:S(2)}, u32[]{:S(2)}) collective-permute-start(bf16[128,1024]{1,0:T(8,128)(2,1)S(1)} %get-tuple-element.17), channel_id=1, source_target_pairs={{0,256},{256,0},{1,257},{257,1},{2,258},{258,2},{3,259},{259,3},{4... | collective-permute-start | bytes 786440 | tf_op jit(solution)/shard_map/ppermute | solution.py:139
  78.9 1.0 copy-start.2
  79.9 16.4 %all-to-all-start.2 = ((f32[4,64,1024]{2,1,0:T(8,128)}), f32[4,64,1024]{2,1,0:T(8,128)S(1)}, u32[]{:S(2)}, u32[]{:S(2)}) async-start(f32[4,64,1024]{2,1,0:T(8,128)} %bitcast.4), calls=%async_computation.2 | async-start | bytes 2097152 | tf_op jit(solution)/shard_map/all_to_all | solution.py:185
  84.5 0.7 copy-start.9
  85.2 0.8 copy-start.4
  96.4 53.1 %collective-permute-start.3 = (bf16[4,128,1280]{2,1,0:T(8,128)(2,1)S(1)}, bf16[4,128,1280]{2,1,0:T(8,128)(2,1)S(1)}, u32[]{:S(2)}, u32[]{:S(2)}) collective-permute-start(bf16[4,128,1280]{2,1,0:T(8,128)(2,1)S(1)} %all-to-all-done.1.same), channel_id=1, source_target_pairs={{0,32},{32,0},{1,33},{33,1},{2,34},{34,2},{3,35},{35,3},{4,36},{36... | collective-permute-start | bytes 3932168 | tf_op jit(solution)/shard_map/ppermute | solution.py:151
  101.9 9.8 %collective-permute-start.11 = (f32[32,1024]{1,0:T(8,128)S(1)}, f32[32,1024]{1,0:T(8,128)S(1)}, u32[]{:S(2)}, u32[]{:S(2)}) collective-permute-start(f32[32,1024]{1,0:T(8,128)S(1)} %get-tuple-element.23), channel_id=1, source_target_pairs={{0,32},{32,0},{1,33},{33,1},{2,34},{34,2},{3,35},{35,3},{4,36},{36... | collective-permute-start | bytes 393224 | tf_op jit(solution)/shard_map/ppermute | solution.py:151
  103.8 39.3 %collective-permute-start.6 = (bf16[128,1024]{1,0:T(8,128)(2,1)}, bf16[128,1024]{1,0:T(8,128)(2,1)S(1)}, u32[]{:S(2)}, u32[]{:S(2)}) collective-permute-start(bf16[128,1024]{1,0:T(8,128)(2,1)} %copy-done.9), channel_id=1, source_target_pairs={{0,192},{64,0},{128,64},{192,128},{1,193},{65,1},{129,65},{193,129... | collective-permute-start | bytes 786440 | tf_op jit(solution)/shard_map/ppermute | solution.py:190
  106.6 38.5 %collective-permute-start.4 = (bf16[128,1024]{1,0:T(8,128)(2,1)}, bf16[128,1024]{1,0:T(8,128)(2,1)}, u32[]{:S(2)}, u32[]{:S(2)}) collective-permute-start(bf16[128,1024]{1,0:T(8,128)(2,1)} %copy-done.9), channel_id=1, source_target_pairs={{0,64},{64,128},{128,192},{192,0},{1,65},{65,129},{129,193},{193,1... | collective-permute-start | bytes 786440 | tf_op jit(solution)/shard_map/ppermute | solution.py:190
  109.1 38.4 %collective-permute-start.5 = (bf16[128,1024]{1,0:T(8,128)(2,1)}, bf16[128,1024]{1,0:T(8,128)(2,1)}, u32[]{:S(2)}, u32[]{:S(2)}) collective-permute-start(bf16[128,1024]{1,0:T(8,128)(2,1)} %copy-done.9), channel_id=1, source_target_pairs={{0,128},{64,192},{128,0},{192,64},{1,129},{65,193},{129,1},{193,65... | collective-permute-start | bytes 786440 | tf_op jit(solution)/shard_map/ppermute | solution.py:190
  112.4 42.0 %all-to-all-start.3 = ((bf16[16,4,1024]{2,1,0:T(4,128)(2,1)}), bf16[16,4,1024]{2,1,0:T(4,128)(2,1)S(1)}, u32[]{:S(2)}, u32[]{:S(2)}) async-start(bf16[16,4,1024]{2,1,0:T(4,128)(2,1)} %shard_map.95), calls=%async_computation.3 | async-start | bytes 262144 | tf_op jit(solution)/shard_map/all_to_all | solution.py:194
  139.7 11.5 %copy-start.1 = (bf16[1024,1024]{1,0:T(8,128)(2,1)S(1)}, bf16[1024,1024]{1,0:T(8,128)(2,1)}, u32[]{:S(2)}) copy-start(bf16[1024,1024]{1,0:T(8,128)(2,1)} %weight.3) | copy-start | bytes 6291460
  139.8 11.4 %collective-permute-start.7 = (bf16[128,1024]{1,0:T(8,128)(2,1)}, bf16[128,1024]{1,0:T(8,128)(2,1)S(1)}, u32[]{:S(2)}, u32[]{:S(2)}) collective-permute-start(bf16[128,1024]{1,0:T(8,128)(2,1)} %copy-done.9), channel_id=1, source_target_pairs={{0,32},{32,0},{1,33},{33,1},{2,34},{34,2},{3,35},{35,3},{4,36},{36... | collective-permute-start | bytes 786440 | tf_op jit(solution)/shard_map/ppermute | solution.py:151
  143.2 8.1 %collective-permute-start.10 = (bf16[128,1024]{1,0:T(8,128)(2,1)S(1)}, bf16[128,1024]{1,0:T(8,128)(2,1)S(1)}, u32[]{:S(2)}, u32[]{:S(2)}) collective-permute-start(bf16[128,1024]{1,0:T(8,128)(2,1)S(1)} %collective-permute-done.6.refs_2_), channel_id=1, source_target_pairs={{0,32},{32,0},{1,33},{33,1},{2,34},{34,2},{3,35},{35,3},{4,36},{36... | collective-permute-start | bytes 786440 | tf_op jit(solution)/shard_map/ppermute | solution.py:151
  145.1 6.1 %collective-permute-start.8 = (bf16[128,1024]{1,0:T(8,128)(2,1)}, bf16[128,1024]{1,0:T(8,128)(2,1)S(1)}, u32[]{:S(2)}, u32[]{:S(2)}) collective-permute-start(bf16[128,1024]{1,0:T(8,128)(2,1)} %collective-permute-done.4.refs_0_), channel_id=1, source_target_pairs={{0,32},{32,0},{1,33},{33,1},{2,34},{34,2},{3,35},{35,3},{4,36},{36... | collective-permute-start | bytes 786440 | tf_op jit(solution)/shard_map/ppermute | solution.py:151
  147.5 3.7 %collective-permute-start.9 = (bf16[128,1024]{1,0:T(8,128)(2,1)}, bf16[128,1024]{1,0:T(8,128)(2,1)S(1)}, u32[]{:S(2)}, u32[]{:S(2)}) collective-permute-start(bf16[128,1024]{1,0:T(8,128)(2,1)} %collective-permute-done.5.refs_1_), channel_id=1, source_target_pairs={{0,32},{32,0},{1,33},{33,1},{2,34},{34,2},{3,35},{35,3},{4,36},{36... | collective-permute-start | bytes 786440 | tf_op jit(solution)/shard_map/ppermute | solution.py:151
  149.5 1.0 copy-start.5

commit v7 on v6

--- a/solution.py
+++ b/solution.py
@@ -67,11 +67,16 @@
     begun[...] = dot(tile[:, 1024:1152], far[...])
 
 
-def prepare_body(place, codes, count, values, features, message, tile):
+def prepare_body(place, codes, count, values_hbm, features, message, tile, values, sems):
+    copies = [pltpu.make_async_copy(values_hbm.at[0], values, sems.at[4])]
+    for y in range(4):
+        copies.append(pltpu.make_async_copy(features, message.at[y, :, COLS], sems.at[y]))
+    for copy in copies:
+        copy.start()
     tile[...] = jnp.zeros(tile.shape, BF16)
     for y in range(4):
-        message[y, :, COLS] = features[...]
         message[y, :, 1024:1280] = jnp.zeros((128, 256), BF16)
+    copies[0].wait()
 
     def slot(k, carry):
         grid_row = lax.div(lax.rem(codes[0, k], 512), 32)
@@ -79,15 +84,17 @@
         own = lax.div(grid_row, 8) == place[0]
 
         at = 512 * other + jnp.where(own, 128 * y, 1024 + 128 * lax.rem(place[2] - y + 4, 4))
-        tile[:, pl.ds(pl.multiple_of(at, 128), 128)] = values[0, k]
+        tile[:, pl.ds(pl.multiple_of(at, 128), 128)] = values[k]
 
         @pl.when(jnp.logical_not(own))
         def _():
-            message[y, :, pl.ds(pl.multiple_of(1024 + 128 * other, 128), 128)] = values[0, k]
+            message[y, :, pl.ds(pl.multiple_of(1024 + 128 * other, 128), 128)] = values[k]
 
         return carry
 
     lax.fori_loop(0, count[0], slot, 0)
+    for copy in copies[1:]:
+        copy.wait()
 
 
 def far_body(same, other, far):
@@ -98,21 +105,16 @@
     far[...] = total.astype(BF16)
 
 
-def partial_body(same, partial):
+def partial_body(same, other, partial):
     total = 0.0
     for y in range(4):
-        total += dot(same[y, :, 1024:1280], same[y, :, COLS], 0, 0)
+        total += dot(same[y, :, 1024:1152], same[y, :, COLS], 0, 0)
+        total += dot(other[y, :, 1152:1280], other[y, :, COLS], 0, 0)
     partial[...] = total
 
 
-def sum_x_body(pieces, keep, send):
+def sum_x_body(pieces, out):
     total = pieces[0] + pieces[1] + pieces[2] + pieces[3]
-    keep[...] = total[0:32]
-    send[...] = total[32:64]
-
-
-def sum_core_body(keep, received, out):
-    total = keep[...] + received[...]
     for z in range(8):
         rows = total[4 * z : 4 * z + 4].astype(BF16)
         out[z] = rows
@@ -155,8 +157,8 @@
     zh, core = lax.axis_index("zh"), lax.axis_index("co")
     hidden = features.shape[1]
     at = jnp.arange(hidden)
-    row = 8 * (at // 256) + 4 * (at // 32 % 2 ^ core) + at % 4
-    source = 32 * (8 * (at // 64 % 4) + at // 4 % 8) + row
+    group = 2 * (at // 256) + (at // 128 % 2 ^ core)
+    source = 32 * (at // 4 % 32) + 4 * group + at % 4
     regroup = (jnp.arange(hidden)[:, None] == source[None, :]).astype(BF16)
 
     def shape(*dims, dtype=F32):
@@ -165,8 +167,16 @@
     rows_f32, rows_bf16 = shape(128, hidden), shape(128, hidden, dtype=BF16)
     message_shape = shape(4, 128, hidden + 256, dtype=BF16)
 
-    message, tile = call(
-        prepare_body, (message_shape, shape(128, 2048, dtype=BF16)),
+    message, tile = pl.pallas_call(
+        prepare_body,
+        out_shape=(message_shape, shape(128, 2048, dtype=BF16)),
+        in_specs=[SMEM] * 3 + [pl.BlockSpec(memory_space=pl.ANY)] * 2,
+        out_specs=(VMEM, VMEM),
+        scratch_shapes=[
+            pltpu.VMEM(block_values.shape[1:], BF16), pltpu.SemaphoreType.DMA((5,)),
+        ],
+        compiler_params=pltpu.CompilerParams(vmem_limit_bytes=16 * 2**20),
+    )(
         jnp.stack([zh, core, lax.axis_index("y")]), block_codes, block_count, block_values, features,
     )
     same = over_y(message)
@@ -181,20 +191,17 @@
     far = partner(slope)
     same = over_y(message)
     output = call(output_body, rows_f32, summed, flops=10**11)
-    partial = call(partial_body, shape(256, hidden), after(same, output))
-    part = lax.all_to_all(partial.reshape(4, 64, hidden), "x", 0, 0)
+    other = other_core(after(same, output))
     begun = call(start_body, rows_f32, tile, far, flops=10**11)
-    keep, send = call(
-        sum_x_body, (shape(32, hidden), shape(32, hidden)), after(part, begun)
-    )
+    partial = call(partial_body, rows_f32, same, after(other, begun))
+    part = lax.all_to_all(partial.reshape(4, 32, hidden), "x", 0, 0)
     others = [lax.ppermute(far, "y", [(i, (i + k) % 4) for i in range(4)]) for k in (1, 2, 3)]
-    other = other_core(after(same, keep))
     near = call(second_body, rows_f32, tile, begun, same, other)
-    part = call(sum_core_body, shape(16, 4, hidden, dtype=BF16), keep, other_core(send))
+    part = call(sum_x_body, shape(16, 4, hidden, dtype=BF16), after(part, *others))
     part = lax.all_to_all(part, ("zh", "zl"), 0, 0)
     swapped = [other_core(v) for v in (far, *others)]
     input_grad = call(backward_body, rows_f32, tile, near, weight, *others, *swapped)
-    part = call(sum_z_body, shape(8, 4, hidden), after(part, input_grad))
+    part = call(sum_z_body, shape(8, 4, hidden), part)
     part = lax.all_to_all(part, ("y", "co"), 0, 0)
     weight_grad = part.reshape(32, hidden)
     return output, input_grad, weight_grad

time: 166 us -> 173 us (1.042)
  starting transfers between devices: 94.2 us -> 106 us
  blocking collectives: 28.4 us -> 18.4 us
  waiting for transfers between devices: 22.3 us -> 25.3 us
  Pallas kernels: 10.8 us -> 12.9 us
    all_to_all x1 -> x2, waiting for transfers between devices: 10.3 us -> 0.01 us  [the longest x1 0.01 us: local(): part = lax.all_to_all(part, ('y', 'co'), 0, 0)]
    ppermute x3, waiting for transfers between devices: 0.01 us -> 10.3 us  [local(): lax.ppermute(far, 'y', [(i, (i + k) % 4) for i in range(4)])]
    all_to_all x1 -> x0, blocking collectives: 9.91 us -> none  [local(): part = lax.all_to_all(part, ('y', 'co'), 0, 0)]
    all_to_all x1 -> x2, starting transfers between devices: 3.98 us -> 12.9 us  [the longest x1 8.77 us: local(): part = lax.all_to_all(part, ('y', 'co'), 0, 0)]
    all_to_all x1, starting transfers between devices: 27.4 us -> 31.9 us  [local(): part = lax.all_to_all(part, ('zh', 'zl'), 0, 0)]
    ppermute x7 -> x6, starting transfers between devices: 24.3 us -> 21.8 us  [other_core(): return lax.ppermute(rows, 'co', SWAP)]
    pallas_call x12 -> x10, Pallas kernels: 10.8 us -> 11.9 us  [call(): pl.pallas_call(body, out_shape=outs, in_specs=[SMEM if a.dtype == jnp.int...]
  transfers between devices with their start and end apart: 15 -> 15, of which waited for: 5 -> 8; matrix products, arithmetic and copies ran while one was open for 1% -> 1% of each run, Pallas kernels for 4% -> 4%
where the time goes in v7:
time: 173 us; the launch traced here: 172 us
  starting transfers between devices  106 us (61%)
  waiting for transfers between devices  25.3 us (15%)
  blocking collectives  18.4 us (11%)
  Pallas kernels  12.9 us (7%)
  local copies, waits for them, and re-layouts  7.34 us (4%)
    all_to_all x1, starting transfers between devices, local(): part = lax.all_to_all(part, ('zh', 'zl'), 0, 0)  31.9 us
    ppermute x2, starting transfers between devices, partner(): return lax.ppermute(rows, 'zh', SWAP)  27.2 us
    ppermute x6, starting transfers between devices, other_core(): return lax.ppermute(rows, 'co', SWAP)  21.8 us
    all_to_all x1, blocking collectives, over_y(): return lax.all_to_all(message, 'y', 0, 0)  18.4 us
    pallas_call x10, Pallas kernels, call(): pl.pallas_call(body, out_shape=outs, in_specs=[SMEM if a.dtype == jnp.int...  11.9 us
    ppermute x3, waiting for transfers between devices, local(): lax.ppermute(far, 'y', [(i, (i + k) % 4) for i in range(4)])  10.3 us
    all_to_all x1, starting transfers between devices, local(): part = lax.all_to_all(part, ('y', 'co'), 0, 0)  8.77 us
    ppermute x3, starting transfers between devices, local(): lax.ppermute(far, 'y', [(i, (i + k) % 4) for i in range(4)])  8.42 us
  transfers between devices with their start and end apart: 15, of which 8 were waited for; matrix products, arithmetic and copies ran while one was open for 1% of the time, Pallas kernels for 4%

profile of v7, /device:TPU:1, one launch (start us, length us, event | category | flops | bytes accessed | tf_op | source)
XLA Modules:
  0.0 172.4 jit_solution(14604131666101620875)
XLA Ops:
  1.4 1.0 copy-done.3
  2.4 0.9 copy-done.7
  4.0 1.0 shard_map.85
  5.0 18.4 %all_to_all.25.same = bf16[4,128,1280]{2,1,0:T(8,128)(2,1)S(1)} all-to-all(bf16[4,128,1280]{2,1,0:T(8,128)(2,1)S(1)} %get-tuple-element.12), channel_id=1, replica_groups=mesh['zh'=2,'y'=4,'co'=2,'x'=4,'zl'=8] {'y'}, dimensions={0} | all-to-all | bytes 2621440 | tf_op jit(solution)/shard_map/all_to_all | solution.py:149
  23.4 7.2 %collective-permute-start = (bf16[4,128,1280]{2,1,0:T(8,128)(2,1)S(1)}, bf16[4,128,1280]{2,1,0:T(8,128)(2,1)S(1)}, u32[]{:S(2)}, u32[]{:S(2)}) collective-permute-start(bf16[4,128,1280]{2,1,0:T(8,128)(2,1)S(1)} %all_to_all.25.same), channel_id=1, source_target_pairs={{0,32},{32,0},{1,33},{33,1},{2,34},{34,2},{3,35},{35,3},{4,36},{36... | collective-permute-start | bytes 3932168 | tf_op jit(solution)/shard_map/ppermute | solution.py:153
  30.7 2.6 %collective-permute-done.other = bf16[4,128,1280]{2,1,0:T(8,128)(2,1)S(1)} collective-permute-done((bf16[4,128,1280]{2,1,0:T(8,128)(2,1)S(1)}, bf16[4,128,1280]{2,1,0:T(8,128)(2,1)S(1)}, u32[]{:S(2)}, u32[]{:S(2)}) %collective-permute-start) | collective-permute-done | bytes 1310752 | tf_op jit(solution)/shard_map/ppermute | solution.py:153
  34.0 15.4 %collective-permute-start.1 = (bf16[128,1024]{1,0:T(8,128)(2,1)S(1)}, bf16[128,1024]{1,0:T(8,128)(2,1)S(1)}, u32[]{:S(2)}, u32[]{:S(2)}) collective-permute-start(bf16[128,1024]{1,0:T(8,128)(2,1)S(1)} %shard_map.87), channel_id=1, source_target_pairs={{0,256},{256,0},{1,257},{257,1},{2,258},{258,2},{3,259},{259,3},{4... | collective-permute-start | bytes 786440 | tf_op jit(solution)/shard_map/ppermute | solution.py:141
  49.4 0.9 fusion.regroup
  51.1 4.8 %collective-permute-done.1.far = bf16[128,1024]{1,0:T(8,128)(2,1)S(1)} collective-permute-done((bf16[128,1024]{1,0:T(8,128)(2,1)S(1)}, bf16[128,1024]{1,0:T(8,128)(2,1)S(1)}, u32[]{:S(2)}, u32[]{:S(2)}) %collective-permute-start.1) | collective-permute-done | bytes 262176 | tf_op jit(solution)/shard_map/ppermute | solution.py:141
  55.8 2.2 %shard_map.88 = (f32[128,1024]{1,0:T(8,128)S(1)}, bf16[4,128,1280]{2,1,0:T(8,128)(2,1)}, bf16[128,1024]{1,0:T(8,128)(2,1)}) custom-call(f32[128,1024]{1,0:T(8,128)S(1)} %shard_map.86.near, bf16[128,1024]{1,0:T(8,128)(2,1)S(1)} %collective-permute-done.1.far, bf16[1024,1024]{1,0:T(8,128)(2,1)S(1)} %copy-done, bf16[128,1024]{1,0:T(8,128)(2,1)S(1)} %copy-done.6, ...), custom_call_target="tpu_custom_call" | custom-call | flops 1 | bytes 1 | tf_op jit(solution)/shard_map/pallas_call | solution.py:22
  58.0 3.5 %all-to-all-start.1 = ((bf16[4,128,1280]{2,1,0:T(8,128)(2,1)}), bf16[4,128,1280]{2,1,0:T(8,128)(2,1)S(1)}, u32[]{:S(2)}, u32[]{:S(2)}) async-start(bf16[4,128,1280]{2,1,0:T(8,128)(2,1)} %get-tuple-element.15), calls=%async_computation.1 | async-start | bytes 2621440 | tf_op jit(solution)/shard_map/all_to_all | solution.py:149
  61.6 11.8 %collective-permute-start.2 = (bf16[128,1024]{1,0:T(8,128)(2,1)}, bf16[128,1024]{1,0:T(8,128)(2,1)S(1)}, u32[]{:S(2)}, u32[]{:S(2)}) collective-permute-start(bf16[128,1024]{1,0:T(8,128)(2,1)} %get-tuple-element.14), channel_id=1, source_target_pairs={{0,256},{256,0},{1,257},{257,1},{2,258},{258,2},{3,259},{259,3},{4... | collective-permute-start | bytes 786440 | tf_op jit(solution)/shard_map/ppermute | solution.py:141
  74.3 4.0 %all-to-all-done.1.same = bf16[4,128,1280]{2,1,0:T(8,128)(2,1)S(1)} async-done(((bf16[4,128,1280]{2,1,0:T(8,128)(2,1)}), bf16[4,128,1280]{2,1,0:T(8,128)(2,1)S(1)}, u32[]{:S(2)}, u32[]{:S(2)}) %all-to-all-start.1) | async-done | bytes 1310752 | tf_op jit(solution)/shard_map/all_to_all | solution.py:149
  78.3 4.0 %collective-permute-start.3 = (bf16[4,128,1280]{2,1,0:T(8,128)(2,1)S(1)}, bf16[4,128,1280]{2,1,0:T(8,128)(2,1)S(1)}, u32[]{:S(2)}, u32[]{:S(2)}) collective-permute-start(bf16[4,128,1280]{2,1,0:T(8,128)(2,1)S(1)} %all-to-all-done.1.same), channel_id=1, source_target_pairs={{0,32},{32,0},{1,33},{33,1},{2,34},{34,2},{3,35},{35,3},{4,36},{36... | collective-permute-start | bytes 3932168 | tf_op jit(solution)/shard_map/ppermute | solution.py:153
  82.3 2.3 %collective-permute-done.2.far = bf16[128,1024]{1,0:T(8,128)(2,1)S(1)} collective-permute-done((bf16[128,1024]{1,0:T(8,128)(2,1)}, bf16[128,1024]{1,0:T(8,128)(2,1)S(1)}, u32[]{:S(2)}, u32[]{:S(2)}) %collective-permute-start.2) | collective-permute-done | bytes 262176 | tf_op jit(solution)/shard_map/ppermute | solution.py:141
  87.6 4.1 %all-to-all-start.2 = ((f32[4,32,1024]{2,1,0:T(8,128)}), f32[4,32,1024]{2,1,0:T(8,128)}, u32[]{:S(2)}, u32[]{:S(2)}) async-start(f32[4,32,1024]{2,1,0:T(8,128)} %bitcast.4), calls=%async_computation.2 | async-start | bytes 1048576 | tf_op jit(solution)/shard_map/all_to_all | solution.py:197
  91.8 2.2 %collective-permute-start.4 = (bf16[128,1024]{1,0:T(8,128)(2,1)}, bf16[128,1024]{1,0:T(8,128)(2,1)S(1)}, u32[]{:S(2)}, u32[]{:S(2)}) collective-permute-start(bf16[128,1024]{1,0:T(8,128)(2,1)} %copy-done.9), channel_id=1, source_target_pairs={{0,64},{64,128},{128,192},{192,0},{1,65},{65,129},{129,193},{193,1... | collective-permute-start | bytes 786440 | tf_op jit(solution)/shard_map/ppermute | solution.py:198
  94.0 3.7 %collective-permute-start.5 = (bf16[128,1024]{1,0:T(8,128)(2,1)}, bf16[128,1024]{1,0:T(8,128)(2,1)}, u32[]{:S(2)}, u32[]{:S(2)}) collective-permute-start(bf16[128,1024]{1,0:T(8,128)(2,1)} %copy-done.9), channel_id=1, source_target_pairs={{0,128},{64,192},{128,0},{192,64},{1,129},{65,193},{129,1},{193,65... | collective-permute-start | bytes 786440 | tf_op jit(solution)/shard_map/ppermute | solution.py:198
  97.7 2.5 %collective-permute-start.6 = (bf16[128,1024]{1,0:T(8,128)(2,1)}, bf16[128,1024]{1,0:T(8,128)(2,1)}, u32[]{:S(2)}, u32[]{:S(2)}) collective-permute-start(bf16[128,1024]{1,0:T(8,128)(2,1)} %copy-done.9), channel_id=1, source_target_pairs={{0,192},{64,0},{128,64},{192,128},{1,193},{65,1},{129,65},{193,129... | collective-permute-start | bytes 786440 | tf_op jit(solution)/shard_map/ppermute | solution.py:198
  100.2 2.4 %collective-permute-done.4.refs_0_ = bf16[128,1024]{1,0:T(8,128)(2,1)S(1)} collective-permute-done((bf16[128,1024]{1,0:T(8,128)(2,1)}, bf16[128,1024]{1,0:T(8,128)(2,1)S(1)}, u32[]{:S(2)}, u32[]{:S(2)}) %collective-permute-start.4) | collective-permute-done | bytes 262176 | tf_op jit(solution)/shard_map/ppermute | solution.py:198
  102.6 4.8 %collective-permute-done.5.refs_1_ = bf16[128,1024]{1,0:T(8,128)(2,1)} collective-permute-done((bf16[128,1024]{1,0:T(8,128)(2,1)}, bf16[128,1024]{1,0:T(8,128)(2,1)}, u32[]{:S(2)}, u32[]{:S(2)}) %collective-permute-start.5) | collective-permute-done | bytes 262176 | tf_op jit(solution)/shard_map/ppermute | solution.py:198
  107.4 3.1 %collective-permute-done.6.refs_2_ = bf16[128,1024]{1,0:T(8,128)(2,1)} collective-permute-done((bf16[128,1024]{1,0:T(8,128)(2,1)}, bf16[128,1024]{1,0:T(8,128)(2,1)}, u32[]{:S(2)}, u32[]{:S(2)}) %collective-permute-start.6) | collective-permute-done | bytes 262176 | tf_op jit(solution)/shard_map/ppermute | solution.py:198
  110.5 1.7 %shard_map.94 = bf16[16,4,1024]{2,1,0:T(4,128)(2,1)} custom-call(f32[4,32,1024]{2,1,0:T(8,128)} %all-to-all-done.2.pieces), custom_call_target="tpu_custom_call" | custom-call | flops 1 | bytes 1 | tf_op jit(solution)/shard_map/pallas_call | solution.py:22
  112.2 31.9 %all-to-all-start.3 = ((bf16[16,4,1024]{2,1,0:T(4,128)(2,1)}), bf16[16,4,1024]{2,1,0:T(4,128)(2,1)S(1)}, u32[]{:S(2)}, u32[]{:S(2)}) async-start(bf16[16,4,1024]{2,1,0:T(4,128)(2,1)} %shard_map.94), calls=%async_computation.3 | async-start | bytes 262144 | tf_op jit(solution)/shard_map/all_to_all | solution.py:201
  144.2 4.4 %collective-permute-start.7 = (bf16[128,1024]{1,0:T(8,128)(2,1)}, bf16[128,1024]{1,0:T(8,128)(2,1)}, u32[]{:S(2)}, u32[]{:S(2)}) collective-permute-start(bf16[128,1024]{1,0:T(8,128)(2,1)} %copy-done.9), channel_id=1, source_target_pairs={{0,32},{32,0},{1,33},{33,1},{2,34},{34,2},{3,35},{35,3},{4,36},{36... | collective-permute-start | bytes 786440 | tf_op jit(solution)/shard_map/ppermute | solution.py:153
  148.5 1.9 %collective-permute-start.10 = (bf16[128,1024]{1,0:T(8,128)(2,1)}, bf16[128,1024]{1,0:T(8,128)(2,1)}, u32[]{:S(2)}, u32[]{:S(2)}) collective-permute-start(bf16[128,1024]{1,0:T(8,128)(2,1)} %collective-permute-done.6.refs_2_), channel_id=1, source_target_pairs={{0,32},{32,0},{1,33},{33,1},{2,34},{34,2},{3,35},{35,3},{4,36},{36... | collective-permute-start | bytes 786440 | tf_op jit(solution)/shard_map/ppermute | solution.py:153
  150.5 2.4 %collective-permute-start.8 = (bf16[128,1024]{1,0:T(8,128)(2,1)S(1)}, bf16[128,1024]{1,0:T(8,128)(2,1)}, u32[]{:S(2)}, u32[]{:S(2)}) collective-permute-start(bf16[128,1024]{1,0:T(8,128)(2,1)S(1)} %collective-permute-done.4.refs_0_), channel_id=1, source_target_pairs={{0,32},{32,0},{1,33},{33,1},{2,34},{34,2},{3,35},{35,3},{4,36},{36... | collective-permute-start | bytes 786440 | tf_op jit(solution)/shard_map/ppermute | solution.py:153
  152.9 1.9 %collective-permute-start.9 = (bf16[128,1024]{1,0:T(8,128)(2,1)}, bf16[128,1024]{1,0:T(8,128)(2,1)}, u32[]{:S(2)}, u32[]{:S(2)}) collective-permute-start(bf16[128,1024]{1,0:T(8,128)(2,1)} %collective-permute-done.5.refs_1_), channel_id=1, source_target_pairs={{0,32},{32,0},{1,33},{33,1},{2,34},{34,2},{3,35},{35,3},{4,36},{36... | collective-permute-start | bytes 786440 | tf_op jit(solution)/shard_map/ppermute | solution.py:153
  154.8 1.3 all-to-all-done.3.pieces
  156.8 8.8 %all-to-all-start.4 = ((f32[8,4,1024]{2,1,0:T(4,128)}), f32[8,4,1024]{2,1,0:T(4,128)S(1)}, u32[]{:S(2)}, u32[]{:S(2)}) async-start(f32[8,4,1024]{2,1,0:T(4,128)} %shard_map.95), calls=%async_computation.4 | async-start | bytes 262144 | tf_op jit(solution)/shard_map/all_to_all | solution.py:205
  165.6 1.0 copy-done.5
  168.2 3.5 %shard_map.92 = f32[128,1024]{1,0:T(8,128)} custom-call(bf16[128,2048]{1,0:T(8,128)(2,1)S(1)} %get-tuple-element.11.tile, f32[128,1024]{1,0:T(8,128)S(1)} %shard_map.91.near, bf16[1024,1024]{1,0:T(8,128)(2,1)S(1)} %copy-done.1, bf16[128,1024]{1,0:T(8,128)(2,1)S(1)} %collective-permute-done.4.refs_0_, bf16[128,1024]{1,0:T(8,128)(2,1)} %collective-permute-done.5.refs_1_, ...), custom_call_target="tpu_custom_call" | custom-call | flops 1 | bytes 1 | tf_op jit(solution)/shard_map/pallas_call | solution.py:22
  (34 shorter events, 9.0 us)
Async XLA Ops:
  1.4 1.0 copy-start.3
  2.4 0.9 copy-start.7
  3.4 0.7 copy-start.8
  23.4 9.9 %collective-permute-start = (bf16[4,128,1280]{2,1,0:T(8,128)(2,1)S(1)}, bf16[4,128,1280]{2,1,0:T(8,128)(2,1)S(1)}, u32[]{:S(2)}, u32[]{:S(2)}) collective-permute-start(bf16[4,128,1280]{2,1,0:T(8,128)(2,1)S(1)} %all_to_all.25.same), channel_id=1, source_target_pairs={{0,32},{32,0},{1,33},{33,1},{2,34},{34,2},{3,35},{35,3},{4,36},{36... | collective-permute-start | bytes 3932168 | tf_op jit(solution)/shard_map/ppermute | solution.py:153
  34.0 21.8 %collective-permute-start.1 = (bf16[128,1024]{1,0:T(8,128)(2,1)S(1)}, bf16[128,1024]{1,0:T(8,128)(2,1)S(1)}, u32[]{:S(2)}, u32[]{:S(2)}) collective-permute-start(bf16[128,1024]{1,0:T(8,128)(2,1)S(1)} %shard_map.87), channel_id=1, source_target_pairs={{0,256},{256,0},{1,257},{257,1},{2,258},{258,2},{3,259},{259,3},{4... | collective-permute-start | bytes 786440 | tf_op jit(solution)/shard_map/ppermute | solution.py:141
  50.3 5.5 %copy-start = (bf16[1024,1024]{1,0:T(8,128)(2,1)S(1)}, bf16[1024,1024]{1,0:T(8,128)(2,1)}, u32[]{:S(2)}) copy-start(bf16[1024,1024]{1,0:T(8,128)(2,1)} %weight.3) | copy-start | bytes 6291460
  50.3 5.5 %copy-start.6 = (bf16[128,1024]{1,0:T(8,128)(2,1)S(1)}, bf16[128,1024]{1,0:T(8,128)(2,1)}, u32[]{:S(2)}) copy-start(bf16[128,1024]{1,0:T(8,128)(2,1)} %cotangent.1) | copy-start | bytes 786436
  58.0 20.3 %all-to-all-start.1 = ((bf16[4,128,1280]{2,1,0:T(8,128)(2,1)}), bf16[4,128,1280]{2,1,0:T(8,128)(2,1)S(1)}, u32[]{:S(2)}, u32[]{:S(2)}) async-start(bf16[4,128,1280]{2,1,0:T(8,128)(2,1)} %get-tuple-element.15), calls=%async_computation.1 | async-start | bytes 2621440 | tf_op jit(solution)/shard_map/all_to_all | solution.py:149
  61.6 23.0 %collective-permute-start.2 = (bf16[128,1024]{1,0:T(8,128)(2,1)}, bf16[128,1024]{1,0:T(8,128)(2,1)S(1)}, u32[]{:S(2)}, u32[]{:S(2)}) collective-permute-start(bf16[128,1024]{1,0:T(8,128)(2,1)} %get-tuple-element.14), channel_id=1, source_target_pairs={{0,256},{256,0},{1,257},{257,1},{2,258},{258,2},{3,259},{259,3},{4... | collective-permute-start | bytes 786440 | tf_op jit(solution)/shard_map/ppermute | solution.py:141
  78.3 7.8 %collective-permute-start.3 = (bf16[4,128,1280]{2,1,0:T(8,128)(2,1)S(1)}, bf16[4,128,1280]{2,1,0:T(8,128)(2,1)S(1)}, u32[]{:S(2)}, u32[]{:S(2)}) collective-permute-start(bf16[4,128,1280]{2,1,0:T(8,128)(2,1)S(1)} %all-to-all-done.1.same), channel_id=1, source_target_pairs={{0,32},{32,0},{1,33},{33,1},{2,34},{34,2},{3,35},{35,3},{4,36},{36... | collective-permute-start | bytes 3932168 | tf_op jit(solution)/shard_map/ppermute | solution.py:153
  84.6 0.7 copy-start.9
  85.3 0.8 copy-start.4
  86.8 0.8 copy-start.2
  87.6 22.9 %all-to-all-start.2 = ((f32[4,32,1024]{2,1,0:T(8,128)}), f32[4,32,1024]{2,1,0:T(8,128)}, u32[]{:S(2)}, u32[]{:S(2)}) async-start(f32[4,32,1024]{2,1,0:T(8,128)} %bitcast.4), calls=%async_computation.2 | async-start | bytes 1048576 | tf_op jit(solution)/shard_map/all_to_all | solution.py:197
  91.8 10.8 %collective-permute-start.4 = (bf16[128,1024]{1,0:T(8,128)(2,1)}, bf16[128,1024]{1,0:T(8,128)(2,1)S(1)}, u32[]{:S(2)}, u32[]{:S(2)}) collective-permute-start(bf16[128,1024]{1,0:T(8,128)(2,1)} %copy-done.9), channel_id=1, source_target_pairs={{0,64},{64,128},{128,192},{192,0},{1,65},{65,129},{129,193},{193,1... | collective-permute-start | bytes 786440 | tf_op jit(solution)/shard_map/ppermute | solution.py:198
  94.0 13.4 %collective-permute-start.5 = (bf16[128,1024]{1,0:T(8,128)(2,1)}, bf16[128,1024]{1,0:T(8,128)(2,1)}, u32[]{:S(2)}, u32[]{:S(2)}) collective-permute-start(bf16[128,1024]{1,0:T(8,128)(2,1)} %copy-done.9), channel_id=1, source_target_pairs={{0,128},{64,192},{128,0},{192,64},{1,129},{65,193},{129,1},{193,65... | collective-permute-start | bytes 786440 | tf_op jit(solution)/shard_map/ppermute | solution.py:198
  97.7 12.8 %collective-permute-start.6 = (bf16[128,1024]{1,0:T(8,128)(2,1)}, bf16[128,1024]{1,0:T(8,128)(2,1)}, u32[]{:S(2)}, u32[]{:S(2)}) collective-permute-start(bf16[128,1024]{1,0:T(8,128)(2,1)} %copy-done.9), channel_id=1, source_target_pairs={{0,192},{64,0},{128,64},{192,128},{1,193},{65,1},{129,65},{193,129... | collective-permute-start | bytes 786440 | tf_op jit(solution)/shard_map/ppermute | solution.py:198
  112.2 43.9 %all-to-all-start.3 = ((bf16[16,4,1024]{2,1,0:T(4,128)(2,1)}), bf16[16,4,1024]{2,1,0:T(4,128)(2,1)S(1)}, u32[]{:S(2)}, u32[]{:S(2)}) async-start(bf16[16,4,1024]{2,1,0:T(4,128)(2,1)} %shard_map.94), calls=%async_computation.3 | async-start | bytes 262144 | tf_op jit(solution)/shard_map/all_to_all | solution.py:201
  144.2 23.2 %collective-permute-start.7 = (bf16[128,1024]{1,0:T(8,128)(2,1)}, bf16[128,1024]{1,0:T(8,128)(2,1)}, u32[]{:S(2)}, u32[]{:S(2)}) collective-permute-start(bf16[128,1024]{1,0:T(8,128)(2,1)} %copy-done.9), channel_id=1, source_target_pairs={{0,32},{32,0},{1,33},{33,1},{2,34},{34,2},{3,35},{35,3},{4,36},{36... | collective-permute-start | bytes 786440 | tf_op jit(solution)/shard_map/ppermute | solution.py:153
  148.5 18.8 %collective-permute-start.10 = (bf16[128,1024]{1,0:T(8,128)(2,1)}, bf16[128,1024]{1,0:T(8,128)(2,1)}, u32[]{:S(2)}, u32[]{:S(2)}) collective-permute-start(bf16[128,1024]{1,0:T(8,128)(2,1)} %collective-permute-done.6.refs_2_), channel_id=1, source_target_pairs={{0,32},{32,0},{1,33},{33,1},{2,34},{34,2},{3,35},{35,3},{4,36},{36... | collective-permute-start | bytes 786440 | tf_op jit(solution)/shard_map/ppermute | solution.py:153
  150.5 16.9 %collective-permute-start.8 = (bf16[128,1024]{1,0:T(8,128)(2,1)S(1)}, bf16[128,1024]{1,0:T(8,128)(2,1)}, u32[]{:S(2)}, u32[]{:S(2)}) collective-permute-start(bf16[128,1024]{1,0:T(8,128)(2,1)S(1)} %collective-permute-done.4.refs_0_), channel_id=1, source_target_pairs={{0,32},{32,0},{1,33},{33,1},{2,34},{34,2},{3,35},{35,3},{4,36},{36... | collective-permute-start | bytes 786440 | tf_op jit(solution)/shard_map/ppermute | solution.py:153
  152.9 14.5 %collective-permute-start.9 = (bf16[128,1024]{1,0:T(8,128)(2,1)}, bf16[128,1024]{1,0:T(8,128)(2,1)}, u32[]{:S(2)}, u32[]{:S(2)}) collective-permute-start(bf16[128,1024]{1,0:T(8,128)(2,1)} %collective-permute-done.5.refs_1_), channel_id=1, source_target_pairs={{0,32},{32,0},{1,33},{33,1},{2,34},{34,2},{3,35},{35,3},{4,36},{36... | collective-permute-start | bytes 786440 | tf_op jit(solution)/shard_map/ppermute | solution.py:153
  156.8 14.9 %all-to-all-start.4 = ((f32[8,4,1024]{2,1,0:T(4,128)}), f32[8,4,1024]{2,1,0:T(4,128)S(1)}, u32[]{:S(2)}, u32[]{:S(2)}) async-start(f32[8,4,1024]{2,1,0:T(4,128)} %shard_map.95), calls=%async_computation.4 | async-start | bytes 262144 | tf_op jit(solution)/shard_map/all_to_all | solution.py:205
  165.6 1.0 copy-start.5
  166.6 1.6 copy-start.1

commit v8 on v4

--- a/solution.py
+++ b/solution.py
@@ -57,11 +57,16 @@
         message[y, :, 1024:1280] = factor[:, 256 * y : 256 * y + 256]
 
 
-def prepare_body(place, codes, count, values, features, message, tile):
+def prepare_body(place, codes, count, values_hbm, features, message, tile, values, sems):
+    copies = [pltpu.make_async_copy(values_hbm.at[0], values, sems.at[4])]
+    for y in range(4):
+        copies.append(pltpu.make_async_copy(features, message.at[y, :, COLS], sems.at[y]))
+    for copy in copies:
+        copy.start()
     tile[...] = jnp.zeros(tile.shape, BF16)
     for y in range(4):
-        message[y, :, COLS] = features[...]
         message[y, :, 1024:1280] = jnp.zeros((128, 256), BF16)
+    copies[0].wait()
 
     def slot(k, carry):
         grid_row = lax.div(lax.rem(codes[0, k], 512), 32)
@@ -70,15 +75,17 @@
 
         @pl.when(own)
         def _():
-            tile[:, pl.ds(pl.multiple_of(512 * other + 128 * y, 128), 128)] = values[0, k]
+            tile[:, pl.ds(pl.multiple_of(512 * other + 128 * y, 128), 128)] = values[k]
 
         @pl.when(jnp.logical_not(own))
         def _():
-            message[y, :, pl.ds(pl.multiple_of(1024 + 128 * other, 128), 128)] = values[0, k]
+            message[y, :, pl.ds(pl.multiple_of(1024 + 128 * other, 128), 128)] = values[k]
 
         return carry
 
     lax.fori_loop(0, count[0], slot, 0)
+    for copy in copies[1:]:
+        copy.wait()
 
 
 def grouped(same, other):
@@ -159,9 +166,19 @@
     rows_f32, rows_bf16 = shape(128, hidden), shape(128, hidden, dtype=BF16)
     message_shape = shape(4, 128, hidden + 256, dtype=BF16)
 
-    message, tile = call(
-        prepare_body, (message_shape, shape(128, 1024, dtype=BF16)),
-        jnp.stack([zh, core]), block_codes, block_count, block_values, features,
+    message, tile = pl.pallas_call(
+        prepare_body,
+        out_shape=(message_shape, shape(128, 1024, dtype=BF16)),
+        in_specs=[SMEM] * 3 + [pl.BlockSpec(memory_space=pltpu.MemorySpace.HBM)] * 2,
+        out_specs=(VMEM, VMEM),
+        scratch_shapes=[
+            pltpu.VMEM(block_values.shape[1:], BF16), pltpu.SemaphoreType.DMA((5,)),
+        ],
+        compiler_params=pltpu.CompilerParams(vmem_limit_bytes=16 * 2**20),
+    )(
+        jnp.stack([zh, core]), block_codes, block_count,
+        pltpu.with_memory_space_constraint(block_values, pltpu.MemorySpace.HBM),
+        pltpu.with_memory_space_constraint(features, pltpu.MemorySpace.HBM),
     )
     same = over_y(message)
     other = other_core(same)
@@ -176,11 +193,12 @@
     other = other_core(same)
     partial = call(partial_body, rows_f32, same, other)
     part = lax.all_to_all(partial.reshape(4, 32, hidden), "x", 0, 0)
-    far = partner(call(far_body, rows_bf16, mirror, same, other))
-    part = call(sum_x_body, shape(16, 4, hidden, dtype=BF16), part)
+    far = call(far_body, rows_bf16, mirror, same, other)
+    part = call(sum_x_body, shape(16, 4, hidden, dtype=BF16), after(part, far))
     part = lax.all_to_all(part, ("zh", "zl"), 0, 0)
-    input_grad = call(backward_body, rows_f32, tile, same, other, far, weight, flops=10**11)
-    part = call(sum_z_body, shape(8, 4, hidden), after(part, input_grad))
+    far = partner(far)
+    input_grad = call(backward_body, rows_f32, tile, same, other, far, weight)
+    part = call(sum_z_body, shape(8, 4, hidden), part)
     part = lax.all_to_all(part, ("y", "co"), 0, 0)
     weight_grad = part.reshape(32, hidden)
     return output, input_grad, weight_grad

time: 154 us -> 170 us (1.10)
  starting transfers between devices: 65.7 us -> 78.1 us
  waiting for transfers between devices: 23.3 us -> 35 us
  blocking collectives: 46.6 us -> 37.4 us
    ppermute x2, waiting for transfers between devices: 4.75 us -> 23.2 us  [partner(): return lax.ppermute(rows, 'zh', SWAP)]
    all_to_all x1, waiting for transfers between devices: 13.3 us -> 0.01 us  [local(): part = lax.all_to_all(part, ('zh', 'zl'), 0, 0)]
    all_to_all x1 -> x0, blocking collectives: 8.97 us -> none  [local(): part = lax.all_to_all(part, ('y', 'co'), 0, 0)]
    all_to_all x0 -> x1, starting transfers between devices: none -> 7.77 us  [local(): part = lax.all_to_all(part, ('y', 'co'), 0, 0)]
    all_to_all x1, waiting for transfers between devices: 0.01 us -> 6.51 us  [local(): part = lax.all_to_all(partial.reshape(4, 32, hidden), 'x', 0, 0)]
    all_to_all x1, starting transfers between devices: 23.3 us -> 27.6 us  [local(): part = lax.all_to_all(part, ('zh', 'zl'), 0, 0)]
    pallas_call x0 -> x1, Pallas kernels: none -> 2.12 us  [local(): pl.pallas_call(prepare_body, out_shape=(message_shape, shape(128, 1024, d...]
    pallas_call x9 -> x8, Pallas kernels: 9 us -> 8.09 us  [call(): pl.pallas_call(body, out_shape=outs, in_specs=[SMEM if a.dtype == jnp.int...]
  transfers between devices with their start and end apart: 6 -> 7, of which waited for: 4 -> 5; matrix products, arithmetic and copies ran while one was open for 1% -> 1% of each run, Pallas kernels for 3% -> 3%
where the time goes in v8:
time: 170 us; the launch traced here: 169 us
  starting transfers between devices  78.1 us (46%)
  blocking collectives  37.4 us (22%)
  waiting for transfers between devices  35 us (21%)
  Pallas kernels  10.2 us (6%)
  local copies, waits for them, and re-layouts  6.08 us (4%)
    all_to_all x2, blocking collectives, over_y(): return lax.all_to_all(message, 'y', 0, 0)  37.4 us
    all_to_all x1, starting transfers between devices, local(): part = lax.all_to_all(part, ('zh', 'zl'), 0, 0)  27.6 us
    ppermute x2, starting transfers between devices, partner(): return lax.ppermute(rows, 'zh', SWAP)  27.4 us
    ppermute x2, waiting for transfers between devices, partner(): return lax.ppermute(rows, 'zh', SWAP)  23.2 us
    ppermute x2, starting transfers between devices, other_core(): return lax.ppermute(rows, 'co', SWAP)  11.3 us
    pallas_call x8, Pallas kernels, call(): pl.pallas_call(body, out_shape=outs, in_specs=[SMEM if a.dtype == jnp.int...  8.09 us
    all_to_all x1, starting transfers between devices, local(): part = lax.all_to_all(part, ('y', 'co'), 0, 0)  7.77 us
    all_to_all x1, waiting for transfers between devices, local(): part = lax.all_to_all(partial.reshape(4, 32, hidden), 'x', 0, 0)  6.51 us
  transfers between devices with their start and end apart: 7, of which 5 were waited for; matrix products, arithmetic and copies ran while one was open for 1% of the time, Pallas kernels for 3%

profile of v8, /device:TPU:1, one launch (start us, length us, event | category | flops | bytes accessed | tf_op | source)
XLA Modules:
  0.0 169.2 jit_solution(16663777544363246288)
XLA Ops:
  1.3 0.1 pad_add_fusion.place
  1.4 0.7 copy-done.7
  2.0 2.1 %shard_map.85 = (bf16[4,128,1280]{2,1,0:T(8,128)(2,1)S(1)}, bf16[128,1024]{1,0:T(8,128)(2,1)S(1)}) custom-call(s32[2]{0:T(128)S(1)} %pad_add_fusion.place, s32[1,16]{1,0:T(1,128)S(1)} %copy-done.7, s32[1]{0:T(128)S(6)} %copy.9.count, bf16[1,16,128,128]{3,2,1,0:T(8,128)(2,1)} %values_hbm.1, bf16[128,1024]{1,0:T(8,128)(2,1)} %features.1), custom_call_target="tpu_custom_call" | custom-call | tf_op jit(solution)/shard_map/pallas_call | solution.py:169
  4.1 18.3 %all_to_all.25.same = bf16[4,128,1280]{2,1,0:T(8,128)(2,1)S(1)} all-to-all(bf16[4,128,1280]{2,1,0:T(8,128)(2,1)S(1)} %get-tuple-element.11), channel_id=1, replica_groups=mesh['zh'=2,'y'=4,'co'=2,'x'=4,'zl'=8] {'y'}, dimensions={0} | all-to-all | bytes 2621440 | tf_op jit(solution)/shard_map/all_to_all | solution.py:148
  22.4 7.3 %collective-permute-start = (bf16[4,128,1280]{2,1,0:T(8,128)(2,1)S(1)}, bf16[4,128,1280]{2,1,0:T(8,128)(2,1)S(1)}, u32[]{:S(2)}, u32[]{:S(2)}) collective-permute-start(bf16[4,128,1280]{2,1,0:T(8,128)(2,1)S(1)} %all_to_all.25.same), channel_id=1, source_target_pairs={{0,32},{32,0},{1,33},{33,1},{2,34},{34,2},{3,35},{35,3},{4,36},{36... | collective-permute-start | bytes 3932168 | tf_op jit(solution)/shard_map/ppermute | solution.py:152
  29.7 2.6 %collective-permute-done.other = bf16[4,128,1280]{2,1,0:T(8,128)(2,1)S(1)} collective-permute-done((bf16[4,128,1280]{2,1,0:T(8,128)(2,1)S(1)}, bf16[4,128,1280]{2,1,0:T(8,128)(2,1)S(1)}, u32[]{:S(2)}, u32[]{:S(2)}) %collective-permute-start) | collective-permute-done | bytes 1310752 | tf_op jit(solution)/shard_map/ppermute | solution.py:152
  32.4 0.7 shard_map.87
  33.1 0.7 copy-done.4
  33.8 15.4 %collective-permute-start.1 = (bf16[128,1024]{1,0:T(8,128)(2,1)S(1)}, bf16[128,1024]{1,0:T(8,128)(2,1)S(1)}, u32[]{:S(2)}, u32[]{:S(2)}) collective-permute-start(bf16[128,1024]{1,0:T(8,128)(2,1)S(1)} %get-tuple-element.12), channel_id=1, source_target_pairs={{0,256},{256,0},{1,257},{257,1},{2,258},{258,2},{3,259},{259,3},{4... | collective-permute-start | bytes 786440 | tf_op jit(solution)/shard_map/ppermute | solution.py:140
  49.2 0.9 fusion.regroup
  50.1 0.7 shard_map.86.near
  50.8 4.8 %collective-permute-done.1.far = bf16[128,1024]{1,0:T(8,128)(2,1)S(1)} collective-permute-done((bf16[128,1024]{1,0:T(8,128)(2,1)S(1)}, bf16[128,1024]{1,0:T(8,128)(2,1)S(1)}, u32[]{:S(2)}, u32[]{:S(2)}) %collective-permute-start.1) | collective-permute-done | bytes 262176 | tf_op jit(solution)/shard_map/ppermute | solution.py:140
  55.6 1.7 %shard_map.88 = (f32[128,1024]{1,0:T(8,128)}, bf16[4,128,1280]{2,1,0:T(8,128)(2,1)S(1)}) custom-call(f32[128,1024]{1,0:T(8,128)S(1)} %shard_map.86.near, bf16[128,1024]{1,0:T(8,128)(2,1)S(1)} %collective-permute-done.1.far, bf16[1024,1024]{1,0:T(8,128)(2,1)S(1)} %copy-done, bf16[128,1024]{1,0:T(8,128)(2,1)S(1)} %copy-done.3, bf16[1024,1024]{1,0:T(8,128)(2,1)S(1)} %fusion.regroup), custom_call_target="tpu_custom_call" | custom-call | flops 1 | bytes 1 | tf_op jit(solution)/shard_map/pallas_call | solution.py:22
  57.3 19.2 %all_to_all.26.same = bf16[4,128,1280]{2,1,0:T(8,128)(2,1)S(1)} all-to-all(bf16[4,128,1280]{2,1,0:T(8,128)(2,1)S(1)} %get-tuple-element.14), channel_id=1, replica_groups=mesh['zh'=2,'y'=4,'co'=2,'x'=4,'zl'=8] {'y'}, dimensions={0} | all-to-all | bytes 2621440 | tf_op jit(solution)/shard_map/all_to_all | solution.py:148
  76.5 4.0 %collective-permute-start.2 = (bf16[4,128,1280]{2,1,0:T(8,128)(2,1)S(1)}, bf16[4,128,1280]{2,1,0:T(8,128)(2,1)S(1)}, u32[]{:S(2)}, u32[]{:S(2)}) collective-permute-start(bf16[4,128,1280]{2,1,0:T(8,128)(2,1)S(1)} %all_to_all.26.same), channel_id=1, source_target_pairs={{0,32},{32,0},{1,33},{33,1},{2,34},{34,2},{3,35},{35,3},{4,36},{36... | collective-permute-start | bytes 3932168 | tf_op jit(solution)/shard_map/ppermute | solution.py:152
  80.5 2.6 %collective-permute-done.2.other = bf16[4,128,1280]{2,1,0:T(8,128)(2,1)S(1)} collective-permute-done((bf16[4,128,1280]{2,1,0:T(8,128)(2,1)S(1)}, bf16[4,128,1280]{2,1,0:T(8,128)(2,1)S(1)}, u32[]{:S(2)}, u32[]{:S(2)}) %collective-permute-start.2) | collective-permute-done | bytes 1310752 | tf_op jit(solution)/shard_map/ppermute | solution.py:152
  83.1 0.7 shard_map.91
  83.9 0.8 copy-done.2
  84.7 4.0 %all-to-all-start.2 = ((f32[4,32,1024]{2,1,0:T(8,128)}), f32[4,32,1024]{2,1,0:T(8,128)S(1)}, u32[]{:S(2)}, u32[]{:S(2)}) async-start(f32[4,32,1024]{2,1,0:T(8,128)} %bitcast.3), calls=%async_computation.2 | async-start | bytes 1048576 | tf_op jit(solution)/shard_map/all_to_all | solution.py:195
  88.6 0.9 copy-done.5
  89.6 0.7 shard_map.89
  90.3 0.7 copy-done.6
  91.0 6.5 %all-to-all-done.2.pieces = f32[4,32,1024]{2,1,0:T(8,128)S(1)} async-done(((f32[4,32,1024]{2,1,0:T(8,128)}), f32[4,32,1024]{2,1,0:T(8,128)S(1)}, u32[]{:S(2)}, u32[]{:S(2)}) %all-to-all-start.2) | async-done | bytes 524320 | tf_op jit(solution)/shard_map/all_to_all | solution.py:195
  97.5 0.7 shard_map.92
  98.2 27.6 %all-to-all-start.3 = ((bf16[16,4,1024]{2,1,0:T(4,128)(2,1)}), bf16[16,4,1024]{2,1,0:T(4,128)(2,1)S(1)}, u32[]{:S(2)}, u32[]{:S(2)}) async-start(bf16[16,4,1024]{2,1,0:T(4,128)(2,1)} %shard_map.92), calls=%async_computation.3 | async-start | bytes 262144 | tf_op jit(solution)/shard_map/all_to_all | solution.py:198
  125.8 12.0 %collective-permute-start.3 = (bf16[128,1024]{1,0:T(8,128)(2,1)}, bf16[128,1024]{1,0:T(8,128)(2,1)S(1)}, u32[]{:S(2)}, u32[]{:S(2)}) collective-permute-start(bf16[128,1024]{1,0:T(8,128)(2,1)} %copy-done.6), channel_id=1, source_target_pairs={{0,256},{256,0},{1,257},{257,1},{2,258},{258,2},{3,259},{259,3},{4... | collective-permute-start | bytes 786440 | tf_op jit(solution)/shard_map/ppermute | solution.py:140
  137.8 0.7 shard_map.93
  138.5 7.8 %all-to-all-start.4 = ((f32[8,4,1024]{2,1,0:T(4,128)}), f32[8,4,1024]{2,1,0:T(4,128)S(1)}, u32[]{:S(2)}, u32[]{:S(2)}) async-start(f32[8,4,1024]{2,1,0:T(4,128)} %shard_map.93), calls=%async_computation.4 | async-start | bytes 262144 | tf_op jit(solution)/shard_map/all_to_all | solution.py:202
  146.3 18.4 %collective-permute-done.3.far = bf16[128,1024]{1,0:T(8,128)(2,1)S(1)} collective-permute-done((bf16[128,1024]{1,0:T(8,128)(2,1)}, bf16[128,1024]{1,0:T(8,128)(2,1)S(1)}, u32[]{:S(2)}, u32[]{:S(2)}) %collective-permute-start.3) | collective-permute-done | bytes 262176 | tf_op jit(solution)/shard_map/ppermute | solution.py:140
  164.7 1.6 copy-done.1
  166.3 2.2 %shard_map.90 = f32[128,1024]{1,0:T(8,128)} custom-call(bf16[128,1024]{1,0:T(8,128)(2,1)S(1)} %get-tuple-element.10.tile, bf16[4,128,1280]{2,1,0:T(8,128)(2,1)S(1)} %all_to_all.26.same, bf16[4,128,1280]{2,1,0:T(8,128)(2,1)S(1)} %collective-permute-done.2.other, bf16[128,1024]{1,0:T(8,128)(2,1)S(1)} %collective-permute-done.3.far, ...), custom_call_target="tpu_custom_call" | custom-call | flops 1 | bytes 1 | tf_op jit(solution)/shard_map/pallas_call | solution.py:22
  168.5 0.7 reshape.78
  (13 shorter events, 0.0 us)
Async XLA Ops:
  1.4 0.7 copy-start.7
  22.4 10.0 %collective-permute-start = (bf16[4,128,1280]{2,1,0:T(8,128)(2,1)S(1)}, bf16[4,128,1280]{2,1,0:T(8,128)(2,1)S(1)}, u32[]{:S(2)}, u32[]{:S(2)}) collective-permute-start(bf16[4,128,1280]{2,1,0:T(8,128)(2,1)S(1)} %all_to_all.25.same), channel_id=1, source_target_pairs={{0,32},{32,0},{1,33},{33,1},{2,34},{34,2},{3,35},{35,3},{4,36},{36... | collective-permute-start | bytes 3932168 | tf_op jit(solution)/shard_map/ppermute | solution.py:152
  33.1 0.7 copy-start.4
  33.8 21.8 %collective-permute-start.1 = (bf16[128,1024]{1,0:T(8,128)(2,1)S(1)}, bf16[128,1024]{1,0:T(8,128)(2,1)S(1)}, u32[]{:S(2)}, u32[]{:S(2)}) collective-permute-start(bf16[128,1024]{1,0:T(8,128)(2,1)S(1)} %get-tuple-element.12), channel_id=1, source_target_pairs={{0,256},{256,0},{1,257},{257,1},{2,258},{258,2},{3,259},{259,3},{4... | collective-permute-start | bytes 786440 | tf_op jit(solution)/shard_map/ppermute | solution.py:140
  50.1 5.5 %copy-start = (bf16[1024,1024]{1,0:T(8,128)(2,1)S(1)}, bf16[1024,1024]{1,0:T(8,128)(2,1)}, u32[]{:S(2)}) copy-start(bf16[1024,1024]{1,0:T(8,128)(2,1)} %weight.3) | copy-start | bytes 6291460
  50.1 5.5 %copy-start.3 = (bf16[128,1024]{1,0:T(8,128)(2,1)S(1)}, bf16[128,1024]{1,0:T(8,128)(2,1)}, u32[]{:S(2)}) copy-start(bf16[128,1024]{1,0:T(8,128)(2,1)} %cotangent.1) | copy-start | bytes 786436
  76.5 6.6 %collective-permute-start.2 = (bf16[4,128,1280]{2,1,0:T(8,128)(2,1)S(1)}, bf16[4,128,1280]{2,1,0:T(8,128)(2,1)S(1)}, u32[]{:S(2)}, u32[]{:S(2)}) collective-permute-start(bf16[4,128,1280]{2,1,0:T(8,128)(2,1)S(1)} %all_to_all.26.same), channel_id=1, source_target_pairs={{0,32},{32,0},{1,33},{33,1},{2,34},{34,2},{3,35},{35,3},{4,36},{36... | collective-permute-start | bytes 3932168 | tf_op jit(solution)/shard_map/ppermute | solution.py:152
  83.9 0.8 copy-start.2
  84.7 12.9 %all-to-all-start.2 = ((f32[4,32,1024]{2,1,0:T(8,128)}), f32[4,32,1024]{2,1,0:T(8,128)S(1)}, u32[]{:S(2)}, u32[]{:S(2)}) async-start(f32[4,32,1024]{2,1,0:T(8,128)} %bitcast.3), calls=%async_computation.2 | async-start | bytes 1048576 | tf_op jit(solution)/shard_map/all_to_all | solution.py:195
  88.6 0.9 copy-start.5
  90.3 0.7 copy-start.6
  98.2 39.6 %all-to-all-start.3 = ((bf16[16,4,1024]{2,1,0:T(4,128)(2,1)}), bf16[16,4,1024]{2,1,0:T(4,128)(2,1)S(1)}, u32[]{:S(2)}, u32[]{:S(2)}) async-start(bf16[16,4,1024]{2,1,0:T(4,128)(2,1)} %shard_map.92), calls=%async_computation.3 | async-start | bytes 262144 | tf_op jit(solution)/shard_map/all_to_all | solution.py:198
  125.8 38.9 %collective-permute-start.3 = (bf16[128,1024]{1,0:T(8,128)(2,1)}, bf16[128,1024]{1,0:T(8,128)(2,1)S(1)}, u32[]{:S(2)}, u32[]{:S(2)}) collective-permute-start(bf16[128,1024]{1,0:T(8,128)(2,1)} %copy-done.6), channel_id=1, source_target_pairs={{0,256},{256,0},{1,257},{257,1},{2,258},{258,2},{3,259},{259,3},{4... | collective-permute-start | bytes 786440 | tf_op jit(solution)/shard_map/ppermute | solution.py:140
  138.5 30.0 %all-to-all-start.4 = ((f32[8,4,1024]{2,1,0:T(4,128)}), f32[8,4,1024]{2,1,0:T(4,128)S(1)}, u32[]{:S(2)}, u32[]{:S(2)}) async-start(f32[8,4,1024]{2,1,0:T(4,128)} %shard_map.93), calls=%async_computation.4 | async-start | bytes 262144 | tf_op jit(solution)/shard_map/all_to_all | solution.py:202
  164.7 1.6 copy-start.1

commit v9 on v8

--- a/solution.py
+++ b/solution.py
@@ -10,6 +10,7 @@
 BF16, F32 = jnp.bfloat16, jnp.float32
 SWAP = [(0, 1), (1, 0)]
 VMEM = pl.BlockSpec(memory_space=pltpu.VMEM)
+HBM = pl.BlockSpec(memory_space=pltpu.MemorySpace.HBM)
 SMEM = pl.BlockSpec(memory_space=pltpu.SMEM)
 COLS = slice(0, 1024)
 
@@ -57,8 +58,11 @@
         message[y, :, 1024:1280] = factor[:, 256 * y : 256 * y + 256]
 
 
-def prepare_body(place, codes, count, values_hbm, features, message, tile, values, sems):
-    copies = [pltpu.make_async_copy(values_hbm.at[0], values, sems.at[4])]
+def prepare_body(place, count, codes_hbm, values_hbm, features, message, tile, codes, values, sems):
+    copies = [
+        pltpu.make_async_copy(codes_hbm, codes, sems.at[5]),
+        pltpu.make_async_copy(values_hbm.at[0], values, sems.at[4]),
+    ]
     for y in range(4):
         copies.append(pltpu.make_async_copy(features, message.at[y, :, COLS], sems.at[y]))
     for copy in copies:
@@ -67,6 +71,7 @@
     for y in range(4):
         message[y, :, 1024:1280] = jnp.zeros((128, 256), BF16)
     copies[0].wait()
+    copies[1].wait()
 
     def slot(k, carry):
         grid_row = lax.div(lax.rem(codes[0, k], 512), 32)
@@ -84,7 +89,7 @@
         return carry
 
     lax.fori_loop(0, count[0], slot, 0)
-    for copy in copies[1:]:
+    for copy in copies[2:]:
         copy.wait()
 
 
@@ -103,16 +108,19 @@
         mirror[y + 4] = other[y, :, 1152:1280]
 
 
-def far_body(mirror, same, other, far):
-    total = 0.0
-    for y in range(4):
-        total += dot(mirror[y], same[y, :, COLS], 0, 0)
-        total += dot(mirror[y + 4], other[y, :, COLS], 0, 0)
-    far[...] = total.astype(BF16)
-
-
-def partial_body(same, other, partial):
+def sums_body(mirror, same, other, far_hbm, partial_hbm, far, partial, sems):
+    far_here = 0.0
+    for y in range(4):
+        far_here += dot(mirror[y], same[y, :, COLS], 0, 0)
+        far_here += dot(mirror[y + 4], other[y, :, COLS], 0, 0)
+    far[...] = far_here.astype(BF16)
+    far_copy = pltpu.make_async_copy(far, far_hbm, sems.at[0])
+    far_copy.start()
     partial[...] = grouped(same, other)
+    partial_copy = pltpu.make_async_copy(partial, partial_hbm, sems.at[1])
+    partial_copy.start()
+    far_copy.wait()
+    partial_copy.wait()
 
 
 def sum_x_body(pieces, out):
@@ -169,16 +177,20 @@
     message, tile = pl.pallas_call(
         prepare_body,
         out_shape=(message_shape, shape(128, 1024, dtype=BF16)),
-        in_specs=[SMEM] * 3 + [pl.BlockSpec(memory_space=pltpu.MemorySpace.HBM)] * 2,
+        in_specs=[SMEM] * 2 + [HBM] * 3,
         out_specs=(VMEM, VMEM),
         scratch_shapes=[
-            pltpu.VMEM(block_values.shape[1:], BF16), pltpu.SemaphoreType.DMA((5,)),
+            pltpu.SMEM(block_codes.shape, jnp.int32),
+            pltpu.VMEM(block_values.shape[1:], BF16),
+            pltpu.SemaphoreType.DMA((6,)),
         ],
         compiler_params=pltpu.CompilerParams(vmem_limit_bytes=16 * 2**20),
     )(
-        jnp.stack([zh, core]), block_codes, block_count,
-        pltpu.with_memory_space_constraint(block_values, pltpu.MemorySpace.HBM),
-        pltpu.with_memory_space_constraint(features, pltpu.MemorySpace.HBM),
+        jnp.stack([zh, core]), block_count,
+        *(
+            pltpu.with_memory_space_constraint(a, pltpu.MemorySpace.HBM)
+            for a in (block_codes, block_values, features)
+        ),
     )
     same = over_y(message)
     other = other_core(same)
@@ -191,14 +203,27 @@
 
     same = over_y(message)
     other = other_core(same)
-    partial = call(partial_body, rows_f32, same, other)
+    far, partial = pl.pallas_call(
+        sums_body,
+        out_shape=(
+            pltpu.HBM(rows_bf16.shape, BF16), pltpu.HBM(rows_f32.shape, F32),
+        ),
+        in_specs=[VMEM] * 3,
+        out_specs=(HBM, HBM),
+        scratch_shapes=[
+            pltpu.VMEM(rows_bf16.shape, BF16),
+            pltpu.VMEM(rows_f32.shape, F32),
+            pltpu.SemaphoreType.DMA((2,)),
+        ],
+        compiler_params=pltpu.CompilerParams(vmem_limit_bytes=16 * 2**20),
+        cost_estimate=pl.CostEstimate(flops=1, bytes_accessed=1, transcendentals=0),
+    )(mirror, same, other)
     part = lax.all_to_all(partial.reshape(4, 32, hidden), "x", 0, 0)
-    far = call(far_body, rows_bf16, mirror, same, other)
-    part = call(sum_x_body, shape(16, 4, hidden, dtype=BF16), after(part, far))
+    far = partner(far)
+    part = call(sum_x_body, shape(16, 4, hidden, dtype=BF16), part)
     part = lax.all_to_all(part, ("zh", "zl"), 0, 0)
-    far = partner(far)
-    input_grad = call(backward_body, rows_f32, tile, same, other, far, weight)
-    part = call(sum_z_body, shape(8, 4, hidden), part)
+    input_grad = call(backward_body, rows_f32, tile, same, other, far, weight, flops=10**11)
+    part = call(sum_z_body, shape(8, 4, hidden), after(part, input_grad))
     part = lax.all_to_all(part, ("y", "co"), 0, 0)
     weight_grad = part.reshape(32, hidden)
     return output, input_grad, weight_grad

time: 170 us -> 152 us (0.89)
  waiting for transfers between devices: 35 us -> 21.7 us
  starting transfers between devices: 78.1 us -> 67.2 us
  blocking collectives: 37.4 us -> 46.6 us
  local copies, waits for them, and re-layouts: 6.08 us -> 2.3 us
    ppermute x2, waiting for transfers between devices: 23.2 us -> 4.76 us  [partner(): return lax.ppermute(rows, 'zh', SWAP)]
    all_to_all x1, waiting for transfers between devices: 0.01 us -> 11.6 us  [local(): part = lax.all_to_all(part, ('zh', 'zl'), 0, 0)]
    all_to_all x0 -> x1, blocking collectives: none -> 9.18 us  [local(): part = lax.all_to_all(part, ('y', 'co'), 0, 0)]
    all_to_all x1 -> x0, starting transfers between devices: 7.77 us -> none  [local(): part = lax.all_to_all(part, ('y', 'co'), 0, 0)]
    all_to_all x1, waiting for transfers between devices: 6.51 us -> 0.01 us  [local(): part = lax.all_to_all(partial.reshape(4, 32, hidden), 'x', 0, 0)]
    unnamed x16 -> x6, local copies, waits for them, and re-layouts: 5.38 us -> 1.6 us
    all_to_all x1, starting transfers between devices: 27.6 us -> 24.7 us  [local(): part = lax.all_to_all(part, ('zh', 'zl'), 0, 0)]
    pallas_call x0 -> x1, Pallas kernels: none -> 2.08 us  [local(): pl.pallas_call(sums_body, out_shape=(pltpu.HBM(rows_bf16.shape, BF16), pl...]
  transfers between devices with their start and end apart: 7 -> 6, of which waited for: 5 -> 4; matrix products, arithmetic and copies ran while one was open for 1% -> 1% of each run, Pallas kernels for 3% -> 3%
where the time goes in v9:
time: 152 us; the launch traced here: 151 us
  starting transfers between devices  67.2 us (44%)
  blocking collectives  46.6 us (31%)
  waiting for transfers between devices  21.7 us (14%)
  Pallas kernels  11.1 us (7%)
  local copies, waits for them, and re-layouts  2.3 us (2%)
    all_to_all x2, blocking collectives, over_y(): return lax.all_to_all(message, 'y', 0, 0)  37.4 us
    ppermute x2, starting transfers between devices, partner(): return lax.ppermute(rows, 'zh', SWAP)  27.3 us
    all_to_all x1, starting transfers between devices, local(): part = lax.all_to_all(part, ('zh', 'zl'), 0, 0)  24.7 us
    all_to_all x1, waiting for transfers between devices, local(): part = lax.all_to_all(part, ('zh', 'zl'), 0, 0)  11.6 us
    ppermute x2, starting transfers between devices, other_core(): return lax.ppermute(rows, 'co', SWAP)  11.3 us
    all_to_all x1, blocking collectives, local(): part = lax.all_to_all(part, ('y', 'co'), 0, 0)  9.18 us
    pallas_call x6, Pallas kernels, call(): pl.pallas_call(body, out_shape=outs, in_specs=[SMEM if a.dtype == jnp.int...  6.91 us
    ppermute x2, waiting for transfers between devices, other_core(): return lax.ppermute(rows, 'co', SWAP)  5.26 us
  transfers between devices with their start and end apart: 6, of which 4 were waited for; matrix products, arithmetic and copies ran while one was open for 1% of the time, Pallas kernels for 3%

profile of v9, /device:TPU:1, one launch (start us, length us, event | category | flops | bytes accessed | tf_op | source)
XLA Modules:
  0.0 151.3 jit_solution(16953615785325927553)
XLA Ops:
  1.3 0.1 pad_add_fusion.place
  1.4 2.1 %shard_map.85 = (bf16[4,128,1280]{2,1,0:T(8,128)(2,1)S(1)}, bf16[128,1024]{1,0:T(8,128)(2,1)S(1)}) custom-call(s32[2]{0:T(128)S(1)} %pad_add_fusion.place, s32[1]{0:T(128)S(6)} %copy.9.count, s32[1,16]{1,0:T(1,128)} %codes_hbm.1, bf16[1,16,128,128]{3,2,1,0:T(8,128)(2,1)} %values_hbm.1, bf16[128,1024]{1,0:T(8,128)(2,1)} %features.1), custom_call_target="tpu_custom_call" | custom-call | tf_op jit(solution)/shard_map/pallas_call | solution.py:177
  3.5 18.3 %all_to_all.25.same = bf16[4,128,1280]{2,1,0:T(8,128)(2,1)S(1)} all-to-all(bf16[4,128,1280]{2,1,0:T(8,128)(2,1)S(1)} %get-tuple-element.13), channel_id=1, replica_groups=mesh['zh'=2,'y'=4,'co'=2,'x'=4,'zl'=8] {'y'}, dimensions={0} | all-to-all | bytes 2621440 | tf_op jit(solution)/shard_map/all_to_all | solution.py:156
  21.7 7.3 %collective-permute-start = (bf16[4,128,1280]{2,1,0:T(8,128)(2,1)S(1)}, bf16[4,128,1280]{2,1,0:T(8,128)(2,1)S(1)}, u32[]{:S(2)}, u32[]{:S(2)}) collective-permute-start(bf16[4,128,1280]{2,1,0:T(8,128)(2,1)S(1)} %all_to_all.25.same), channel_id=1, source_target_pairs={{0,32},{32,0},{1,33},{33,1},{2,34},{34,2},{3,35},{35,3},{4,36},{36... | collective-permute-start | bytes 3932168 | tf_op jit(solution)/shard_map/ppermute | solution.py:160
  29.1 2.6 %collective-permute-done.other = bf16[4,128,1280]{2,1,0:T(8,128)(2,1)S(1)} collective-permute-done((bf16[4,128,1280]{2,1,0:T(8,128)(2,1)S(1)}, bf16[4,128,1280]{2,1,0:T(8,128)(2,1)S(1)}, u32[]{:S(2)}, u32[]{:S(2)}) %collective-permute-start) | collective-permute-done | bytes 1310752 | tf_op jit(solution)/shard_map/ppermute | solution.py:160
  31.7 0.7 shard_map.87
  32.4 15.5 %collective-permute-start.1 = (bf16[128,1024]{1,0:T(8,128)(2,1)S(1)}, bf16[128,1024]{1,0:T(8,128)(2,1)S(1)}, u32[]{:S(2)}, u32[]{:S(2)}) collective-permute-start(bf16[128,1024]{1,0:T(8,128)(2,1)S(1)} %get-tuple-element.14), channel_id=1, source_target_pairs={{0,256},{256,0},{1,257},{257,1},{2,258},{258,2},{3,259},{259,3},{4... | collective-permute-start | bytes 786440 | tf_op jit(solution)/shard_map/ppermute | solution.py:148
  47.9 0.9 fusion.regroup
  48.8 0.0 copy-start
  48.8 0.0 copy-start.2
  48.8 0.7 shard_map.86.near
  49.5 4.8 %collective-permute-done.1.far = bf16[128,1024]{1,0:T(8,128)(2,1)S(1)} collective-permute-done((bf16[128,1024]{1,0:T(8,128)(2,1)S(1)}, bf16[128,1024]{1,0:T(8,128)(2,1)S(1)}, u32[]{:S(2)}, u32[]{:S(2)}) %collective-permute-start.1) | collective-permute-done | bytes 262176 | tf_op jit(solution)/shard_map/ppermute | solution.py:148
  54.3 0.0 copy-done
  54.3 0.0 copy-done.2
  54.3 1.7 %shard_map.88 = (f32[128,1024]{1,0:T(8,128)}, bf16[4,128,1280]{2,1,0:T(8,128)(2,1)S(1)}) custom-call(f32[128,1024]{1,0:T(8,128)S(1)} %shard_map.86.near, bf16[128,1024]{1,0:T(8,128)(2,1)S(1)} %collective-permute-done.1.far, bf16[1024,1024]{1,0:T(8,128)(2,1)S(1)} %copy-done, bf16[128,1024]{1,0:T(8,128)(2,1)S(1)} %copy-done.2, bf16[1024,1024]{1,0:T(8,128)(2,1)S(1)} %fusion.regroup), custom_call_target="tpu_custom_call" | custom-call | flops 1 | bytes 1 | tf_op jit(solution)/shard_map/pallas_call | solution.py:23
  55.9 19.2 %all_to_all.26.same = bf16[4,128,1280]{2,1,0:T(8,128)(2,1)S(1)} all-to-all(bf16[4,128,1280]{2,1,0:T(8,128)(2,1)S(1)} %get-tuple-element.16), channel_id=1, replica_groups=mesh['zh'=2,'y'=4,'co'=2,'x'=4,'zl'=8] {'y'}, dimensions={0} | all-to-all | bytes 2621440 | tf_op jit(solution)/shard_map/all_to_all | solution.py:156
  75.1 4.0 %collective-permute-start.2 = (bf16[4,128,1280]{2,1,0:T(8,128)(2,1)S(1)}, bf16[4,128,1280]{2,1,0:T(8,128)(2,1)S(1)}, u32[]{:S(2)}, u32[]{:S(2)}) collective-permute-start(bf16[4,128,1280]{2,1,0:T(8,128)(2,1)S(1)} %all_to_all.26.same), channel_id=1, source_target_pairs={{0,32},{32,0},{1,33},{33,1},{2,34},{34,2},{3,35},{35,3},{4,36},{36... | collective-permute-start | bytes 3932168 | tf_op jit(solution)/shard_map/ppermute | solution.py:160
  79.1 2.6 %collective-permute-done.2.other = bf16[4,128,1280]{2,1,0:T(8,128)(2,1)S(1)} collective-permute-done((bf16[4,128,1280]{2,1,0:T(8,128)(2,1)S(1)}, bf16[4,128,1280]{2,1,0:T(8,128)(2,1)S(1)}, u32[]{:S(2)}, u32[]{:S(2)}) %collective-permute-start.2) | collective-permute-done | bytes 1310752 | tf_op jit(solution)/shard_map/ppermute | solution.py:160
  81.8 2.1 %shard_map.89 = (bf16[128,1024]{1,0:T(8,128)(2,1)}, f32[128,1024]{1,0:T(8,128)}) custom-call(bf16[8,128,128]{2,1,0:T(8,128)(2,1)S(1)} %get-tuple-element.17.mirror, bf16[4,128,1280]{2,1,0:T(8,128)(2,1)S(1)} %all_to_all.26.same, bf16[4,128,1280]{2,1,0:T(8,128)(2,1)S(1)} %collective-permute-done.2.other), custom_call_target="tpu_custom_call" | custom-call | flops 1 | bytes 1 | tf_op jit(solution)/shard_map/pallas_call | solution.py:206
  83.8 4.0 %all-to-all-start.2 = ((f32[4,32,1024]{2,1,0:T(8,128)}), f32[4,32,1024]{2,1,0:T(8,128)S(1)}, u32[]{:S(2)}, u32[]{:S(2)}) async-start(f32[4,32,1024]{2,1,0:T(8,128)} %bitcast.3), calls=%async_computation.2 | async-start | bytes 1048576 | tf_op jit(solution)/shard_map/all_to_all | solution.py:221
  87.9 11.8 %collective-permute-start.3 = (bf16[128,1024]{1,0:T(8,128)(2,1)}, bf16[128,1024]{1,0:T(8,128)(2,1)}, u32[]{:S(2)}, u32[]{:S(2)}) collective-permute-start(bf16[128,1024]{1,0:T(8,128)(2,1)} %get-tuple-element.18), channel_id=1, source_target_pairs={{0,256},{256,0},{1,257},{257,1},{2,258},{258,2},{3,259},{259,3},{4... | collective-permute-start | bytes 786440 | tf_op jit(solution)/shard_map/ppermute | solution.py:148
  99.7 0.0 all-to-all-done.2.pieces
  99.7 0.7 shard_map.91
  100.4 24.7 %all-to-all-start.3 = ((bf16[16,4,1024]{2,1,0:T(4,128)(2,1)}), bf16[16,4,1024]{2,1,0:T(4,128)(2,1)S(1)}, u32[]{:S(2)}, u32[]{:S(2)}) async-start(bf16[16,4,1024]{2,1,0:T(4,128)(2,1)} %shard_map.91), calls=%async_computation.3 | async-start | bytes 262144 | tf_op jit(solution)/shard_map/all_to_all | solution.py:224
  125.0 0.0 collective-permute-done.3.far
  125.1 0.0 copy-start.1
  125.1 1.6 %copy-done.1 = bf16[1024,1024]{1,0:T(8,128)(2,1)S(1)} copy-done((bf16[1024,1024]{1,0:T(8,128)(2,1)S(1)}, bf16[1024,1024]{1,0:T(8,128)(2,1)}, u32[]{:S(2)}) %copy-start.1) | copy-done | bytes 2097176
  126.7 3.1 %shard_map.90 = f32[128,1024]{1,0:T(8,128)} custom-call(bf16[128,1024]{1,0:T(8,128)(2,1)S(1)} %get-tuple-element.12.tile, bf16[4,128,1280]{2,1,0:T(8,128)(2,1)S(1)} %all_to_all.26.same, bf16[4,128,1280]{2,1,0:T(8,128)(2,1)S(1)} %collective-permute-done.2.other, bf16[128,1024]{1,0:T(8,128)(2,1)} %collective-permute-done.3.far, bf16[1024,1024]{1,0:T(8,128)(2,1)S(1)} %copy-done.1), custom_call_target="tpu_custom_call" | custom-call | flops 99999997952 | bytes 1 | tf_op jit(solution)/shard_map/pallas_call | solution.py:23
  129.8 11.6 %all-to-all-done.3.pieces = bf16[16,4,1024]{2,1,0:T(4,128)(2,1)S(1)} async-done(((bf16[16,4,1024]{2,1,0:T(4,128)(2,1)}), bf16[16,4,1024]{2,1,0:T(4,128)(2,1)S(1)}, u32[]{:S(2)}, u32[]{:S(2)}) %all-to-all-start.3) | async-done | bytes 131104 | tf_op jit(solution)/shard_map/all_to_all | solution.py:224
  141.4 9.2 %all_to_all.27 = f32[8,4,1024]{2,1,0:T(4,128)S(1)} all-to-all(f32[8,4,1024]{2,1,0:T(4,128)S(1)} %shard_map.92), channel_id=1, replica_groups=mesh['zh'=2,'y'=4,'co'=2,'x'=4,'zl'=8] {'y','co'}, dimensions={0} | all-to-all | bytes 262144 | tf_op jit(solution)/shard_map/all_to_all | solution.py:227
  150.6 0.7 reshape.78
  (2 shorter events, 0.0 us)
Async XLA Ops:
  21.7 10.0 %collective-permute-start = (bf16[4,128,1280]{2,1,0:T(8,128)(2,1)S(1)}, bf16[4,128,1280]{2,1,0:T(8,128)(2,1)S(1)}, u32[]{:S(2)}, u32[]{:S(2)}) collective-permute-start(bf16[4,128,1280]{2,1,0:T(8,128)(2,1)S(1)} %all_to_all.25.same), channel_id=1, source_target_pairs={{0,32},{32,0},{1,33},{33,1},{2,34},{34,2},{3,35},{35,3},{4,36},{36... | collective-permute-start | bytes 3932168 | tf_op jit(solution)/shard_map/ppermute | solution.py:160
  32.4 21.8 %collective-permute-start.1 = (bf16[128,1024]{1,0:T(8,128)(2,1)S(1)}, bf16[128,1024]{1,0:T(8,128)(2,1)S(1)}, u32[]{:S(2)}, u32[]{:S(2)}) collective-permute-start(bf16[128,1024]{1,0:T(8,128)(2,1)S(1)} %get-tuple-element.14), channel_id=1, source_target_pairs={{0,256},{256,0},{1,257},{257,1},{2,258},{258,2},{3,259},{259,3},{4... | collective-permute-start | bytes 786440 | tf_op jit(solution)/shard_map/ppermute | solution.py:148
  48.8 5.5 %copy-start = (bf16[1024,1024]{1,0:T(8,128)(2,1)S(1)}, bf16[1024,1024]{1,0:T(8,128)(2,1)}, u32[]{:S(2)}) copy-start(bf16[1024,1024]{1,0:T(8,128)(2,1)} %weight.3) | copy-start | bytes 6291460
  48.8 5.5 %copy-start.2 = (bf16[128,1024]{1,0:T(8,128)(2,1)S(1)}, bf16[128,1024]{1,0:T(8,128)(2,1)}, u32[]{:S(2)}) copy-start(bf16[128,1024]{1,0:T(8,128)(2,1)} %cotangent.1) | copy-start | bytes 786436
  75.1 6.6 %collective-permute-start.2 = (bf16[4,128,1280]{2,1,0:T(8,128)(2,1)S(1)}, bf16[4,128,1280]{2,1,0:T(8,128)(2,1)S(1)}, u32[]{:S(2)}, u32[]{:S(2)}) collective-permute-start(bf16[4,128,1280]{2,1,0:T(8,128)(2,1)S(1)} %all_to_all.26.same), channel_id=1, source_target_pairs={{0,32},{32,0},{1,33},{33,1},{2,34},{34,2},{3,35},{35,3},{4,36},{36... | collective-permute-start | bytes 3932168 | tf_op jit(solution)/shard_map/ppermute | solution.py:160
  83.8 15.8 %all-to-all-start.2 = ((f32[4,32,1024]{2,1,0:T(8,128)}), f32[4,32,1024]{2,1,0:T(8,128)S(1)}, u32[]{:S(2)}, u32[]{:S(2)}) async-start(f32[4,32,1024]{2,1,0:T(8,128)} %bitcast.3), calls=%async_computation.2 | async-start | bytes 1048576 | tf_op jit(solution)/shard_map/all_to_all | solution.py:221
  87.9 37.2 %collective-permute-start.3 = (bf16[128,1024]{1,0:T(8,128)(2,1)}, bf16[128,1024]{1,0:T(8,128)(2,1)}, u32[]{:S(2)}, u32[]{:S(2)}) collective-permute-start(bf16[128,1024]{1,0:T(8,128)(2,1)} %get-tuple-element.18), channel_id=1, source_target_pairs={{0,256},{256,0},{1,257},{257,1},{2,258},{258,2},{3,259},{259,3},{4... | collective-permute-start | bytes 786440 | tf_op jit(solution)/shard_map/ppermute | solution.py:148
  100.4 41.0 %all-to-all-start.3 = ((bf16[16,4,1024]{2,1,0:T(4,128)(2,1)}), bf16[16,4,1024]{2,1,0:T(4,128)(2,1)S(1)}, u32[]{:S(2)}, u32[]{:S(2)}) async-start(bf16[16,4,1024]{2,1,0:T(4,128)(2,1)} %shard_map.91), calls=%async_computation.3 | async-start | bytes 262144 | tf_op jit(solution)/shard_map/all_to_all | solution.py:224
  125.1 1.6 %copy-start.1 = (bf16[1024,1024]{1,0:T(8,128)(2,1)S(1)}, bf16[1024,1024]{1,0:T(8,128)(2,1)}, u32[]{:S(2)}) copy-start(bf16[1024,1024]{1,0:T(8,128)(2,1)} %weight.3) | copy-start | bytes 6291460

commit v10 on v9

--- a/solution.py
+++ b/solution.py
@@ -116,7 +116,7 @@
     far[...] = far_here.astype(BF16)
     far_copy = pltpu.make_async_copy(far, far_hbm, sems.at[0])
     far_copy.start()
-    partial[...] = grouped(same, other)
+    partial[...] = grouped(same, other).astype(BF16)
     partial_copy = pltpu.make_async_copy(partial, partial_hbm, sems.at[1])
     partial_copy.start()
     far_copy.wait()
@@ -124,7 +124,8 @@
 
 
 def sum_x_body(pieces, out):
-    total = pieces[0] + pieces[1] + pieces[2] + pieces[3]
+    total = pieces[0].astype(F32) + pieces[1].astype(F32)
+    total += pieces[2].astype(F32) + pieces[3].astype(F32)
     for z in range(8):
         rows = total[4 * z : 4 * z + 4].astype(BF16)
         out[z] = rows
@@ -206,13 +207,13 @@
     far, partial = pl.pallas_call(
         sums_body,
         out_shape=(
-            pltpu.HBM(rows_bf16.shape, BF16), pltpu.HBM(rows_f32.shape, F32),
+            pltpu.HBM(rows_bf16.shape, BF16), pltpu.HBM(rows_bf16.shape, BF16),
         ),
         in_specs=[VMEM] * 3,
         out_specs=(HBM, HBM),
         scratch_shapes=[
             pltpu.VMEM(rows_bf16.shape, BF16),
-            pltpu.VMEM(rows_f32.shape, F32),
+            pltpu.VMEM(rows_bf16.shape, BF16),
             pltpu.SemaphoreType.DMA((2,)),
         ],
         compiler_params=pltpu.CompilerParams(vmem_limit_bytes=16 * 2**20),

time: 152 us -> 152 us (level)
  blocking collectives: 46.6 us -> 58.6 us
  starting transfers between devices: 67.2 us -> 60.1 us
  waiting for transfers between devices: 21.7 us -> 16.6 us
    all_to_all x0 -> x1, blocking collectives: none -> 9.55 us  [local(): part = lax.all_to_all(partial.reshape(4, 32, hidden), 'x', 0, 0)]
    all_to_all x1, waiting for transfers between devices: 11.6 us -> 6.59 us  [local(): part = lax.all_to_all(part, ('zh', 'zl'), 0, 0)]
    all_to_all x1 -> x0, starting transfers between devices: 4.01 us -> none  [local(): part = lax.all_to_all(partial.reshape(4, 32, hidden), 'x', 0, 0)]
    all_to_all x1, starting transfers between devices: 24.7 us -> 21.5 us  [local(): part = lax.all_to_all(part, ('zh', 'zl'), 0, 0)]
    all_to_all x1, blocking collectives: 9.18 us -> 11.6 us  [local(): part = lax.all_to_all(part, ('y', 'co'), 0, 0)]
  transfers between devices with their start and end apart: 6 -> 5, of which waited for: 4 -> 4; matrix products, arithmetic and copies ran while one was open for 1% -> 1% of each run, Pallas kernels for 3% -> 3%
where the time goes in v10:
time: 152 us
  starting transfers between devices  60.1 us (40%)
  blocking collectives  58.6 us (39%)
  waiting for transfers between devices  16.6 us (11%)
  Pallas kernels  11 us (7%)
  local copies, waits for them, and re-layouts  2.98 us (2%)
    all_to_all x2, blocking collectives, over_y(): return lax.all_to_all(message, 'y', 0, 0)  37.4 us
    ppermute x2, starting transfers between devices, partner(): return lax.ppermute(rows, 'zh', SWAP)  27.3 us
    all_to_all x1, starting transfers between devices, local(): part = lax.all_to_all(part, ('zh', 'zl'), 0, 0)  21.5 us
    all_to_all x1, blocking collectives, local(): part = lax.all_to_all(part, ('y', 'co'), 0, 0)  11.6 us
    ppermute x2, starting transfers between devices, other_core(): return lax.ppermute(rows, 'co', SWAP)  11.3 us
    all_to_all x1, blocking collectives, local(): part = lax.all_to_all(partial.reshape(4, 32, hidden), 'x', 0, 0)  9.55 us
    pallas_call x6, Pallas kernels, call(): pl.pallas_call(body, out_shape=outs, in_specs=[SMEM if a.dtype == jnp.int...  6.9 us
    all_to_all x1, waiting for transfers between devices, local(): part = lax.all_to_all(part, ('zh', 'zl'), 0, 0)  6.59 us
  transfers between devices with their start and end apart: 5, of which 4 were waited for; matrix products, arithmetic and copies ran while one was open for 1% of the time, Pallas kernels for 3%

profile of v10, /device:TPU:1, one launch (start us, length us, event | category | flops | bytes accessed | tf_op | source)
XLA Modules:
  0.0 151.7 jit_solution(4818497897801324951)
XLA Ops:
  1.3 0.1 pad_add_fusion.place
  1.4 2.1 %shard_map.85 = (bf16[4,128,1280]{2,1,0:T(8,128)(2,1)S(1)}, bf16[128,1024]{1,0:T(8,128)(2,1)S(1)}) custom-call(s32[2]{0:T(128)S(1)} %pad_add_fusion.place, s32[1]{0:T(128)S(6)} %copy.9.count, s32[1,16]{1,0:T(1,128)} %codes_hbm.1, bf16[1,16,128,128]{3,2,1,0:T(8,128)(2,1)} %values_hbm.1, bf16[128,1024]{1,0:T(8,128)(2,1)} %features.1), custom_call_target="tpu_custom_call" | custom-call | tf_op jit(solution)/shard_map/pallas_call | solution.py:178
  3.4 0.0 copy-start.4
  3.4 18.3 %all_to_all.25.same = bf16[4,128,1280]{2,1,0:T(8,128)(2,1)S(1)} all-to-all(bf16[4,128,1280]{2,1,0:T(8,128)(2,1)S(1)} %get-tuple-element.13), channel_id=1, replica_groups=mesh['zh'=2,'y'=4,'co'=2,'x'=4,'zl'=8] {'y'}, dimensions={0} | all-to-all | bytes 2621440 | tf_op jit(solution)/shard_map/all_to_all | solution.py:157
  21.7 7.3 %collective-permute-start = (bf16[4,128,1280]{2,1,0:T(8,128)(2,1)S(1)}, bf16[4,128,1280]{2,1,0:T(8,128)(2,1)S(1)}, u32[]{:S(2)}, u32[]{:S(2)}) collective-permute-start(bf16[4,128,1280]{2,1,0:T(8,128)(2,1)S(1)} %all_to_all.25.same), channel_id=1, source_target_pairs={{0,32},{32,0},{1,33},{33,1},{2,34},{34,2},{3,35},{35,3},{4,36},{36... | collective-permute-start | bytes 3932168 | tf_op jit(solution)/shard_map/ppermute | solution.py:161
  29.0 2.6 %collective-permute-done.other = bf16[4,128,1280]{2,1,0:T(8,128)(2,1)S(1)} collective-permute-done((bf16[4,128,1280]{2,1,0:T(8,128)(2,1)S(1)}, bf16[4,128,1280]{2,1,0:T(8,128)(2,1)S(1)}, u32[]{:S(2)}, u32[]{:S(2)}) %collective-permute-start) | collective-permute-done | bytes 1310752 | tf_op jit(solution)/shard_map/ppermute | solution.py:161
  31.7 0.7 shard_map.87
  32.4 15.5 %collective-permute-start.1 = (bf16[128,1024]{1,0:T(8,128)(2,1)S(1)}, bf16[128,1024]{1,0:T(8,128)(2,1)S(1)}, u32[]{:S(2)}, u32[]{:S(2)}) collective-permute-start(bf16[128,1024]{1,0:T(8,128)(2,1)S(1)} %get-tuple-element.14), channel_id=1, source_target_pairs={{0,256},{256,0},{1,257},{257,1},{2,258},{258,2},{3,259},{259,3},{4... | collective-permute-start | bytes 786440 | tf_op jit(solution)/shard_map/ppermute | solution.py:149
  47.9 0.9 fusion.regroup
  48.7 0.0 copy-done.4
  48.8 0.0 copy-start
  48.8 0.0 copy-start.3
  48.8 0.7 shard_map.86.near
  49.5 4.8 %collective-permute-done.1.far = bf16[128,1024]{1,0:T(8,128)(2,1)S(1)} collective-permute-done((bf16[128,1024]{1,0:T(8,128)(2,1)S(1)}, bf16[128,1024]{1,0:T(8,128)(2,1)S(1)}, u32[]{:S(2)}, u32[]{:S(2)}) %collective-permute-start.1) | collective-permute-done | bytes 262176 | tf_op jit(solution)/shard_map/ppermute | solution.py:149
  54.2 0.0 copy-done
  54.2 0.0 copy-done.3
  54.2 1.7 %shard_map.88 = (f32[128,1024]{1,0:T(8,128)}, bf16[4,128,1280]{2,1,0:T(8,128)(2,1)S(1)}) custom-call(f32[128,1024]{1,0:T(8,128)S(1)} %shard_map.86.near, bf16[128,1024]{1,0:T(8,128)(2,1)S(1)} %collective-permute-done.1.far, bf16[1024,1024]{1,0:T(8,128)(2,1)S(1)} %copy-done, bf16[128,1024]{1,0:T(8,128)(2,1)S(1)} %copy-done.3, bf16[1024,1024]{1,0:T(8,128)(2,1)S(1)} %fusion.regroup), custom_call_target="tpu_custom_call" | custom-call | flops 1 | bytes 1 | tf_op jit(solution)/shard_map/pallas_call | solution.py:23
  55.9 19.2 %all_to_all.26.same = bf16[4,128,1280]{2,1,0:T(8,128)(2,1)S(1)} all-to-all(bf16[4,128,1280]{2,1,0:T(8,128)(2,1)S(1)} %get-tuple-element.16), channel_id=1, replica_groups=mesh['zh'=2,'y'=4,'co'=2,'x'=4,'zl'=8] {'y'}, dimensions={0} | all-to-all | bytes 2621440 | tf_op jit(solution)/shard_map/all_to_all | solution.py:157
  75.1 4.0 %collective-permute-start.2 = (bf16[4,128,1280]{2,1,0:T(8,128)(2,1)S(1)}, bf16[4,128,1280]{2,1,0:T(8,128)(2,1)S(1)}, u32[]{:S(2)}, u32[]{:S(2)}) collective-permute-start(bf16[4,128,1280]{2,1,0:T(8,128)(2,1)S(1)} %all_to_all.26.same), channel_id=1, source_target_pairs={{0,32},{32,0},{1,33},{33,1},{2,34},{34,2},{3,35},{35,3},{4,36},{36... | collective-permute-start | bytes 3932168 | tf_op jit(solution)/shard_map/ppermute | solution.py:161
  79.1 2.6 %collective-permute-done.2.other = bf16[4,128,1280]{2,1,0:T(8,128)(2,1)S(1)} collective-permute-done((bf16[4,128,1280]{2,1,0:T(8,128)(2,1)S(1)}, bf16[4,128,1280]{2,1,0:T(8,128)(2,1)S(1)}, u32[]{:S(2)}, u32[]{:S(2)}) %collective-permute-start.2) | collective-permute-done | bytes 1310752 | tf_op jit(solution)/shard_map/ppermute | solution.py:161
  81.7 2.0 %shard_map.89 = (bf16[128,1024]{1,0:T(8,128)(2,1)}, bf16[128,1024]{1,0:T(8,128)(2,1)}) custom-call(bf16[8,128,128]{2,1,0:T(8,128)(2,1)S(1)} %get-tuple-element.17.mirror, bf16[4,128,1280]{2,1,0:T(8,128)(2,1)S(1)} %all_to_all.26.same, bf16[4,128,1280]{2,1,0:T(8,128)(2,1)S(1)} %collective-permute-done.2.other), custom_call_target="tpu_custom_call" | custom-call | flops 1 | bytes 1 | tf_op jit(solution)/shard_map/pallas_call | solution.py:207
  83.8 11.8 %collective-permute-start.3 = (bf16[128,1024]{1,0:T(8,128)(2,1)}, bf16[128,1024]{1,0:T(8,128)(2,1)}, u32[]{:S(2)}, u32[]{:S(2)}) collective-permute-start(bf16[128,1024]{1,0:T(8,128)(2,1)} %get-tuple-element.18), channel_id=1, source_target_pairs={{0,256},{256,0},{1,257},{257,1},{2,258},{258,2},{3,259},{259,3},{4... | collective-permute-start | bytes 786440 | tf_op jit(solution)/shard_map/ppermute | solution.py:149
  95.6 9.5 %all_to_all.27.pieces = bf16[4,32,1024]{2,1,0:T(8,128)(2,1)S(1)} all-to-all(bf16[4,32,1024]{2,1,0:T(8,128)(2,1)} %bitcast.3), channel_id=1, replica_groups=mesh['zh'=2,'y'=4,'co'=2,'x'=4,'zl'=8] {'x'}, dimensions={0} | all-to-all | bytes 524288 | tf_op jit(solution)/shard_map/all_to_all | solution.py:222
  105.1 0.7 shard_map.91
  105.8 21.5 %all-to-all-start.3 = ((bf16[16,4,1024]{2,1,0:T(4,128)(2,1)}), bf16[16,4,1024]{2,1,0:T(4,128)(2,1)S(1)}, u32[]{:S(2)}, u32[]{:S(2)}) async-start(bf16[16,4,1024]{2,1,0:T(4,128)(2,1)} %shard_map.91), calls=%async_computation.3 | async-start | bytes 262144 | tf_op jit(solution)/shard_map/all_to_all | solution.py:225
  127.4 0.0 collective-permute-done.3.far
  127.4 1.3 copy-done.2
  128.7 0.9 copy-done.5
  129.7 3.1 %shard_map.90 = f32[128,1024]{1,0:T(8,128)} custom-call(bf16[128,1024]{1,0:T(8,128)(2,1)S(1)} %copy-done.5, bf16[4,128,1280]{2,1,0:T(8,128)(2,1)S(1)} %all_to_all.26.same, bf16[4,128,1280]{2,1,0:T(8,128)(2,1)S(1)} %copy-done.2, bf16[128,1024]{1,0:T(8,128)(2,1)} %collective-permute-done.3.far, bf16[1024,1024]{1,0:T(8,128)(2,1)S(1)} %copy-done), custom_call_target="tpu_custom_call" | custom-call | flops 99999997952 | bytes 1 | tf_op jit(solution)/shard_map/pallas_call | solution.py:23
  132.8 6.6 %all-to-all-done.3.pieces = bf16[16,4,1024]{2,1,0:T(4,128)(2,1)S(1)} async-done(((bf16[16,4,1024]{2,1,0:T(4,128)(2,1)}), bf16[16,4,1024]{2,1,0:T(4,128)(2,1)S(1)}, u32[]{:S(2)}, u32[]{:S(2)}) %all-to-all-start.3) | async-done | bytes 131104 | tf_op jit(solution)/shard_map/all_to_all | solution.py:225
  139.4 11.6 %all_to_all.28 = f32[8,4,1024]{2,1,0:T(4,128)S(1)} all-to-all(f32[8,4,1024]{2,1,0:T(4,128)S(1)} %shard_map.92), channel_id=1, replica_groups=mesh['zh'=2,'y'=4,'co'=2,'x'=4,'zl'=8] {'y','co'}, dimensions={0} | all-to-all | bytes 262144 | tf_op jit(solution)/shard_map/all_to_all | solution.py:228
  151.0 0.7 reshape.78
  (6 shorter events, 0.0 us)
Async XLA Ops:
  3.4 45.3 %copy-start.4 = (bf16[128,1024]{1,0:T(8,128)(2,1)}, bf16[128,1024]{1,0:T(8,128)(2,1)S(1)}, u32[]{:S(2)}) copy-start(bf16[128,1024]{1,0:T(8,128)(2,1)S(1)} %get-tuple-element.12.tile) | copy-start | bytes 786436
  21.7 10.0 %collective-permute-start = (bf16[4,128,1280]{2,1,0:T(8,128)(2,1)S(1)}, bf16[4,128,1280]{2,1,0:T(8,128)(2,1)S(1)}, u32[]{:S(2)}, u32[]{:S(2)}) collective-permute-start(bf16[4,128,1280]{2,1,0:T(8,128)(2,1)S(1)} %all_to_all.25.same), channel_id=1, source_target_pairs={{0,32},{32,0},{1,33},{33,1},{2,34},{34,2},{3,35},{35,3},{4,36},{36... | collective-permute-start | bytes 3932168 | tf_op jit(solution)/shard_map/ppermute | solution.py:161
  32.4 21.8 %collective-permute-start.1 = (bf16[128,1024]{1,0:T(8,128)(2,1)S(1)}, bf16[128,1024]{1,0:T(8,128)(2,1)S(1)}, u32[]{:S(2)}, u32[]{:S(2)}) collective-permute-start(bf16[128,1024]{1,0:T(8,128)(2,1)S(1)} %get-tuple-element.14), channel_id=1, source_target_pairs={{0,256},{256,0},{1,257},{257,1},{2,258},{258,2},{3,259},{259,3},{4... | collective-permute-start | bytes 786440 | tf_op jit(solution)/shard_map/ppermute | solution.py:149
  48.8 5.5 %copy-start = (bf16[1024,1024]{1,0:T(8,128)(2,1)S(1)}, bf16[1024,1024]{1,0:T(8,128)(2,1)}, u32[]{:S(2)}) copy-start(bf16[1024,1024]{1,0:T(8,128)(2,1)} %weight.3) | copy-start | bytes 6291460
  48.8 5.5 %copy-start.3 = (bf16[128,1024]{1,0:T(8,128)(2,1)S(1)}, bf16[128,1024]{1,0:T(8,128)(2,1)}, u32[]{:S(2)}) copy-start(bf16[128,1024]{1,0:T(8,128)(2,1)} %cotangent.1) | copy-start | bytes 786436
  75.1 6.6 %collective-permute-start.2 = (bf16[4,128,1280]{2,1,0:T(8,128)(2,1)S(1)}, bf16[4,128,1280]{2,1,0:T(8,128)(2,1)S(1)}, u32[]{:S(2)}, u32[]{:S(2)}) collective-permute-start(bf16[4,128,1280]{2,1,0:T(8,128)(2,1)S(1)} %all_to_all.26.same), channel_id=1, source_target_pairs={{0,32},{32,0},{1,33},{33,1},{2,34},{34,2},{3,35},{35,3},{4,36},{36... | collective-permute-start | bytes 3932168 | tf_op jit(solution)/shard_map/ppermute | solution.py:161
  81.7 2.0 %copy-start.1 = (bf16[4,128,1280]{2,1,0:T(8,128)(2,1)}, bf16[4,128,1280]{2,1,0:T(8,128)(2,1)S(1)}, u32[]{:S(2)}) copy-start(bf16[4,128,1280]{2,1,0:T(8,128)(2,1)S(1)} %collective-permute-done.2.other) | copy-start | bytes 3932164
  83.8 43.6 %collective-permute-start.3 = (bf16[128,1024]{1,0:T(8,128)(2,1)}, bf16[128,1024]{1,0:T(8,128)(2,1)}, u32[]{:S(2)}, u32[]{:S(2)}) collective-permute-start(bf16[128,1024]{1,0:T(8,128)(2,1)} %get-tuple-element.18), channel_id=1, source_target_pairs={{0,256},{256,0},{1,257},{257,1},{2,258},{258,2},{3,259},{259,3},{4... | collective-permute-start | bytes 786440 | tf_op jit(solution)/shard_map/ppermute | solution.py:149
  105.8 33.5 %all-to-all-start.3 = ((bf16[16,4,1024]{2,1,0:T(4,128)(2,1)}), bf16[16,4,1024]{2,1,0:T(4,128)(2,1)S(1)}, u32[]{:S(2)}, u32[]{:S(2)}) async-start(bf16[16,4,1024]{2,1,0:T(4,128)(2,1)} %shard_map.91), calls=%async_computation.3 | async-start | bytes 262144 | tf_op jit(solution)/shard_map/all_to_all | solution.py:225
  127.4 1.3 copy-start.2
  128.7 0.9 copy-start.5

commit v11 on v9

--- a/solution.py
+++ b/solution.py
@@ -146,6 +146,17 @@
 
 def partner(rows):
     return lax.ppermute(rows, "zh", SWAP)
+
+
+def partner_by_fours(rows):
+    pairs = []
+    for z in range(16):
+        for core in range(2):
+            to = (z + (4 if core == 0 else -4)) % 16
+            pairs.append((z // 8 * 16 + core * 8 + z % 8, to // 8 * 16 + core * 8 + to % 8))
+    for _ in range(2):
+        rows = lax.ppermute(rows, ("zh", "co", "zl"), pairs)
+    return rows
 
 
 def after(value, *others):
@@ -195,7 +206,7 @@
     same = over_y(message)
     other = other_core(same)
     far, mirror = call(first_far_body, (rows_bf16, shape(8, 128, 128, dtype=BF16)), same, other)
-    far = partner(far)
+    far = partner_by_fours(far)
     near = call(near_body, rows_f32, tile, same, other)
     output, message = call(
         forward_body, (rows_f32, message_shape), near, far, weight, cotangent, regroup

time: 152 us -> 160 us (1.053)
  waiting for transfers between devices: 21.7 us -> 40.8 us
  starting transfers between devices: 67.2 us -> 54.9 us
  blocking collectives: 46.6 us -> 48.4 us
    ppermute x0 -> x2, starting transfers between devices: none -> 20.2 us  [partner_by_fours(): rows = lax.ppermute(rows, ('zh', 'co', 'zl'), pairs)]
    ppermute x0 -> x2, waiting for transfers between devices: none -> 19.3 us  [partner_by_fours(): rows = lax.ppermute(rows, ('zh', 'co', 'zl'), pairs)]
    ppermute x2 -> x1, starting transfers between devices: 27.3 us -> 10.2 us  [partner(): return lax.ppermute(rows, 'zh', SWAP)]
    all_to_all x1, starting transfers between devices: 24.7 us -> 8.62 us  [local(): part = lax.all_to_all(part, ('zh', 'zl'), 0, 0)]
    all_to_all x1, waiting for transfers between devices: 11.6 us -> 1.18 us  [local(): part = lax.all_to_all(part, ('zh', 'zl'), 0, 0)]
    ppermute x2 -> x1, waiting for transfers between devices: 4.76 us -> 15 us  [partner(): return lax.ppermute(rows, 'zh', SWAP)]
    all_to_all x1, blocking collectives: 9.18 us -> 11.5 us  [local(): part = lax.all_to_all(part, ('y', 'co'), 0, 0)]
  transfers between devices with their start and end apart: 6 -> 7, of which waited for: 4 -> 6; matrix products, arithmetic and copies ran while one was open for 1% -> 1% of each run, Pallas kernels for 3% -> 3%
where the time goes in v11:
time: 160 us
  starting transfers between devices  54.9 us (34%)
  blocking collectives  48.4 us (30%)
  waiting for transfers between devices  40.8 us (25%)
  Pallas kernels  11.2 us (7%)
  local copies, waits for them, and re-layouts  2.3 us (1%)
    all_to_all x2, blocking collectives, over_y(): return lax.all_to_all(message, 'y', 0, 0)  36.9 us
    ppermute x2, starting transfers between devices, partner_by_fours(): rows = lax.ppermute(rows, ('zh', 'co', 'zl'), pairs)  20.2 us
    ppermute x2, waiting for transfers between devices, partner_by_fours(): rows = lax.ppermute(rows, ('zh', 'co', 'zl'), pairs)  19.3 us
    ppermute x1, waiting for transfers between devices, partner(): return lax.ppermute(rows, 'zh', SWAP)  15 us
    ppermute x2, starting transfers between devices, other_core(): return lax.ppermute(rows, 'co', SWAP)  11.9 us
    all_to_all x1, blocking collectives, local(): part = lax.all_to_all(part, ('y', 'co'), 0, 0)  11.5 us
    ppermute x1, starting transfers between devices, partner(): return lax.ppermute(rows, 'zh', SWAP)  10.2 us
    all_to_all x1, starting transfers between devices, local(): part = lax.all_to_all(part, ('zh', 'zl'), 0, 0)  8.62 us
  transfers between devices with their start and end apart: 7, of which 6 were waited for; matrix products, arithmetic and copies ran while one was open for 1% of the time, Pallas kernels for 3%

profile of v11, /device:TPU:1, one launch (start us, length us, event | category | flops | bytes accessed | tf_op | source)
XLA Modules:
  0.0 159.9 jit_solution(9382621893747898440)
XLA Ops:
  1.3 0.1 pad_add_fusion.place
  1.4 2.1 %shard_map.85 = (bf16[4,128,1280]{2,1,0:T(8,128)(2,1)S(1)}, bf16[128,1024]{1,0:T(8,128)(2,1)S(1)}) custom-call(s32[2]{0:T(128)S(1)} %pad_add_fusion.place, s32[1]{0:T(128)S(6)} %copy.9.count, s32[1,16]{1,0:T(1,128)} %codes_hbm.1, bf16[1,16,128,128]{3,2,1,0:T(8,128)(2,1)} %values_hbm.1, bf16[128,1024]{1,0:T(8,128)(2,1)} %features.1), custom_call_target="tpu_custom_call" | custom-call | tf_op jit(solution)/shard_map/pallas_call | solution.py:188
  3.5 18.3 %all_to_all.25.same = bf16[4,128,1280]{2,1,0:T(8,128)(2,1)S(1)} all-to-all(bf16[4,128,1280]{2,1,0:T(8,128)(2,1)S(1)} %get-tuple-element.13), channel_id=1, replica_groups=mesh['zh'=2,'y'=4,'co'=2,'x'=4,'zl'=8] {'y'}, dimensions={0} | all-to-all | bytes 2621440 | tf_op jit(solution)/shard_map/all_to_all | solution.py:167
  21.7 7.3 %collective-permute-start = (bf16[4,128,1280]{2,1,0:T(8,128)(2,1)S(1)}, bf16[4,128,1280]{2,1,0:T(8,128)(2,1)S(1)}, u32[]{:S(2)}, u32[]{:S(2)}) collective-permute-start(bf16[4,128,1280]{2,1,0:T(8,128)(2,1)S(1)} %all_to_all.25.same), channel_id=1, source_target_pairs={{0,32},{32,0},{1,33},{33,1},{2,34},{34,2},{3,35},{35,3},{4,36},{36... | collective-permute-start | bytes 3932168 | tf_op jit(solution)/shard_map/ppermute | solution.py:171
  29.1 2.6 %collective-permute-done.other = bf16[4,128,1280]{2,1,0:T(8,128)(2,1)S(1)} collective-permute-done((bf16[4,128,1280]{2,1,0:T(8,128)(2,1)S(1)}, bf16[4,128,1280]{2,1,0:T(8,128)(2,1)S(1)}, u32[]{:S(2)}, u32[]{:S(2)}) %collective-permute-start) | collective-permute-done | bytes 1310752 | tf_op jit(solution)/shard_map/ppermute | solution.py:171
  31.7 0.7 shard_map.87
  32.4 12.5 %collective-permute-start.1 = (bf16[128,1024]{1,0:T(8,128)(2,1)S(1)}, bf16[128,1024]{1,0:T(8,128)(2,1)S(1)}, u32[]{:S(2)}, u32[]{:S(2)}) collective-permute-start(bf16[128,1024]{1,0:T(8,128)(2,1)S(1)} %get-tuple-element.14), channel_id=1, source_target_pairs={{0,4},{32,292},{1,5},{33,293},{2,6},{34,294},{3,7},{35,295},{4,256... | collective-permute-start | bytes 786440 | tf_op jit(solution)/shard_map/ppermute | solution.py:158
  44.9 11.7 %collective-permute-done.1 = bf16[128,1024]{1,0:T(8,128)(2,1)S(1)} collective-permute-done((bf16[128,1024]{1,0:T(8,128)(2,1)S(1)}, bf16[128,1024]{1,0:T(8,128)(2,1)S(1)}, u32[]{:S(2)}, u32[]{:S(2)}) %collective-permute-start.1) | collective-permute-done | bytes 262176 | tf_op jit(solution)/shard_map/ppermute | solution.py:158
  56.7 7.7 %collective-permute-start.2 = (bf16[128,1024]{1,0:T(8,128)(2,1)S(1)}, bf16[128,1024]{1,0:T(8,128)(2,1)S(1)}, u32[]{:S(2)}, u32[]{:S(2)}) collective-permute-start(bf16[128,1024]{1,0:T(8,128)(2,1)S(1)} %collective-permute-done.1), channel_id=1, source_target_pairs={{0,4},{32,292},{1,5},{33,293},{2,6},{34,294},{3,7},{35,295},{4,256... | collective-permute-start | bytes 786440 | tf_op jit(solution)/shard_map/ppermute | solution.py:158
  64.4 0.9 fusion.regroup
  65.3 0.0 copy-start
  65.3 0.0 copy-start.2
  65.3 0.7 shard_map.86.near
  66.0 7.5 %collective-permute-done.2.far = bf16[128,1024]{1,0:T(8,128)(2,1)S(1)} collective-permute-done((bf16[128,1024]{1,0:T(8,128)(2,1)S(1)}, bf16[128,1024]{1,0:T(8,128)(2,1)S(1)}, u32[]{:S(2)}, u32[]{:S(2)}) %collective-permute-start.2) | collective-permute-done | bytes 262176 | tf_op jit(solution)/shard_map/ppermute | solution.py:158
  73.5 0.0 copy-done
  73.5 0.0 copy-done.2
  73.5 1.7 %shard_map.88 = (f32[128,1024]{1,0:T(8,128)}, bf16[4,128,1280]{2,1,0:T(8,128)(2,1)S(1)}) custom-call(f32[128,1024]{1,0:T(8,128)S(1)} %shard_map.86.near, bf16[128,1024]{1,0:T(8,128)(2,1)S(1)} %collective-permute-done.2.far, bf16[1024,1024]{1,0:T(8,128)(2,1)S(1)} %copy-done, bf16[128,1024]{1,0:T(8,128)(2,1)S(1)} %copy-done.2, bf16[1024,1024]{1,0:T(8,128)(2,1)S(1)} %fusion.regroup), custom_call_target="tpu_custom_call" | custom-call | flops 1 | bytes 1 | tf_op jit(solution)/shard_map/pallas_call | solution.py:23
  75.2 18.6 %all_to_all.26.same = bf16[4,128,1280]{2,1,0:T(8,128)(2,1)S(1)} all-to-all(bf16[4,128,1280]{2,1,0:T(8,128)(2,1)S(1)} %get-tuple-element.16), channel_id=1, replica_groups=mesh['zh'=2,'y'=4,'co'=2,'x'=4,'zl'=8] {'y'}, dimensions={0} | all-to-all | bytes 2621440 | tf_op jit(solution)/shard_map/all_to_all | solution.py:167
  93.9 4.6 %collective-permute-start.3 = (bf16[4,128,1280]{2,1,0:T(8,128)(2,1)S(1)}, bf16[4,128,1280]{2,1,0:T(8,128)(2,1)S(1)}, u32[]{:S(2)}, u32[]{:S(2)}) collective-permute-start(bf16[4,128,1280]{2,1,0:T(8,128)(2,1)S(1)} %all_to_all.26.same), channel_id=1, source_target_pairs={{0,32},{32,0},{1,33},{33,1},{2,34},{34,2},{3,35},{35,3},{4,36},{36... | collective-permute-start | bytes 3932168 | tf_op jit(solution)/shard_map/ppermute | solution.py:171
  98.4 2.6 %collective-permute-done.3.other = bf16[4,128,1280]{2,1,0:T(8,128)(2,1)S(1)} collective-permute-done((bf16[4,128,1280]{2,1,0:T(8,128)(2,1)S(1)}, bf16[4,128,1280]{2,1,0:T(8,128)(2,1)S(1)}, u32[]{:S(2)}, u32[]{:S(2)}) %collective-permute-start.3) | collective-permute-done | bytes 1310752 | tf_op jit(solution)/shard_map/ppermute | solution.py:171
  101.1 2.1 %shard_map.89 = (bf16[128,1024]{1,0:T(8,128)(2,1)}, f32[128,1024]{1,0:T(8,128)}) custom-call(bf16[8,128,128]{2,1,0:T(8,128)(2,1)S(1)} %get-tuple-element.17.mirror, bf16[4,128,1280]{2,1,0:T(8,128)(2,1)S(1)} %all_to_all.26.same, bf16[4,128,1280]{2,1,0:T(8,128)(2,1)S(1)} %collective-permute-done.3.other), custom_call_target="tpu_custom_call" | custom-call | flops 1 | bytes 1 | tf_op jit(solution)/shard_map/pallas_call | solution.py:217
  103.2 4.0 %all-to-all-start.2 = ((f32[4,32,1024]{2,1,0:T(8,128)}), f32[4,32,1024]{2,1,0:T(8,128)S(1)}, u32[]{:S(2)}, u32[]{:S(2)}) async-start(f32[4,32,1024]{2,1,0:T(8,128)} %bitcast.3), calls=%async_computation.2 | async-start | bytes 1048576 | tf_op jit(solution)/shard_map/all_to_all | solution.py:232
  107.1 10.2 %collective-permute-start.4 = (bf16[128,1024]{1,0:T(8,128)(2,1)}, bf16[128,1024]{1,0:T(8,128)(2,1)}, u32[]{:S(2)}, u32[]{:S(2)}) collective-permute-start(bf16[128,1024]{1,0:T(8,128)(2,1)} %get-tuple-element.18), channel_id=1, source_target_pairs={{0,256},{256,0},{1,257},{257,1},{2,258},{258,2},{3,259},{259,3},{4... | collective-permute-start | bytes 786440 | tf_op jit(solution)/shard_map/ppermute | solution.py:148
  117.4 0.0 all-to-all-done.2.pieces
  117.4 0.7 shard_map.91
  118.1 8.6 %all-to-all-start.3 = ((bf16[16,4,1024]{2,1,0:T(4,128)(2,1)}), bf16[16,4,1024]{2,1,0:T(4,128)(2,1)S(1)}, u32[]{:S(2)}, u32[]{:S(2)}) async-start(bf16[16,4,1024]{2,1,0:T(4,128)(2,1)} %shard_map.91), calls=%async_computation.3 | async-start | bytes 262144 | tf_op jit(solution)/shard_map/all_to_all | solution.py:235
  126.7 15.0 %collective-permute-done.4.far = bf16[128,1024]{1,0:T(8,128)(2,1)} collective-permute-done((bf16[128,1024]{1,0:T(8,128)(2,1)}, bf16[128,1024]{1,0:T(8,128)(2,1)}, u32[]{:S(2)}, u32[]{:S(2)}) %collective-permute-start.4) | collective-permute-done | bytes 262176 | tf_op jit(solution)/shard_map/ppermute | solution.py:148
  141.8 1.6 copy-done.1
  143.3 3.1 %shard_map.90 = f32[128,1024]{1,0:T(8,128)} custom-call(bf16[128,1024]{1,0:T(8,128)(2,1)S(1)} %get-tuple-element.12.tile, bf16[4,128,1280]{2,1,0:T(8,128)(2,1)S(1)} %all_to_all.26.same, bf16[4,128,1280]{2,1,0:T(8,128)(2,1)S(1)} %collective-permute-done.3.other, bf16[128,1024]{1,0:T(8,128)(2,1)} %collective-permute-done.4.far, bf16[1024,1024]{1,0:T(8,128)(2,1)S(1)} %copy-done.1), custom_call_target="tpu_custom_call" | custom-call | flops 99999997952 | bytes 1 | tf_op jit(solution)/shard_map/pallas_call | solution.py:23
  146.5 1.2 all-to-all-done.3.pieces
  147.7 11.5 %all_to_all.27 = f32[8,4,1024]{2,1,0:T(4,128)S(1)} all-to-all(f32[8,4,1024]{2,1,0:T(4,128)S(1)} %shard_map.92), channel_id=1, replica_groups=mesh['zh'=2,'y'=4,'co'=2,'x'=4,'zl'=8] {'y','co'}, dimensions={0} | all-to-all | bytes 262144 | tf_op jit(solution)/shard_map/all_to_all | solution.py:238
  159.2 0.7 reshape.78
  (3 shorter events, 0.0 us)
Async XLA Ops:
  21.7 10.0 %collective-permute-start = (bf16[4,128,1280]{2,1,0:T(8,128)(2,1)S(1)}, bf16[4,128,1280]{2,1,0:T(8,128)(2,1)S(1)}, u32[]{:S(2)}, u32[]{:S(2)}) collective-permute-start(bf16[4,128,1280]{2,1,0:T(8,128)(2,1)S(1)} %all_to_all.25.same), channel_id=1, source_target_pairs={{0,32},{32,0},{1,33},{33,1},{2,34},{34,2},{3,35},{35,3},{4,36},{36... | collective-permute-start | bytes 3932168 | tf_op jit(solution)/shard_map/ppermute | solution.py:171
  32.4 24.2 %collective-permute-start.1 = (bf16[128,1024]{1,0:T(8,128)(2,1)S(1)}, bf16[128,1024]{1,0:T(8,128)(2,1)S(1)}, u32[]{:S(2)}, u32[]{:S(2)}) collective-permute-start(bf16[128,1024]{1,0:T(8,128)(2,1)S(1)} %get-tuple-element.14), channel_id=1, source_target_pairs={{0,4},{32,292},{1,5},{33,293},{2,6},{34,294},{3,7},{35,295},{4,256... | collective-permute-start | bytes 786440 | tf_op jit(solution)/shard_map/ppermute | solution.py:158
  56.7 16.9 %collective-permute-start.2 = (bf16[128,1024]{1,0:T(8,128)(2,1)S(1)}, bf16[128,1024]{1,0:T(8,128)(2,1)S(1)}, u32[]{:S(2)}, u32[]{:S(2)}) collective-permute-start(bf16[128,1024]{1,0:T(8,128)(2,1)S(1)} %collective-permute-done.1), channel_id=1, source_target_pairs={{0,4},{32,292},{1,5},{33,293},{2,6},{34,294},{3,7},{35,295},{4,256... | collective-permute-start | bytes 786440 | tf_op jit(solution)/shard_map/ppermute | solution.py:158
  65.3 8.3 %copy-start = (bf16[1024,1024]{1,0:T(8,128)(2,1)S(1)}, bf16[1024,1024]{1,0:T(8,128)(2,1)}, u32[]{:S(2)}) copy-start(bf16[1024,1024]{1,0:T(8,128)(2,1)} %weight.3) | copy-start | bytes 6291460
  65.3 8.3 %copy-start.2 = (bf16[128,1024]{1,0:T(8,128)(2,1)S(1)}, bf16[128,1024]{1,0:T(8,128)(2,1)}, u32[]{:S(2)}) copy-start(bf16[128,1024]{1,0:T(8,128)(2,1)} %cotangent.1) | copy-start | bytes 786436
  93.9 7.2 %collective-permute-start.3 = (bf16[4,128,1280]{2,1,0:T(8,128)(2,1)S(1)}, bf16[4,128,1280]{2,1,0:T(8,128)(2,1)S(1)}, u32[]{:S(2)}, u32[]{:S(2)}) collective-permute-start(bf16[4,128,1280]{2,1,0:T(8,128)(2,1)S(1)} %all_to_all.26.same), channel_id=1, source_target_pairs={{0,32},{32,0},{1,33},{33,1},{2,34},{34,2},{3,35},{35,3},{4,36},{36... | collective-permute-start | bytes 3932168 | tf_op jit(solution)/shard_map/ppermute | solution.py:171
  103.2 14.2 %all-to-all-start.2 = ((f32[4,32,1024]{2,1,0:T(8,128)}), f32[4,32,1024]{2,1,0:T(8,128)S(1)}, u32[]{:S(2)}, u32[]{:S(2)}) async-start(f32[4,32,1024]{2,1,0:T(8,128)} %bitcast.3), calls=%async_computation.2 | async-start | bytes 1048576 | tf_op jit(solution)/shard_map/all_to_all | solution.py:232
  107.1 34.6 %collective-permute-start.4 = (bf16[128,1024]{1,0:T(8,128)(2,1)}, bf16[128,1024]{1,0:T(8,128)(2,1)}, u32[]{:S(2)}, u32[]{:S(2)}) collective-permute-start(bf16[128,1024]{1,0:T(8,128)(2,1)} %get-tuple-element.18), channel_id=1, source_target_pairs={{0,256},{256,0},{1,257},{257,1},{2,258},{258,2},{3,259},{259,3},{4... | collective-permute-start | bytes 786440 | tf_op jit(solution)/shard_map/ppermute | solution.py:148
  118.1 29.6 %all-to-all-start.3 = ((bf16[16,4,1024]{2,1,0:T(4,128)(2,1)}), bf16[16,4,1024]{2,1,0:T(4,128)(2,1)S(1)}, u32[]{:S(2)}, u32[]{:S(2)}) async-start(bf16[16,4,1024]{2,1,0:T(4,128)(2,1)} %shard_map.91), calls=%async_computation.3 | async-start | bytes 262144 | tf_op jit(solution)/shard_map/all_to_all | solution.py:235
  141.7 1.6 copy-start.1

commit v12 on v9

--- a/solution.py
+++ b/solution.py
@@ -58,7 +58,7 @@
         message[y, :, 1024:1280] = factor[:, 256 * y : 256 * y + 256]
 
 
-def prepare_body(place, count, codes_hbm, values_hbm, features, message, tile, codes, values, sems):
+def prepare_body(count, codes_hbm, values_hbm, features, message, tile, codes, values, sems):
     copies = [
         pltpu.make_async_copy(codes_hbm, codes, sems.at[5]),
         pltpu.make_async_copy(values_hbm.at[0], values, sems.at[4]),
@@ -70,13 +70,14 @@
     tile[...] = jnp.zeros(tile.shape, BF16)
     for y in range(4):
         message[y, :, 1024:1280] = jnp.zeros((128, 256), BF16)
+    zh, core = lax.axis_index("zh"), lax.axis_index("co")
     copies[0].wait()
     copies[1].wait()
 
     def slot(k, carry):
         grid_row = lax.div(lax.rem(codes[0, k], 512), 32)
-        y, other = lax.div(lax.rem(grid_row, 8), 2), lax.rem(grid_row + place[1], 2)
-        own = lax.div(grid_row, 8) == place[0]
+        y, other = lax.div(lax.rem(grid_row, 8), 2), lax.rem(grid_row + core, 2)
+        own = lax.div(grid_row, 8) == zh
 
         @pl.when(own)
         def _():
@@ -161,7 +162,7 @@
 
 
 def local(features, weight, cotangent, block_values, block_codes, block_count):
-    zh, core = lax.axis_index("zh"), lax.axis_index("co")
+    core = lax.axis_index("co")
     hidden = features.shape[1]
     at = jnp.arange(hidden)
     group = 2 * (at // 256) + (at // 128 % 2 ^ core)
@@ -177,7 +178,7 @@
     message, tile = pl.pallas_call(
         prepare_body,
         out_shape=(message_shape, shape(128, 1024, dtype=BF16)),
-        in_specs=[SMEM] * 2 + [HBM] * 3,
+        in_specs=[SMEM] + [HBM] * 3,
         out_specs=(VMEM, VMEM),
         scratch_shapes=[
             pltpu.SMEM(block_codes.shape, jnp.int32),
@@ -186,7 +187,7 @@
         ],
         compiler_params=pltpu.CompilerParams(vmem_limit_bytes=16 * 2**20),
     )(
-        jnp.stack([zh, core]), block_count,
+        block_count,
         *(
             pltpu.with_memory_space_constraint(a, pltpu.MemorySpace.HBM)
             for a in (block_codes, block_values, features)

time: 152 us -> 151 us (level)
  no operation moved by 1% of the time
where the time goes in v12:
time: 151 us
  starting transfers between devices  67.3 us (45%)
  blocking collectives  46.5 us (31%)
  waiting for transfers between devices  21.7 us (14%)
  Pallas kernels  10.6 us (7%)
  local copies, waits for them, and re-layouts  2.3 us (2%)
    all_to_all x2, blocking collectives, over_y(): return lax.all_to_all(message, 'y', 0, 0)  37.4 us
    ppermute x2, starting transfers between devices, partner(): return lax.ppermute(rows, 'zh', SWAP)  27.3 us
    all_to_all x1, starting transfers between devices, local(): part = lax.all_to_all(part, ('zh', 'zl'), 0, 0)  24.6 us
    all_to_all x1, waiting for transfers between devices, local(): part = lax.all_to_all(part, ('zh', 'zl'), 0, 0)  11.6 us
    ppermute x2, starting transfers between devices, other_core(): return lax.ppermute(rows, 'co', SWAP)  11.3 us
    all_to_all x1, blocking collectives, local(): part = lax.all_to_all(part, ('y', 'co'), 0, 0)  9.05 us
    pallas_call x6, Pallas kernels, call(): pl.pallas_call(body, out_shape=outs, in_specs=[SMEM if a.dtype == jnp.int...  6.9 us
    ppermute x2, waiting for transfers between devices, other_core(): return lax.ppermute(rows, 'co', SWAP)  5.26 us
  transfers between devices with their start and end apart: 6, of which 4 were waited for; matrix products, arithmetic and copies ran while one was open for 1% of the time, Pallas kernels for 3%

profile of v12, /device:TPU:1, one launch (start us, length us, event | category | flops | bytes accessed | tf_op | source)
XLA Modules:
  0.0 150.6 jit_solution(5629478335231037704)
XLA Ops:
  1.3 1.6 %shard_map.85 = (bf16[4,128,1280]{2,1,0:T(8,128)(2,1)S(1)}, bf16[128,1024]{1,0:T(8,128)(2,1)S(1)}) custom-call(s32[1]{0:T(128)S(6)} %copy.9.count, s32[1,16]{1,0:T(1,128)} %codes_hbm.1, bf16[1,16,128,128]{3,2,1,0:T(8,128)(2,1)} %values_hbm.1, bf16[128,1024]{1,0:T(8,128)(2,1)} %features.1), custom_call_target="tpu_custom_call" | custom-call | tf_op jit(solution)/shard_map/pallas_call | solution.py:178
  2.9 18.3 %all_to_all.25.same = bf16[4,128,1280]{2,1,0:T(8,128)(2,1)S(1)} all-to-all(bf16[4,128,1280]{2,1,0:T(8,128)(2,1)S(1)} %get-tuple-element.13), channel_id=1, replica_groups=mesh['zh'=2,'y'=4,'co'=2,'x'=4,'zl'=8] {'y'}, dimensions={0} | all-to-all | bytes 2621440 | tf_op jit(solution)/shard_map/all_to_all | solution.py:157
  21.1 7.3 %collective-permute-start = (bf16[4,128,1280]{2,1,0:T(8,128)(2,1)S(1)}, bf16[4,128,1280]{2,1,0:T(8,128)(2,1)S(1)}, u32[]{:S(2)}, u32[]{:S(2)}) collective-permute-start(bf16[4,128,1280]{2,1,0:T(8,128)(2,1)S(1)} %all_to_all.25.same), channel_id=1, source_target_pairs={{0,32},{32,0},{1,33},{33,1},{2,34},{34,2},{3,35},{35,3},{4,36},{36... | collective-permute-start | bytes 3932168 | tf_op jit(solution)/shard_map/ppermute | solution.py:161
  28.5 2.6 %collective-permute-done.other = bf16[4,128,1280]{2,1,0:T(8,128)(2,1)S(1)} collective-permute-done((bf16[4,128,1280]{2,1,0:T(8,128)(2,1)S(1)}, bf16[4,128,1280]{2,1,0:T(8,128)(2,1)S(1)}, u32[]{:S(2)}, u32[]{:S(2)}) %collective-permute-start) | collective-permute-done | bytes 1310752 | tf_op jit(solution)/shard_map/ppermute | solution.py:161
  31.1 0.7 shard_map.87
  31.8 15.4 %collective-permute-start.1 = (bf16[128,1024]{1,0:T(8,128)(2,1)S(1)}, bf16[128,1024]{1,0:T(8,128)(2,1)S(1)}, u32[]{:S(2)}, u32[]{:S(2)}) collective-permute-start(bf16[128,1024]{1,0:T(8,128)(2,1)S(1)} %get-tuple-element.14), channel_id=1, source_target_pairs={{0,256},{256,0},{1,257},{257,1},{2,258},{258,2},{3,259},{259,3},{4... | collective-permute-start | bytes 786440 | tf_op jit(solution)/shard_map/ppermute | solution.py:149
  47.3 0.9 fusion.regroup
  48.2 0.0 copy-start
  48.2 0.0 copy-start.2
  48.2 0.7 shard_map.86.near
  48.9 4.7 %collective-permute-done.1.far = bf16[128,1024]{1,0:T(8,128)(2,1)S(1)} collective-permute-done((bf16[128,1024]{1,0:T(8,128)(2,1)S(1)}, bf16[128,1024]{1,0:T(8,128)(2,1)S(1)}, u32[]{:S(2)}, u32[]{:S(2)}) %collective-permute-start.1) | collective-permute-done | bytes 262176 | tf_op jit(solution)/shard_map/ppermute | solution.py:149
  53.6 0.0 copy-done
  53.6 0.0 copy-done.2
  53.6 1.7 %shard_map.88 = (f32[128,1024]{1,0:T(8,128)}, bf16[4,128,1280]{2,1,0:T(8,128)(2,1)S(1)}) custom-call(f32[128,1024]{1,0:T(8,128)S(1)} %shard_map.86.near, bf16[128,1024]{1,0:T(8,128)(2,1)S(1)} %collective-permute-done.1.far, bf16[1024,1024]{1,0:T(8,128)(2,1)S(1)} %copy-done, bf16[128,1024]{1,0:T(8,128)(2,1)S(1)} %copy-done.2, bf16[1024,1024]{1,0:T(8,128)(2,1)S(1)} %fusion.regroup), custom_call_target="tpu_custom_call" | custom-call | flops 1 | bytes 1 | tf_op jit(solution)/shard_map/pallas_call | solution.py:23
  55.3 19.2 %all_to_all.26.same = bf16[4,128,1280]{2,1,0:T(8,128)(2,1)S(1)} all-to-all(bf16[4,128,1280]{2,1,0:T(8,128)(2,1)S(1)} %get-tuple-element.16), channel_id=1, replica_groups=mesh['zh'=2,'y'=4,'co'=2,'x'=4,'zl'=8] {'y'}, dimensions={0} | all-to-all | bytes 2621440 | tf_op jit(solution)/shard_map/all_to_all | solution.py:157
  74.5 4.0 %collective-permute-start.2 = (bf16[4,128,1280]{2,1,0:T(8,128)(2,1)S(1)}, bf16[4,128,1280]{2,1,0:T(8,128)(2,1)S(1)}, u32[]{:S(2)}, u32[]{:S(2)}) collective-permute-start(bf16[4,128,1280]{2,1,0:T(8,128)(2,1)S(1)} %all_to_all.26.same), channel_id=1, source_target_pairs={{0,32},{32,0},{1,33},{33,1},{2,34},{34,2},{3,35},{35,3},{4,36},{36... | collective-permute-start | bytes 3932168 | tf_op jit(solution)/shard_map/ppermute | solution.py:161
  78.5 2.6 %collective-permute-done.2.other = bf16[4,128,1280]{2,1,0:T(8,128)(2,1)S(1)} collective-permute-done((bf16[4,128,1280]{2,1,0:T(8,128)(2,1)S(1)}, bf16[4,128,1280]{2,1,0:T(8,128)(2,1)S(1)}, u32[]{:S(2)}, u32[]{:S(2)}) %collective-permute-start.2) | collective-permute-done | bytes 1310752 | tf_op jit(solution)/shard_map/ppermute | solution.py:161
  81.1 2.1 %shard_map.89 = (bf16[128,1024]{1,0:T(8,128)(2,1)}, f32[128,1024]{1,0:T(8,128)}) custom-call(bf16[8,128,128]{2,1,0:T(8,128)(2,1)S(1)} %get-tuple-element.17.mirror, bf16[4,128,1280]{2,1,0:T(8,128)(2,1)S(1)} %all_to_all.26.same, bf16[4,128,1280]{2,1,0:T(8,128)(2,1)S(1)} %collective-permute-done.2.other), custom_call_target="tpu_custom_call" | custom-call | flops 1 | bytes 1 | tf_op jit(solution)/shard_map/pallas_call | solution.py:207
  83.2 4.1 %all-to-all-start.2 = ((f32[4,32,1024]{2,1,0:T(8,128)}), f32[4,32,1024]{2,1,0:T(8,128)S(1)}, u32[]{:S(2)}, u32[]{:S(2)}) async-start(f32[4,32,1024]{2,1,0:T(8,128)} %bitcast.1), calls=%async_computation.2 | async-start | bytes 1048576 | tf_op jit(solution)/shard_map/all_to_all | solution.py:222
  87.3 11.8 %collective-permute-start.3 = (bf16[128,1024]{1,0:T(8,128)(2,1)}, bf16[128,1024]{1,0:T(8,128)(2,1)}, u32[]{:S(2)}, u32[]{:S(2)}) collective-permute-start(bf16[128,1024]{1,0:T(8,128)(2,1)} %get-tuple-element.18), channel_id=1, source_target_pairs={{0,256},{256,0},{1,257},{257,1},{2,258},{258,2},{3,259},{259,3},{4... | collective-permute-start | bytes 786440 | tf_op jit(solution)/shard_map/ppermute | solution.py:149
  99.1 0.0 all-to-all-done.2.pieces
  99.1 0.7 shard_map.91
  99.8 24.6 %all-to-all-start.3 = ((bf16[16,4,1024]{2,1,0:T(4,128)(2,1)}), bf16[16,4,1024]{2,1,0:T(4,128)(2,1)S(1)}, u32[]{:S(2)}, u32[]{:S(2)}) async-start(bf16[16,4,1024]{2,1,0:T(4,128)(2,1)} %shard_map.91), calls=%async_computation.3 | async-start | bytes 262144 | tf_op jit(solution)/shard_map/all_to_all | solution.py:225
  124.4 0.0 collective-permute-done.3.far
  124.4 0.0 copy-start.1
  124.4 1.6 %copy-done.1 = bf16[1024,1024]{1,0:T(8,128)(2,1)S(1)} copy-done((bf16[1024,1024]{1,0:T(8,128)(2,1)S(1)}, bf16[1024,1024]{1,0:T(8,128)(2,1)}, u32[]{:S(2)}) %copy-start.1) | copy-done | bytes 2097176
  126.0 3.1 %shard_map.90 = f32[128,1024]{1,0:T(8,128)} custom-call(bf16[128,1024]{1,0:T(8,128)(2,1)S(1)} %get-tuple-element.12.tile, bf16[4,128,1280]{2,1,0:T(8,128)(2,1)S(1)} %all_to_all.26.same, bf16[4,128,1280]{2,1,0:T(8,128)(2,1)S(1)} %collective-permute-done.2.other, bf16[128,1024]{1,0:T(8,128)(2,1)} %collective-permute-done.3.far, bf16[1024,1024]{1,0:T(8,128)(2,1)S(1)} %copy-done.1), custom_call_target="tpu_custom_call" | custom-call | flops 99999997952 | bytes 1 | tf_op jit(solution)/shard_map/pallas_call | solution.py:23
  129.1 11.6 %all-to-all-done.3.pieces = bf16[16,4,1024]{2,1,0:T(4,128)(2,1)S(1)} async-done(((bf16[16,4,1024]{2,1,0:T(4,128)(2,1)}), bf16[16,4,1024]{2,1,0:T(4,128)(2,1)S(1)}, u32[]{:S(2)}, u32[]{:S(2)}) %all-to-all-start.3) | async-done | bytes 131104 | tf_op jit(solution)/shard_map/all_to_all | solution.py:225
  140.8 9.0 %all_to_all.27 = f32[8,4,1024]{2,1,0:T(4,128)S(1)} all-to-all(f32[8,4,1024]{2,1,0:T(4,128)S(1)} %shard_map.92), channel_id=1, replica_groups=mesh['zh'=2,'y'=4,'co'=2,'x'=4,'zl'=8] {'y','co'}, dimensions={0} | all-to-all | bytes 262144 | tf_op jit(solution)/shard_map/all_to_all | solution.py:228
  149.9 0.7 reshape.78
  (2 shorter events, 0.0 us)
Async XLA Ops:
  21.1 10.0 %collective-permute-start = (bf16[4,128,1280]{2,1,0:T(8,128)(2,1)S(1)}, bf16[4,128,1280]{2,1,0:T(8,128)(2,1)S(1)}, u32[]{:S(2)}, u32[]{:S(2)}) collective-permute-start(bf16[4,128,1280]{2,1,0:T(8,128)(2,1)S(1)} %all_to_all.25.same), channel_id=1, source_target_pairs={{0,32},{32,0},{1,33},{33,1},{2,34},{34,2},{3,35},{35,3},{4,36},{36... | collective-permute-start | bytes 3932168 | tf_op jit(solution)/shard_map/ppermute | solution.py:161
  31.8 21.8 %collective-permute-start.1 = (bf16[128,1024]{1,0:T(8,128)(2,1)S(1)}, bf16[128,1024]{1,0:T(8,128)(2,1)S(1)}, u32[]{:S(2)}, u32[]{:S(2)}) collective-permute-start(bf16[128,1024]{1,0:T(8,128)(2,1)S(1)} %get-tuple-element.14), channel_id=1, source_target_pairs={{0,256},{256,0},{1,257},{257,1},{2,258},{258,2},{3,259},{259,3},{4... | collective-permute-start | bytes 786440 | tf_op jit(solution)/shard_map/ppermute | solution.py:149
  48.2 5.5 %copy-start = (bf16[1024,1024]{1,0:T(8,128)(2,1)S(1)}, bf16[1024,1024]{1,0:T(8,128)(2,1)}, u32[]{:S(2)}) copy-start(bf16[1024,1024]{1,0:T(8,128)(2,1)} %weight.3) | copy-start | bytes 6291460
  48.2 5.5 %copy-start.2 = (bf16[128,1024]{1,0:T(8,128)(2,1)S(1)}, bf16[128,1024]{1,0:T(8,128)(2,1)}, u32[]{:S(2)}) copy-start(bf16[128,1024]{1,0:T(8,128)(2,1)} %cotangent.1) | copy-start | bytes 786436
  74.5 6.7 %collective-permute-start.2 = (bf16[4,128,1280]{2,1,0:T(8,128)(2,1)S(1)}, bf16[4,128,1280]{2,1,0:T(8,128)(2,1)S(1)}, u32[]{:S(2)}, u32[]{:S(2)}) collective-permute-start(bf16[4,128,1280]{2,1,0:T(8,128)(2,1)S(1)} %all_to_all.26.same), channel_id=1, source_target_pairs={{0,32},{32,0},{1,33},{33,1},{2,34},{34,2},{3,35},{35,3},{4,36},{36... | collective-permute-start | bytes 3932168 | tf_op jit(solution)/shard_map/ppermute | solution.py:161
  83.2 15.9 %all-to-all-start.2 = ((f32[4,32,1024]{2,1,0:T(8,128)}), f32[4,32,1024]{2,1,0:T(8,128)S(1)}, u32[]{:S(2)}, u32[]{:S(2)}) async-start(f32[4,32,1024]{2,1,0:T(8,128)} %bitcast.1), calls=%async_computation.2 | async-start | bytes 1048576 | tf_op jit(solution)/shard_map/all_to_all | solution.py:222
  87.3 37.2 %collective-permute-start.3 = (bf16[128,1024]{1,0:T(8,128)(2,1)}, bf16[128,1024]{1,0:T(8,128)(2,1)}, u32[]{:S(2)}, u32[]{:S(2)}) collective-permute-start(bf16[128,1024]{1,0:T(8,128)(2,1)} %get-tuple-element.18), channel_id=1, source_target_pairs={{0,256},{256,0},{1,257},{257,1},{2,258},{258,2},{3,259},{259,3},{4... | collective-permute-start | bytes 786440 | tf_op jit(solution)/shard_map/ppermute | solution.py:149
  99.8 41.0 %all-to-all-start.3 = ((bf16[16,4,1024]{2,1,0:T(4,128)(2,1)}), bf16[16,4,1024]{2,1,0:T(4,128)(2,1)S(1)}, u32[]{:S(2)}, u32[]{:S(2)}) async-start(bf16[16,4,1024]{2,1,0:T(4,128)(2,1)} %shard_map.91), calls=%async_computation.3 | async-start | bytes 262144 | tf_op jit(solution)/shard_map/all_to_all | solution.py:225
  124.4 1.6 %copy-start.1 = (bf16[1024,1024]{1,0:T(8,128)(2,1)S(1)}, bf16[1024,1024]{1,0:T(8,128)(2,1)}, u32[]{:S(2)}) copy-start(bf16[1024,1024]{1,0:T(8,128)(2,1)} %weight.3) | copy-start | bytes 6291460
